TPU v7x, 128 devices: a whole 4x4x4 slice. The times are simulated.
128 devices in a mesh: ha: 8 (over x_lo, y), wa: 16 (over x_hi, z, core).
Axes of the slice: x: 4 (x_hi: 2, x_lo: 2; x = x_hi * 2 + x_lo), y: 4, z: 4, core: 2. Of those that a mesh axis runs over, the one named last changes fastest.
Arguments:
- features: bfloat16 [4, 256, 512, 192], P(None, 'ha', 'wa'), may hold values from -6 to 6
- conv_first: bfloat16 [3, 3, 3, 192, 192], replicated, may hold values from -0.078125 to 0.078125
- bias_first: float32 [192], replicated, may hold values from -3 to 3
- gain_first: float32 [192], replicated, may hold values from 0.5 to 2
- conv_second: bfloat16 [3, 3, 3, 192, 192], replicated, may hold values from -0.078125 to 0.078125
- gain_second: float32 [192], replicated, may hold values from 0.5 to 2
- up_weight: bfloat16 [3, 3, 192, 96], replicated, may hold values from -0.15625 to 0.15625
- cotangent: bfloat16 [4, 512, 1024, 96], P(None, 'ha', 'wa'), may hold values from -6 to 6
Outputs:
- feature_grad: bfloat16 [4, 256, 512, 192], P(None, 'ha', 'wa')
All inputs are finite; a program needn't handle non-finite values.
Results may differ from a plain program's by a relative error of at most 0.0051.
Values may be sent and summed in bfloat16 or wider, within the bound.
No kernel may reach another device: no remote copies, remote signals or barrier semaphores. Data moves between devices by JAX's collectives and lax.ppermute only.
A program may use at most 192 MiB of HBM per device.

v0:
```python
import jax
import jax.numpy as jnp
from jax import lax
from jax.experimental import pallas as pl
from jax.experimental.pallas import tpu as pltpu
from jax.sharding import PartitionSpec as P

COLS = 40
WIDE = 48
LANES = (640, 512, 640)
F32 = jnp.float32
BF16 = jnp.bfloat16


def shift_pair(value_up, value_down, axis):
    count = lax.axis_size(axis)
    up = [(i, (i + 1) % count) for i in range(count - 1)]
    down = [(j, i) for i, j in up]
    return lax.ppermute(value_up, axis, up), lax.ppermute(value_down, axis, down)


def halves(field, axis):
    half = field.shape[-1] // 2
    return jnp.concatenate([field[..., :half], field[..., half:]], axis=axis)


def rms_scale(value):
    return lax.rsqrt(jnp.sum(value * value, axis=-1, keepdims=True) * (1.0 / 192) + 1e-06)


def sigmoid(value):
    return 0.5 * jnp.tanh(0.5 * value) + 0.5


def put_row(ref, e, value, count):
    low, high = value[:, :128], value[:, 128:]
    high = jnp.concatenate([high, high], axis=1)
    lane = lax.broadcasted_iota(jnp.int32, high.shape, 1)
    size = value.shape[0]
    high_next = pltpu.roll(high, size - 1, 0)[:count].astype(BF16)
    ref[e, :count, 0:128] = pltpu.roll(low, 1, 0)[:count].astype(BF16)
    ref[e, :count, 128:256] = low[:count].astype(BF16)
    ref[e, :count, 256:384] = pltpu.roll(low, size - 1, 0)[:count].astype(BF16)
    both = jnp.where(lane < 64, pltpu.roll(high, 1, 0), high)
    ref[e, :count, 384:512] = both[:count].astype(BF16)
    ref[e, :count, 512:576] = high_next[:, :64]
    before = e - 1 if isinstance(e, int) and e else jnp.maximum(e - 1, 0)
    ref[before, :count, 576:640] = high_next[:, 64:]


def weight_rows(w_ref, k):
    rows = []
    for p in range(3):
        w = [w_ref[k, p, q] for q in range(3)]
        rows += [w[0][:128], w[1][:128], w[2][:128], w[0][128:], w[1][128:]]
        if p == 0:
            rows += [w[2][128:], w_ref[k, 1, 2, 128:, :]]
        if p == 2:
            rows += [w[2][128:], jnp.zeros((64, 192), BF16)]
    return jnp.concatenate(rows, axis=0)


def pack_adjoint(dst, w_ref):
    for k in range(3):
        base = 0
        for p in range(3):
            w = [w_ref[2 - k, 2 - p, 2 - q] for q in range(3)]
            for q in range(3):
                dst[k, :, base + 128 * q : base + 128 * q + 128] = w[q][:, :128]
            dst[k, :, base + 384 : base + 512] = jnp.concatenate([w[0][:, 128:], w[1][:, 128:]], axis=1)
            if p != 1:
                other = w_ref[2 - k, 1, 0][:, 128:] if p == 0 else jnp.zeros((192, 64), BF16)
                dst[k, :, base + 512 : base + 640] = jnp.concatenate([w[2][:, 128:], other], axis=1)
            base += LANES[p]


def operand(refs, frames, row, rows, cols):
    parts = []
    for s in frames:
        for p in range(3):
            piece = refs[s][pl.ds(row + p, rows), :cols, 0 : LANES[p]]
            parts.append(piece.reshape(rows * cols, LANES[p]))
    return jnp.concatenate(parts, axis=1)


def body(*refs):
    flags, feat, feat_side, cot, cot_side, before, after, w1, w2, wup, bias, gain1, gain2, out = refs[:14]
    act, grad, pre, block = (refs[14 + 4 * n : 18 + 4 * n] for n in range(4))
    acc, pooled = refs[30:32], refs[32:34]
    line, mask, w2t, w1t, wu = refs[34:]

    for n in range(4):
        act[n][35, :, 576:640] = jnp.zeros((WIDE, 64), BF16)
        grad[n][35, :, 576:640] = jnp.zeros((WIDE, 64), BF16)
    line[...] = jnp.zeros_like(line)
    s = lax.broadcasted_iota(jnp.int32, mask.shape, 0)
    good = (s < 32) | ((s < 34) & (flags[3] > 0)) | ((s >= 38) & (flags[2] > 0))
    mask[...] = jnp.where(good, 1.0, 0.0)
    pack_adjoint(w2t, w2)
    pack_adjoint(w1t, w1)
    for p in range(3):
        for q in range(3):
            tap = 128 * (3 * p + q)
            wu[:, tap : tap + 96] = wup[2 - p, 2 - q]
            wu[:, tap + 96 : tap + 128] = jnp.zeros((192, 32), BF16)

    def edge(value, b, r, first, last):
        if r in first:
            return value * jnp.where((b == 0) & (flags[0] == 0), 0.0, 1.0)
        if r in last:
            return value * jnp.where((b == 1) & (flags[1] == 0), 0.0, 1.0)
        return value

    def activate(t):
        def one(e, x):
            x = x.astype(F32)
            n = x * rms_scale(x) * gain1[...]
            put_row(act[t], e, n * sigmoid(n), COLS)

        def run(b):
            for r in range(2):
                x = jnp.where(b == 0, before[t, r].astype(F32), after[t, r].astype(F32))
                one(r + 34 * b, jnp.concatenate([x[:COLS], x[COLS:]], axis=1))
            for r in range(16):
                i = 16 * b + r
                one(i + 2, jnp.concatenate([feat[t, i].astype(F32), feat_side[t, i].astype(F32)], axis=0))

        return run

    def pool(t):
        dst = pooled[t % 2]

        def own(y):
            return jnp.concatenate([cot[t, y], cot_side[t, y]], axis=0).astype(F32)

        def one(e, rows, slot):
            for m in range(2):
                line[slot, m, :, 0:96] = rows[m] + rows[m + 1]
                even = line[slot, m, pl.ds(0, 40, stride=2), :]
                odd = line[slot, m, pl.ds(1, 40, stride=2), :]
                dst[m, e, :COLS, 0:128] = (pltpu.roll(odd, 1, 0) + even).astype(BF16)
                dst[m, e, :COLS, 128:256] = (even + odd).astype(BF16)
                dst[m, e, :COLS, 256:384] = (odd + pltpu.roll(even, 39, 0)).astype(BF16)

        def run(b):
            top = [before[t, 2 + r].astype(F32) for r in range(5)] + [own(0), own(1)]
            low = [own(63)] + [after[t, 2 + r].astype(F32) for r in range(5)]
            low.append(low[-1])
            ends = [jnp.where(b == 0, x, y) for x, y in zip(top, low)]
            for r in range(3):
                one(34 * b + r, ends[2 * r : 2 * r + 3], r)
            for r in range(16):
                e = jnp.minimum(3 + 16 * b + r, 33)
                one(e, [own(2 * e - 5 + m) for m in range(3)], 3 + r % 13)

        return run

    def keep_block(t):
        def run(b):
            for r in range(18):
                e = 18 * b + r
                value = edge(acc[t % 2][e, :COLS] * mask[...], b, r, (0, 1), (16, 17))
                put_row(grad[t], e, value, COLS)
                block[t][e] = value[:32]

        return run

    def norm_back(v, gain, top):
        scale = rms_scale(v)
        n = v * scale * gain
        s = sigmoid(n)
        u = gain * (top * (s * (1.0 + n * (1.0 - s))))
        mean = jnp.sum(v * u, axis=-1, keepdims=True) * (1.0 / 192)
        return scale * u - v * (scale * scale * scale * mean)

    def pre_grad(t):
        def run(b):
            for r in range(17):
                o = 17 * b + r
                g = norm_back(pre[t][o], gain2[...], acc[t % 2][o, :COLS])
                put_row(act[t], o, edge(g * mask[...], b, r, (0,), (16,)), 32)

        return run

    def finish(t):
        def run(b):
            for r in range(16):
                i = 16 * b + r
                g = norm_back(feat[t, i].astype(F32), gain1[...], acc[t % 2][i, 0:32])
                out[t, i] = (block[t][i + 2] + g).astype(BF16)

        return run

    def first_conv(t):
        frames = range(max(0, t - 2), t + 1)

        def run(b):
            w = jnp.concatenate([weight_rows(w1, s - t + 2) for s in frames], axis=0)
            value = jnp.dot(operand(act, frames, 17 * b, 17, WIDE), w, preferred_element_type=F32)
            pre[t][pl.ds(17 * b, 17)] = value.reshape(17, WIDE, 192)[:, :COLS] + bias[...].reshape(1, 1, 192)

        return run

    def adjoint(src, w, t, rows, cols):
        frames = range(t, min(4, t + 3))

        def run(b):
            rhs = jnp.concatenate([w[s - t] for s in frames], axis=1)
            lhs = operand(src, frames, rows * b, rows, cols)
            value = lax.dot_general(lhs, rhs, (((1,), (1,)), ((), ())), preferred_element_type=F32)
            acc[t % 2][pl.ds(rows * b, rows), :cols] = value.reshape(rows, cols, 192)

        return run

    def up_conv(t):
        src = pooled[t % 2]

        def run(b):
            parts = [src[0, pl.ds(18 * b, 18)], src[1, pl.ds(18 * b, 18)], src[0, pl.ds(18 * b + 1, 18)]]
            lhs = jnp.concatenate([x.reshape(18 * WIDE, 384) for x in parts], axis=1)
            value = lax.dot_general(lhs, wu[...], (((1,), (1,)), ((), ())), preferred_element_type=F32)
            acc[t % 2][pl.ds(18 * b, 18)] = value.reshape(18, WIDE, 192)

        return run

    second = lambda t: adjoint(grad, w2t, t, 17, WIDE)
    last = lambda t: adjoint(act, w1t, t, 16, 32)
    steps = [
        [activate(0)],
        [first_conv(0), activate(1)],
        [first_conv(1), activate(2)],
        [first_conv(2), activate(3)],
        [first_conv(3), pool(0)],
        [up_conv(0), pool(1)],
        [up_conv(1), keep_block(0), pool(2)],
        [up_conv(2), keep_block(1), pool(3)],
        [up_conv(3), keep_block(2)],
        [second(0), keep_block(3)],
        [second(1), pre_grad(0)],
        [second(2), pre_grad(1)],
        [second(3), pre_grad(2)],
        [last(0), pre_grad(3)],
        [last(1), finish(0)],
        [last(2), finish(1)],
        [last(3), finish(2)],
        [finish(3)],
    ]
    for jobs in steps:

        def step(b, carry):
            for job in jobs:
                job(b)
            return carry

        lax.fori_loop(0, 2, step, 0)


def per_device(
    features, conv_first, bias_first, gain_first, conv_second, gain_second, up_weight, cotangent
):
    def cols(lo_f, lo_c):
        parts = [cotangent[:, :, lo_c : lo_c + 5], halves(features[:, :, lo_f : lo_f + 2], 1)]
        return jnp.pad(jnp.concatenate(parts, axis=2), ((0, 0), (0, 0), (0, 1), (0, 0)))

    left, right = shift_pair(cols(30, 59), cols(0, 0), "wa")

    def ring(first, last, width):
        gap = jnp.zeros(first.shape[:2] + (width - 2 * first.shape[2], first.shape[3]), BF16)
        return jnp.concatenate([first, gap, last], axis=2)

    cot_side = ring(right[:, :, :5], left[:, :, :5], 16)
    whole = lambda side: jnp.concatenate([side[:, :32, 5:7], side[:, 32:, 5:7]], axis=3)
    feat_side = ring(whole(right), whole(left), 8)

    def rows(lo_f, lo_c):
        f = jnp.concatenate([features[:, lo_f : lo_f + 2], feat_side[:, lo_f : lo_f + 2]], axis=2)
        c = jnp.concatenate([cotangent[:, lo_c : lo_c + 5], cot_side[:, lo_c : lo_c + 5]], axis=2)
        return jnp.concatenate([halves(f, 2), c], axis=1)

    before, after = shift_pair(rows(30, 59), rows(0, 0), "ha")
    ha, wa = lax.axis_index("ha"), lax.axis_index("wa")
    flags = jnp.stack(
        [ha > 0, ha < lax.axis_size("ha") - 1, wa > 0, wa < lax.axis_size("wa") - 1]
    ).astype(jnp.int32)
    vmem = pl.BlockSpec(memory_space=pltpu.VMEM)
    return pl.pallas_call(
        body,
        out_shape=jax.ShapeDtypeStruct(features.shape, BF16),
        in_specs=[pl.BlockSpec(memory_space=pltpu.SMEM)] + [vmem] * 12,
        out_specs=vmem,
        scratch_shapes=[pltpu.VMEM((36, WIDE, 640), BF16)] * 8
        + [pltpu.VMEM((34, COLS, 192), F32)] * 4
        + [pltpu.VMEM((36, 32, 192), F32)] * 4
        + [pltpu.VMEM((36, WIDE, 192), F32)] * 2
        + [pltpu.VMEM((2, 37, WIDE, 384), BF16)] * 2
        + [
            pltpu.VMEM((16, 2, 80, 128), F32),
            pltpu.VMEM((COLS, 192), F32),
            pltpu.VMEM((3, 192, 1792), BF16),
            pltpu.VMEM((3, 192, 1792), BF16),
            pltpu.VMEM((192, 1152), BF16),
        ],
        compiler_params=pltpu.CompilerParams(vmem_limit_bytes=60 * 1024 * 1024),
        name="block_backward",
    )(
        flags, features, feat_side, cotangent, cot_side, before, after, conv_first, conv_second,
        up_weight, bias_first.reshape(1, 192), gain_first.reshape(1, 192), gain_second.reshape(1, 192),
    )


def solution(mesh):
    placed = (P(None, "ha", "wa", None), P(), P(), P(), P(), P(), P(), P(None, "ha", "wa", None))
    return jax.shard_map(
        per_device, mesh=mesh, in_specs=placed, out_specs=P(None, "ha", "wa", None), check_vma=False
    )
```

profile of v0, /device:TPU:6, one launch (start us, length us, event | category | flops | bytes accessed | tf_op | source)
XLA Modules:
  0.0 111.2 jit_solution(15835940851468745758)
XLA Ops:
  0.0 1.7 %fusion.19 = (bf16[4,32,2,96]{3,2,1,0:T(2,128)(2,1)S(1)}, bf16[4,32,2,96]{3,2,1,0:T(2,128)(2,1)S(1)}, bf16[4,32,2,96]{3,2,1,0:T(2,128)(2,1)S(1)}, bf16[4,32,2,96]{3,2,1,0:T(2,128)(2,1)S(1)}) fusion(bf16[4,32,32,192]{3,2,1,0:T(8,128)(2,1)} %refs_1_.1), kind=kLoop, calls=%fused_computation.29 | loop fusion | bytes 393216 | tf_op jit(solution)/shard_map/slice | solution.py:24
  1.7 1.4 %fusion.17 = (bf16[4,64,5,96]{3,2,1,0:T(8,128)(2,1)S(1)}, bf16[4,64,5,96]{3,2,1,0:T(8,128)(2,1)S(1)}) fusion(bf16[4,64,64,96]{3,2,1,0:T(8,128)(2,1)} %refs_3_.1), kind=kLoop, calls=%fused_computation.27 | loop fusion | bytes 983040 | tf_op jit(solution)/shard_map/slice | solution.py:262
  3.1 0.4 fusion.12
  3.6 1.9 %collective-permute-start.1 = (bf16[4,64,8,96]{3,2,1,0:T(8,128)(2,1)S(1)}, bf16[4,64,8,96]{3,2,1,0:T(8,128)(2,1)S(1)}, u32[]{:S(2)}, u32[]{:S(2)}) collective-permute-start(bf16[4,64,8,96]{3,2,1,0:T(8,128)(2,1)S(1)} %fusion.12), channel_id=1, source_target_pairs={{0,1},{1,2},{2,3},{3,4},{4,5},{5,6},{6,7},{7,8},{8,9},{9,10},{10,1... | collective-permute-start | bytes 1179656 | tf_op jit(solution)/shard_map/ppermute | solution.py:19
  5.5 0.4 fusion.10
  5.9 7.3 %collective-permute-start = (bf16[4,64,8,96]{3,2,1,0:T(8,128)(2,1)S(1)}, bf16[4,64,8,96]{3,2,1,0:T(8,128)(2,1)S(1)}, u32[]{:S(2)}, u32[]{:S(2)}) collective-permute-start(bf16[4,64,8,96]{3,2,1,0:T(8,128)(2,1)S(1)} %fusion.10), channel_id=1, source_target_pairs={{1,0},{2,1},{3,2},{4,3},{5,4},{6,5},{7,6},{8,7},{9,8},{10,9},{11,1... | collective-permute-start | bytes 1179656 | tf_op jit(solution)/shard_map/ppermute | solution.py:19
  13.2 0.1 pad.26.clone
  13.3 0.1 pad.22.clone
  13.4 1.1 %fusion.16 = (bf16[4,5,64,96]{3,2,1,0:T(8,128)(2,1)S(1)}, bf16[4,5,64,96]{3,2,1,0:T(8,128)(2,1)S(1)}) fusion(bf16[4,64,64,96]{3,2,1,0:T(8,128)(2,1)} %refs_3_.1), kind=kLoop, calls=%fused_computation.26 | loop fusion | bytes 983040 | tf_op jit(solution)/shard_map/slice | solution.py:277
  14.5 1.0 fusion.18
  15.5 2.2 %collective-permute-done.1 = bf16[4,64,8,96]{3,2,1,0:T(8,128)(2,1)S(1)} collective-permute-done((bf16[4,64,8,96]{3,2,1,0:T(8,128)(2,1)S(1)}, bf16[4,64,8,96]{3,2,1,0:T(8,128)(2,1)S(1)}, u32[]{:S(2)}, u32[]{:S(2)}) %collective-permute-start.1) | collective-permute-done | bytes 393248 | tf_op jit(solution)/shard_map/ppermute | solution.py:19
  17.7 0.1 fusion.23
  17.8 2.1 %collective-permute-done = bf16[4,64,8,96]{3,2,1,0:T(8,128)(2,1)S(1)} collective-permute-done((bf16[4,64,8,96]{3,2,1,0:T(8,128)(2,1)S(1)}, bf16[4,64,8,96]{3,2,1,0:T(8,128)(2,1)S(1)}, u32[]{:S(2)}, u32[]{:S(2)}) %collective-permute-start) | collective-permute-done | bytes 393248 | tf_op jit(solution)/shard_map/ppermute | solution.py:19
  19.9 0.1 fusion.22
  20.0 0.7 maximum_maximum_fusion.refs_2_
  20.7 0.0 copy-start.1
  20.7 0.5 pad_maximum_fusion.refs_4_
  21.2 0.0 copy-start
  21.2 0.3 copy-done.1
  21.5 0.1 fusion.9
  21.6 3.5 %collective-permute-start.2 = (bf16[4,7,80,96]{3,2,1,0:T(8,128)(2,1)S(1)}, bf16[4,7,80,96]{3,2,1,0:T(8,128)(2,1)S(1)}, u32[]{:S(2)}, u32[]{:S(2)}) collective-permute-start(bf16[4,7,80,96]{3,2,1,0:T(8,128)(2,1)S(1)} %fusion.9), channel_id=1, source_target_pairs={{0,16},{16,32},{32,48},{48,64},{64,80},{80,96},{96,112},{1,17},{17... | collective-permute-start | bytes 1290248 | tf_op jit(solution)/shard_map/ppermute | solution.py:19
  25.2 0.1 fusion.7
  25.3 0.0 copy-done
  25.3 4.5 %collective-permute-start.3 = (bf16[4,7,80,96]{3,2,1,0:T(8,128)(2,1)S(1)}, bf16[4,7,80,96]{3,2,1,0:T(8,128)(2,1)S(1)}, u32[]{:S(2)}, u32[]{:S(2)}) collective-permute-start(bf16[4,7,80,96]{3,2,1,0:T(8,128)(2,1)S(1)} %fusion.7), channel_id=1, source_target_pairs={{16,0},{32,16},{48,32},{64,48},{80,64},{96,80},{112,96},{17,1},{33... | collective-permute-start | bytes 1290248 | tf_op jit(solution)/shard_map/ppermute | solution.py:19
  29.8 0.6 add_convert_fusion.refs_0_
  30.4 8.8 %collective-permute-done.2.refs_5_ = bf16[4,7,80,96]{3,2,1,0:T(8,128)(2,1)S(1)} collective-permute-done((bf16[4,7,80,96]{3,2,1,0:T(8,128)(2,1)S(1)}, bf16[4,7,80,96]{3,2,1,0:T(8,128)(2,1)S(1)}, u32[]{:S(2)}, u32[]{:S(2)}) %collective-permute-start.2) | collective-permute-done | bytes 430112 | tf_op jit(solution)/shard_map/ppermute | solution.py:19
  39.1 0.0 copy-start.2
  39.1 1.4 %collective-permute-done.3.refs_6_ = bf16[4,7,80,96]{3,2,1,0:T(8,128)(2,1)S(1)} collective-permute-done((bf16[4,7,80,96]{3,2,1,0:T(8,128)(2,1)S(1)}, bf16[4,7,80,96]{3,2,1,0:T(8,128)(2,1)S(1)}, u32[]{:S(2)}, u32[]{:S(2)}) %collective-permute-start.3) | collective-permute-done | bytes 430112 | tf_op jit(solution)/shard_map/ppermute | solution.py:19
  40.5 0.0 copy-start.3
  40.5 0.0 copy-done.2
  40.5 0.8 copy-done.3
  41.3 69.9 %block_backward.1 = bf16[4,32,32,192]{3,2,1,0:T(8,128)(2,1)} custom-call(s32[4]{0:T(128)} %add_convert_fusion.refs_0_, bf16[4,32,32,192]{3,2,1,0:T(8,128)(2,1)} %refs_1_.1, bf16[4,32,8,192]{3,2,1,0:T(8,128)(2,1)} %copy-done.1, bf16[4,64,64,96]{3,2,1,0:T(8,128)(2,1)} %refs_3_.1, bf16[4,64,16,96]{3,2,1,0:T(8,128)(2,1)} %copy-done, ...), custom_call_target="tpu_custom_call" | custom-call | tf_op jit(solution)/shard_map/block_backward/pallas_call | solution.py:286
  (6 shorter events, 0.1 us)
Async XLA Ops:
  3.6 14.1 %collective-permute-start.1 = (bf16[4,64,8,96]{3,2,1,0:T(8,128)(2,1)S(1)}, bf16[4,64,8,96]{3,2,1,0:T(8,128)(2,1)S(1)}, u32[]{:S(2)}, u32[]{:S(2)}) collective-permute-start(bf16[4,64,8,96]{3,2,1,0:T(8,128)(2,1)S(1)} %fusion.12), channel_id=1, source_target_pairs={{0,1},{1,2},{2,3},{3,4},{4,5},{5,6},{6,7},{7,8},{8,9},{9,10},{10,1... | collective-permute-start | bytes 1179656 | tf_op jit(solution)/shard_map/ppermute | solution.py:19
  5.9 13.9 %collective-permute-start = (bf16[4,64,8,96]{3,2,1,0:T(8,128)(2,1)S(1)}, bf16[4,64,8,96]{3,2,1,0:T(8,128)(2,1)S(1)}, u32[]{:S(2)}, u32[]{:S(2)}) collective-permute-start(bf16[4,64,8,96]{3,2,1,0:T(8,128)(2,1)S(1)} %fusion.10), channel_id=1, source_target_pairs={{1,0},{2,1},{3,2},{4,3},{5,4},{6,5},{7,6},{8,7},{9,8},{10,9},{11,1... | collective-permute-start | bytes 1179656 | tf_op jit(solution)/shard_map/ppermute | solution.py:19
  20.7 0.8 copy-start.1
  21.2 4.1 %copy-start = (bf16[4,64,16,96]{3,2,1,0:T(8,128)(2,1)}, bf16[4,64,16,96]{3,2,1,0:T(8,128)(2,1)S(1)}, u32[]{:S(2)}) copy-start(bf16[4,64,16,96]{3,2,1,0:T(8,128)(2,1)S(1)} %pad_maximum_fusion.refs_4_) | copy-start | bytes 2359300
  21.6 17.5 %collective-permute-start.2 = (bf16[4,7,80,96]{3,2,1,0:T(8,128)(2,1)S(1)}, bf16[4,7,80,96]{3,2,1,0:T(8,128)(2,1)S(1)}, u32[]{:S(2)}, u32[]{:S(2)}) collective-permute-start(bf16[4,7,80,96]{3,2,1,0:T(8,128)(2,1)S(1)} %fusion.9), channel_id=1, source_target_pairs={{0,16},{16,32},{32,48},{48,64},{64,80},{80,96},{96,112},{1,17},{17... | collective-permute-start | bytes 1290248 | tf_op jit(solution)/shard_map/ppermute | solution.py:19
  25.3 15.2 %collective-permute-start.3 = (bf16[4,7,80,96]{3,2,1,0:T(8,128)(2,1)S(1)}, bf16[4,7,80,96]{3,2,1,0:T(8,128)(2,1)S(1)}, u32[]{:S(2)}, u32[]{:S(2)}) collective-permute-start(bf16[4,7,80,96]{3,2,1,0:T(8,128)(2,1)S(1)} %fusion.7), channel_id=1, source_target_pairs={{16,0},{32,16},{48,32},{64,48},{80,64},{96,80},{112,96},{17,1},{33... | collective-permute-start | bytes 1290248 | tf_op jit(solution)/shard_map/ppermute | solution.py:19
  39.1 1.4 %copy-start.2 = (bf16[4,7,80,96]{3,2,1,0:T(8,128)(2,1)}, bf16[4,7,80,96]{3,2,1,0:T(8,128)(2,1)S(1)}, u32[]{:S(2)}) copy-start(bf16[4,7,80,96]{3,2,1,0:T(8,128)(2,1)S(1)} %collective-permute-done.2.refs_5_) | copy-start | bytes 1290244
  40.5 0.8 copy-start.3
where the time goes:
time: 113 us; the launch traced here: 111 us
  Pallas kernels  69.9 us (62%)
  starting transfers between devices  17.1 us (15%)
  waiting for transfers between devices  14.3 us (13%)
  local copies, waits for them, and re-layouts  6.76 us (6%)
  other arithmetic  2.89 us (3%)
    pallas_call x1, Pallas kernels, per_device(): pl.pallas_call(body, out_shape=jax.ShapeDtypeStruct(features.shape, BF16)...  69.9 us
    ppermute x2, starting transfers between devices, shift_pair(): lax.ppermute(value_down, axis, down)  11.7 us
    ppermute x2, waiting for transfers between devices, shift_pair(): lax.ppermute(value_up, axis, up)  10.9 us
    ppermute x2, starting transfers between devices, shift_pair(): lax.ppermute(value_up, axis, up)  5.41 us
    ppermute x2, waiting for transfers between devices, shift_pair(): lax.ppermute(value_down, axis, down)  3.42 us
  transfers between devices with their start and end apart: 4, of which 4 were waited for; matrix products, arithmetic and copies ran while one was open for 3% of the time, Pallas kernels for 0%

commit v1 on v0

--- a/solution.py
+++ b/solution.py
@@ -7,6 +7,7 @@
 
 COLS = 40
 WIDE = 48
+DEEP = 5
 LANES = (640, 512, 640)
 F32 = jnp.float32
 BF16 = jnp.bfloat16
@@ -32,20 +33,30 @@
     return 0.5 * jnp.tanh(0.5 * value) + 0.5
 
 
-def put_row(ref, e, value, count):
+def put_row(ref, tail, e, value):
     low, high = value[:, :128], value[:, 128:]
     high = jnp.concatenate([high, high], axis=1)
     lane = lax.broadcasted_iota(jnp.int32, high.shape, 1)
-    size = value.shape[0]
-    high_next = pltpu.roll(high, size - 1, 0)[:count].astype(BF16)
-    ref[e, :count, 0:128] = pltpu.roll(low, 1, 0)[:count].astype(BF16)
-    ref[e, :count, 128:256] = low[:count].astype(BF16)
-    ref[e, :count, 256:384] = pltpu.roll(low, size - 1, 0)[:count].astype(BF16)
-    both = jnp.where(lane < 64, pltpu.roll(high, 1, 0), high)
-    ref[e, :count, 384:512] = both[:count].astype(BF16)
-    ref[e, :count, 512:576] = high_next[:, :64]
-    before = e - 1 if isinstance(e, int) and e else jnp.maximum(e - 1, 0)
-    ref[before, :count, 576:640] = high_next[:, 64:]
+    left = jnp.where(lane < 64, pltpu.roll(high, 1, 0), high)
+    after = pltpu.roll(high, COLS - 1, 0)
+    before = jnp.maximum(e - 1, 0)
+    for n, x in enumerate([pltpu.roll(low, 1, 0), low, pltpu.roll(low, COLS - 1, 0), left]):
+        ref[e, :, 128 * n : 128 * n + 128] = x[:32].astype(BF16)
+        if tail is not None:
+            tail[n, pl.ds(8 * e, 8), :] = x[32:]
+    own = after[:32].astype(BF16)
+    ref[e, :, 512:576] = own[:, :64]
+    ref[before, :, 576:640] = own[:, 64:]
+    if tail is not None:
+        tail[4, pl.ds(8 * e, 8), 0:64] = after[32:, :64]
+        tail[4, pl.ds(8 * before, 8), 64:128] = after[32:, 64:]
+
+
+def build_strip(dst, tail):
+    for r in range(DEEP + 2):
+        for n in range(5):
+            sides = [tail[n, pl.ds(8 * r + first, 8, stride=8 * DEEP), :] for first in (7, 0)]
+            dst[r, :, 128 * n : 128 * n + 128] = jnp.concatenate(sides, axis=0).astype(BF16)
 
 
 def weight_rows(w_ref, k):
@@ -74,28 +85,40 @@
             base += LANES[p]
 
 
-def operand(refs, frames, row, rows, cols):
+def operand(refs, strips, frames, row, rows, strip_row):
     parts = []
     for s in frames:
         for p in range(3):
-            piece = refs[s][pl.ds(row + p, rows), :cols, 0 : LANES[p]]
-            parts.append(piece.reshape(rows * cols, LANES[p]))
+            lanes = LANES[p]
+            piece = refs[s][pl.ds(row + p, rows), :, 0:lanes].reshape(rows * 32, lanes)
+            if strips is not None:
+                side = strips[s][pl.ds(strip_row + p, 3), :, 0:lanes].reshape(48, lanes)
+                piece = jnp.concatenate([piece, side], axis=0)
+            parts.append(piece)
     return jnp.concatenate(parts, axis=1)
 
 
 def body(*refs):
     flags, feat, feat_side, cot, cot_side, before, after, w1, w2, wup, bias, gain1, gain2, out = refs[:14]
-    act, grad, pre, block = (refs[14 + 4 * n : 18 + 4 * n] for n in range(4))
-    acc, pooled = refs[30:32], refs[32:34]
-    line, mask, w2t, w1t, wu = refs[34:]
+    act, grad, act_strip, grad_strip, pre, pre_strip, block = (refs[14 + 4 * n : 18 + 4 * n] for n in range(7))
+    acc_up, acc, acc_strip, pooled = (refs[42 + 2 * n : 44 + 2 * n] for n in range(4))
+    acc_last = (refs[50], acc_up[1], acc_up[0], refs[50])
+    act_tail, grad_tail, edges, line, mask, strip_mask, w2t, w1t, wu = refs[51:]
 
     for n in range(4):
-        act[n][35, :, 576:640] = jnp.zeros((WIDE, 64), BF16)
-        grad[n][35, :, 576:640] = jnp.zeros((WIDE, 64), BF16)
+        act[n][35, :, 576:640] = jnp.zeros((32, 64), BF16)
+        grad[n][35, :, 576:640] = jnp.zeros((32, 64), BF16)
+    for tail in (act_tail, grad_tail):
+        tail[:, 35 * 8 :, :] = jnp.zeros((5, 56, 128), F32)
     line[...] = jnp.zeros_like(line)
     s = lax.broadcasted_iota(jnp.int32, mask.shape, 0)
     good = (s < 32) | ((s < 34) & (flags[3] > 0)) | ((s >= 38) & (flags[2] > 0))
     mask[...] = jnp.where(good, 1.0, 0.0)
+    r, s = (lax.broadcasted_iota(jnp.int32, strip_mask.shape, n) for n in range(2))
+    o = DEEP * lax.rem(s, 8) + r
+    good = jnp.where(s < 8, flags[2], flags[3]) > 0
+    good &= ((o > 0) | (flags[0] > 0)) & ((o < 33) | (flags[1] > 0))
+    strip_mask[...] = jnp.where(good, 1.0, 0.0)
     pack_adjoint(w2t, w2)
     pack_adjoint(w1t, w1)
     for p in range(3):
@@ -115,7 +138,7 @@
         def one(e, x):
             x = x.astype(F32)
             n = x * rms_scale(x) * gain1[...]
-            put_row(act[t], e, n * sigmoid(n), COLS)
+            put_row(act[t], act_tail, e, n * sigmoid(n))
 
         def run(b):
             for r in range(2):
@@ -159,8 +182,8 @@
         def run(b):
             for r in range(18):
                 e = 18 * b + r
-                value = edge(acc[t % 2][e, :COLS] * mask[...], b, r, (0, 1), (16, 17))
-                put_row(grad[t], e, value, COLS)
+                value = edge(acc_up[t % 2][e] * mask[...], b, r, (0, 1), (16, 17))
+                put_row(grad[t], grad_tail, e, value)
                 block[t][e] = value[:32]
 
         return run
@@ -173,12 +196,23 @@
         mean = jnp.sum(v * u, axis=-1, keepdims=True) * (1.0 / 192)
         return scale * u - v * (scale * scale * scale * mean)
 
+    def strip_grad(t):
+        g = norm_back(pre_strip[t][...], gain2[...].reshape(1, 1, 192), acc_strip[t % 2][...])
+        g = g * strip_mask[...]
+        for r in range(DEEP):
+            edges[16 * r : 16 * r + 16, :] = g[r]
+
     def pre_grad(t):
+        spot = lax.broadcasted_iota(jnp.int32, (8, 192), 0)
+
         def run(b):
             for r in range(17):
                 o = 17 * b + r
-                g = norm_back(pre[t][o], gain2[...], acc[t % 2][o, :COLS])
-                put_row(act[t], o, edge(g * mask[...], b, r, (0,), (16,)), 32)
+                g = norm_back(pre[t][o], gain2[...], acc[t % 2][o])
+                at = 16 * lax.rem(o, DEEP) + lax.div(o, DEEP)
+                left, right = edges[pl.ds(at, 1), :], edges[pl.ds(at + 8, 1), :]
+                side = jnp.where(spot == 0, right, jnp.where(spot == 7, left, 0.0))
+                put_row(act[t], None, o, jnp.concatenate([edge(g, b, r, (0,), (16,)), side], axis=0))
 
         return run
 
@@ -186,29 +220,45 @@
         def run(b):
             for r in range(16):
                 i = 16 * b + r
-                g = norm_back(feat[t, i].astype(F32), gain1[...], acc[t % 2][i, 0:32])
+                g = norm_back(feat[t, i].astype(F32), gain1[...], acc_last[t][i, :32])
                 out[t, i] = (block[t][i + 2] + g).astype(BF16)
 
         return run
+
+    def split(value, b, main, strip, add):
+        main[pl.ds(17 * b, 17)] = value[: 17 * 32].reshape(17, 32, 192) + add
+        strip[pl.ds(2 * b, 3)] = value[17 * 32 :].reshape(3, 16, 192) + add
 
     def first_conv(t):
         frames = range(max(0, t - 2), t + 1)
 
         def run(b):
             w = jnp.concatenate([weight_rows(w1, s - t + 2) for s in frames], axis=0)
-            value = jnp.dot(operand(act, frames, 17 * b, 17, WIDE), w, preferred_element_type=F32)
-            pre[t][pl.ds(17 * b, 17)] = value.reshape(17, WIDE, 192)[:, :COLS] + bias[...].reshape(1, 1, 192)
-
-        return run
-
-    def adjoint(src, w, t, rows, cols):
+            lhs = operand(act, act_strip, frames, 17 * b, 17, 2 * b)
+            value = jnp.dot(lhs, w, preferred_element_type=F32)
+            split(value, b, pre[t], pre_strip[t], bias[...].reshape(1, 1, 192))
+
+        return run
+
+    def transposed(lhs, w, frames):
+        rhs = jnp.concatenate([w[s - frames[0]] for s in frames], axis=1)
+        return lax.dot_general(lhs, rhs, (((1,), (1,)), ((), ())), preferred_element_type=F32)
+
+    def second(t):
         frames = range(t, min(4, t + 3))
 
         def run(b):
-            rhs = jnp.concatenate([w[s - t] for s in frames], axis=1)
-            lhs = operand(src, frames, rows * b, rows, cols)
-            value = lax.dot_general(lhs, rhs, (((1,), (1,)), ((), ())), preferred_element_type=F32)
-            acc[t % 2][pl.ds(rows * b, rows), :cols] = value.reshape(rows, cols, 192)
+            value = transposed(operand(grad, grad_strip, frames, 17 * b, 17, 2 * b), w2t, frames)
+            split(value, b, acc[t % 2], acc_strip[t % 2], 0.0)
+
+        return run
+
+    def last(t):
+        frames = range(t, min(4, t + 3))
+
+        def run(b):
+            value = transposed(operand(act, None, frames, 16 * b, 16, 0), w1t, frames)
+            acc_last[t][pl.ds(16 * b, 16), :32] = value.reshape(16, 32, 192)
 
         return run
 
@@ -219,33 +269,28 @@
             parts = [src[0, pl.ds(18 * b, 18)], src[1, pl.ds(18 * b, 18)], src[0, pl.ds(18 * b + 1, 18)]]
             lhs = jnp.concatenate([x.reshape(18 * WIDE, 384) for x in parts], axis=1)
             value = lax.dot_general(lhs, wu[...], (((1,), (1,)), ((), ())), preferred_element_type=F32)
-            acc[t % 2][pl.ds(18 * b, 18)] = value.reshape(18, WIDE, 192)
-
-        return run
-
-    second = lambda t: adjoint(grad, w2t, t, 17, WIDE)
-    last = lambda t: adjoint(act, w1t, t, 16, 32)
+            acc_up[t % 2][pl.ds(18 * b, 18)] = value.reshape(18, WIDE, 192)[:, :COLS]
+
+        return run
+
+    act_done = lambda t: lambda: build_strip(act_strip[t], act_tail)
+    grad_done = lambda t: lambda: build_strip(grad_strip[t], grad_tail)
+    second_done = lambda t: lambda: strip_grad(t)
     steps = [
-        [activate(0)],
-        [first_conv(0), activate(1)],
-        [first_conv(1), activate(2)],
-        [first_conv(2), activate(3)],
-        [first_conv(3), pool(0)],
-        [up_conv(0), pool(1)],
-        [up_conv(1), keep_block(0), pool(2)],
-        [up_conv(2), keep_block(1), pool(3)],
-        [up_conv(3), keep_block(2)],
-        [second(0), keep_block(3)],
-        [second(1), pre_grad(0)],
-        [second(2), pre_grad(1)],
-        [second(3), pre_grad(2)],
-        [last(0), pre_grad(3)],
-        [last(1), finish(0)],
-        [last(2), finish(1)],
-        [last(3), finish(2)],
-        [finish(3)],
+        ([activate(0), pool(3)], [act_done(0)]),
+        ([first_conv(0), up_conv(3), activate(1), pool(2)], [act_done(1)]),
+        ([first_conv(1), up_conv(2), activate(2), keep_block(3)], [act_done(2), grad_done(3)]),
+        ([first_conv(2), activate(3), keep_block(2)], [act_done(3), grad_done(2)]),
+        ([first_conv(3), second(3), pool(1), pool(0)], [second_done(3)]),
+        ([second(2), up_conv(1), pre_grad(3)], [second_done(2)]),
+        ([up_conv(0), last(3), keep_block(1), pre_grad(2)], [grad_done(1)]),
+        ([second(1), keep_block(0), finish(3)], [grad_done(0), second_done(1)]),
+        ([second(0), pre_grad(1)], [second_done(0)]),
+        ([last(2), last(1), pre_grad(0)], []),
+        ([last(0), finish(2), finish(1)], []),
+        ([finish(0)], []),
     ]
-    for jobs in steps:
+    for jobs, then in steps:
 
         def step(b, carry):
             for job in jobs:
@@ -253,6 +298,8 @@
             return carry
 
         lax.fori_loop(0, 2, step, 0)
+        for job in then:
+            job()
 
 
 def per_device(
@@ -288,14 +335,22 @@
         out_shape=jax.ShapeDtypeStruct(features.shape, BF16),
         in_specs=[pl.BlockSpec(memory_space=pltpu.SMEM)] + [vmem] * 12,
         out_specs=vmem,
-        scratch_shapes=[pltpu.VMEM((36, WIDE, 640), BF16)] * 8
-        + [pltpu.VMEM((34, COLS, 192), F32)] * 4
+        scratch_shapes=[pltpu.VMEM((36, 32, 640), BF16)] * 8
+        + [pltpu.VMEM((DEEP + 2, 16, 640), BF16)] * 8
+        + [pltpu.VMEM((34, 32, 192), F32)] * 4
+        + [pltpu.VMEM((DEEP, 16, 192), F32)] * 4
         + [pltpu.VMEM((36, 32, 192), F32)] * 4
-        + [pltpu.VMEM((36, WIDE, 192), F32)] * 2
+        + [pltpu.VMEM((36, COLS, 192), F32)] * 2
+        + [pltpu.VMEM((34, 32, 192), F32)] * 2
+        + [pltpu.VMEM((DEEP, 16, 192), F32)] * 2
         + [pltpu.VMEM((2, 37, WIDE, 384), BF16)] * 2
+        + [pltpu.VMEM((32, 32, 192), F32)]
+        + [pltpu.VMEM((5, 8 * (7 + 7 * DEEP), 128), F32)] * 2
         + [
+            pltpu.VMEM((16 * DEEP, 192), F32),
             pltpu.VMEM((16, 2, 80, 128), F32),
             pltpu.VMEM((COLS, 192), F32),
+            pltpu.VMEM((DEEP, 16, 192), F32),
             pltpu.VMEM((3, 192, 1792), BF16),
             pltpu.VMEM((3, 192, 1792), BF16),
             pltpu.VMEM((192, 1152), BF16),

time: 113 us -> 105 us (0.929)
  Pallas kernels: 69.9 us -> 62.1 us
    pallas_call x1, Pallas kernels: 69.9 us -> 62.1 us  [per_device(): pl.pallas_call(body, out_shape=jax.ShapeDtypeStruct(features.shape, BF16)...]
where the time goes in v1:
time: 105 us; the launch traced here: 103 us
  Pallas kernels  62.1 us (59%)
  starting transfers between devices  17.1 us (16%)
  waiting for transfers between devices  14.3 us (14%)
  local copies, waits for them, and re-layouts  6.76 us (6%)
  other arithmetic  2.89 us (3%)
    pallas_call x1, Pallas kernels, per_device(): pl.pallas_call(body, out_shape=jax.ShapeDtypeStruct(features.shape, BF16)...  62.1 us
    ppermute x2, starting transfers between devices, shift_pair(): lax.ppermute(value_down, axis, down)  11.7 us
    ppermute x2, waiting for transfers between devices, shift_pair(): lax.ppermute(value_up, axis, up)  10.9 us
    ppermute x2, starting transfers between devices, shift_pair(): lax.ppermute(value_up, axis, up)  5.41 us
    ppermute x2, waiting for transfers between devices, shift_pair(): lax.ppermute(value_down, axis, down)  3.42 us
  transfers between devices with their start and end apart: 4, of which 4 were waited for; matrix products, arithmetic and copies ran while one was open for 3% of the time, Pallas kernels for 0%

profile of v1, /device:TPU:6, one launch (start us, length us, event | category | flops | bytes accessed | tf_op | source)
XLA Modules:
  0.0 103.4 jit_solution(3381545606198467565)
XLA Ops:
  0.0 1.7 %fusion.19 = (bf16[4,32,2,96]{3,2,1,0:T(2,128)(2,1)S(1)}, bf16[4,32,2,96]{3,2,1,0:T(2,128)(2,1)S(1)}, bf16[4,32,2,96]{3,2,1,0:T(2,128)(2,1)S(1)}, bf16[4,32,2,96]{3,2,1,0:T(2,128)(2,1)S(1)}) fusion(bf16[4,32,32,192]{3,2,1,0:T(8,128)(2,1)} %refs_1_.1), kind=kLoop, calls=%fused_computation.29 | loop fusion | bytes 393216 | tf_op jit(solution)/shard_map/slice | solution.py:25
  1.7 1.4 %fusion.17 = (bf16[4,64,5,96]{3,2,1,0:T(8,128)(2,1)S(1)}, bf16[4,64,5,96]{3,2,1,0:T(8,128)(2,1)S(1)}) fusion(bf16[4,64,64,96]{3,2,1,0:T(8,128)(2,1)} %refs_3_.1), kind=kLoop, calls=%fused_computation.27 | loop fusion | bytes 983040 | tf_op jit(solution)/shard_map/slice | solution.py:309
  3.1 0.4 fusion.12
  3.6 1.9 %collective-permute-start.1 = (bf16[4,64,8,96]{3,2,1,0:T(8,128)(2,1)S(1)}, bf16[4,64,8,96]{3,2,1,0:T(8,128)(2,1)S(1)}, u32[]{:S(2)}, u32[]{:S(2)}) collective-permute-start(bf16[4,64,8,96]{3,2,1,0:T(8,128)(2,1)S(1)} %fusion.12), channel_id=1, source_target_pairs={{0,1},{1,2},{2,3},{3,4},{4,5},{5,6},{6,7},{7,8},{8,9},{9,10},{10,1... | collective-permute-start | bytes 1179656 | tf_op jit(solution)/shard_map/ppermute | solution.py:20
  5.5 0.4 fusion.10
  5.9 7.3 %collective-permute-start = (bf16[4,64,8,96]{3,2,1,0:T(8,128)(2,1)S(1)}, bf16[4,64,8,96]{3,2,1,0:T(8,128)(2,1)S(1)}, u32[]{:S(2)}, u32[]{:S(2)}) collective-permute-start(bf16[4,64,8,96]{3,2,1,0:T(8,128)(2,1)S(1)} %fusion.10), channel_id=1, source_target_pairs={{1,0},{2,1},{3,2},{4,3},{5,4},{6,5},{7,6},{8,7},{9,8},{10,9},{11,1... | collective-permute-start | bytes 1179656 | tf_op jit(solution)/shard_map/ppermute | solution.py:20
  13.2 0.1 pad.26.clone
  13.3 0.1 pad.22.clone
  13.4 1.1 %fusion.16 = (bf16[4,5,64,96]{3,2,1,0:T(8,128)(2,1)S(1)}, bf16[4,5,64,96]{3,2,1,0:T(8,128)(2,1)S(1)}) fusion(bf16[4,64,64,96]{3,2,1,0:T(8,128)(2,1)} %refs_3_.1), kind=kLoop, calls=%fused_computation.26 | loop fusion | bytes 983040 | tf_op jit(solution)/shard_map/slice | solution.py:324
  14.5 1.0 fusion.18
  15.5 2.2 %collective-permute-done.1 = bf16[4,64,8,96]{3,2,1,0:T(8,128)(2,1)S(1)} collective-permute-done((bf16[4,64,8,96]{3,2,1,0:T(8,128)(2,1)S(1)}, bf16[4,64,8,96]{3,2,1,0:T(8,128)(2,1)S(1)}, u32[]{:S(2)}, u32[]{:S(2)}) %collective-permute-start.1) | collective-permute-done | bytes 393248 | tf_op jit(solution)/shard_map/ppermute | solution.py:20
  17.7 0.1 fusion.23
  17.8 2.1 %collective-permute-done = bf16[4,64,8,96]{3,2,1,0:T(8,128)(2,1)S(1)} collective-permute-done((bf16[4,64,8,96]{3,2,1,0:T(8,128)(2,1)S(1)}, bf16[4,64,8,96]{3,2,1,0:T(8,128)(2,1)S(1)}, u32[]{:S(2)}, u32[]{:S(2)}) %collective-permute-start) | collective-permute-done | bytes 393248 | tf_op jit(solution)/shard_map/ppermute | solution.py:20
  19.9 0.1 fusion.22
  20.0 0.7 maximum_maximum_fusion.refs_2_
  20.7 0.0 copy-start.1
  20.7 0.5 pad_maximum_fusion.refs_4_
  21.2 0.0 copy-start
  21.2 0.3 copy-done.1
  21.5 0.1 fusion.9
  21.6 3.5 %collective-permute-start.2 = (bf16[4,7,80,96]{3,2,1,0:T(8,128)(2,1)S(1)}, bf16[4,7,80,96]{3,2,1,0:T(8,128)(2,1)S(1)}, u32[]{:S(2)}, u32[]{:S(2)}) collective-permute-start(bf16[4,7,80,96]{3,2,1,0:T(8,128)(2,1)S(1)} %fusion.9), channel_id=1, source_target_pairs={{0,16},{16,32},{32,48},{48,64},{64,80},{80,96},{96,112},{1,17},{17... | collective-permute-start | bytes 1290248 | tf_op jit(solution)/shard_map/ppermute | solution.py:20
  25.2 0.1 fusion.7
  25.3 0.0 copy-done
  25.3 4.5 %collective-permute-start.3 = (bf16[4,7,80,96]{3,2,1,0:T(8,128)(2,1)S(1)}, bf16[4,7,80,96]{3,2,1,0:T(8,128)(2,1)S(1)}, u32[]{:S(2)}, u32[]{:S(2)}) collective-permute-start(bf16[4,7,80,96]{3,2,1,0:T(8,128)(2,1)S(1)} %fusion.7), channel_id=1, source_target_pairs={{16,0},{32,16},{48,32},{64,48},{80,64},{96,80},{112,96},{17,1},{33... | collective-permute-start | bytes 1290248 | tf_op jit(solution)/shard_map/ppermute | solution.py:20
  29.8 0.6 add_convert_fusion.refs_0_
  30.4 8.8 %collective-permute-done.2.refs_5_ = bf16[4,7,80,96]{3,2,1,0:T(8,128)(2,1)S(1)} collective-permute-done((bf16[4,7,80,96]{3,2,1,0:T(8,128)(2,1)S(1)}, bf16[4,7,80,96]{3,2,1,0:T(8,128)(2,1)S(1)}, u32[]{:S(2)}, u32[]{:S(2)}) %collective-permute-start.2) | collective-permute-done | bytes 430112 | tf_op jit(solution)/shard_map/ppermute | solution.py:20
  39.1 0.0 copy-start.2
  39.1 1.4 %collective-permute-done.3.refs_6_ = bf16[4,7,80,96]{3,2,1,0:T(8,128)(2,1)S(1)} collective-permute-done((bf16[4,7,80,96]{3,2,1,0:T(8,128)(2,1)S(1)}, bf16[4,7,80,96]{3,2,1,0:T(8,128)(2,1)S(1)}, u32[]{:S(2)}, u32[]{:S(2)}) %collective-permute-start.3) | collective-permute-done | bytes 430112 | tf_op jit(solution)/shard_map/ppermute | solution.py:20
  40.5 0.0 copy-start.3
  40.5 0.0 copy-done.2
  40.5 0.8 copy-done.3
  41.3 62.1 %block_backward.1 = bf16[4,32,32,192]{3,2,1,0:T(8,128)(2,1)} custom-call(s32[4]{0:T(128)} %add_convert_fusion.refs_0_, bf16[4,32,32,192]{3,2,1,0:T(8,128)(2,1)} %refs_1_.1, bf16[4,32,8,192]{3,2,1,0:T(8,128)(2,1)} %copy-done.1, bf16[4,64,64,96]{3,2,1,0:T(8,128)(2,1)} %refs_3_.1, bf16[4,64,16,96]{3,2,1,0:T(8,128)(2,1)} %copy-done, ...), custom_call_target="tpu_custom_call" | custom-call | tf_op jit(solution)/shard_map/block_backward/pallas_call | solution.py:333
  (6 shorter events, 0.1 us)
Async XLA Ops:
  3.6 14.1 %collective-permute-start.1 = (bf16[4,64,8,96]{3,2,1,0:T(8,128)(2,1)S(1)}, bf16[4,64,8,96]{3,2,1,0:T(8,128)(2,1)S(1)}, u32[]{:S(2)}, u32[]{:S(2)}) collective-permute-start(bf16[4,64,8,96]{3,2,1,0:T(8,128)(2,1)S(1)} %fusion.12), channel_id=1, source_target_pairs={{0,1},{1,2},{2,3},{3,4},{4,5},{5,6},{6,7},{7,8},{8,9},{9,10},{10,1... | collective-permute-start | bytes 1179656 | tf_op jit(solution)/shard_map/ppermute | solution.py:20
  5.9 13.9 %collective-permute-start = (bf16[4,64,8,96]{3,2,1,0:T(8,128)(2,1)S(1)}, bf16[4,64,8,96]{3,2,1,0:T(8,128)(2,1)S(1)}, u32[]{:S(2)}, u32[]{:S(2)}) collective-permute-start(bf16[4,64,8,96]{3,2,1,0:T(8,128)(2,1)S(1)} %fusion.10), channel_id=1, source_target_pairs={{1,0},{2,1},{3,2},{4,3},{5,4},{6,5},{7,6},{8,7},{9,8},{10,9},{11,1... | collective-permute-start | bytes 1179656 | tf_op jit(solution)/shard_map/ppermute | solution.py:20
  20.7 0.8 copy-start.1
  21.2 4.1 %copy-start = (bf16[4,64,16,96]{3,2,1,0:T(8,128)(2,1)}, bf16[4,64,16,96]{3,2,1,0:T(8,128)(2,1)S(1)}, u32[]{:S(2)}) copy-start(bf16[4,64,16,96]{3,2,1,0:T(8,128)(2,1)S(1)} %pad_maximum_fusion.refs_4_) | copy-start | bytes 2359300
  21.6 17.5 %collective-permute-start.2 = (bf16[4,7,80,96]{3,2,1,0:T(8,128)(2,1)S(1)}, bf16[4,7,80,96]{3,2,1,0:T(8,128)(2,1)S(1)}, u32[]{:S(2)}, u32[]{:S(2)}) collective-permute-start(bf16[4,7,80,96]{3,2,1,0:T(8,128)(2,1)S(1)} %fusion.9), channel_id=1, source_target_pairs={{0,16},{16,32},{32,48},{48,64},{64,80},{80,96},{96,112},{1,17},{17... | collective-permute-start | bytes 1290248 | tf_op jit(solution)/shard_map/ppermute | solution.py:20
  25.3 15.2 %collective-permute-start.3 = (bf16[4,7,80,96]{3,2,1,0:T(8,128)(2,1)S(1)}, bf16[4,7,80,96]{3,2,1,0:T(8,128)(2,1)S(1)}, u32[]{:S(2)}, u32[]{:S(2)}) collective-permute-start(bf16[4,7,80,96]{3,2,1,0:T(8,128)(2,1)S(1)} %fusion.7), channel_id=1, source_target_pairs={{16,0},{32,16},{48,32},{64,48},{80,64},{96,80},{112,96},{17,1},{33... | collective-permute-start | bytes 1290248 | tf_op jit(solution)/shard_map/ppermute | solution.py:20
  39.1 1.4 %copy-start.2 = (bf16[4,7,80,96]{3,2,1,0:T(8,128)(2,1)}, bf16[4,7,80,96]{3,2,1,0:T(8,128)(2,1)S(1)}, u32[]{:S(2)}) copy-start(bf16[4,7,80,96]{3,2,1,0:T(8,128)(2,1)S(1)} %collective-permute-done.2.refs_5_) | copy-start | bytes 1290244
  40.5 0.8 copy-start.3

commit v2 on v1

--- a/solution.py
+++ b/solution.py
@@ -18,11 +18,6 @@
     up = [(i, (i + 1) % count) for i in range(count - 1)]
     down = [(j, i) for i, j in up]
     return lax.ppermute(value_up, axis, up), lax.ppermute(value_down, axis, down)
-
-
-def halves(field, axis):
-    half = field.shape[-1] // 2
-    return jnp.concatenate([field[..., :half], field[..., half:]], axis=axis)
 
 
 def rms_scale(value):
@@ -98,18 +93,87 @@
     return jnp.concatenate(parts, axis=1)
 
 
-def body(*refs):
-    flags, feat, feat_side, cot, cot_side, before, after, w1, w2, wup, bias, gain1, gain2, out = refs[:14]
-    act, grad, act_strip, grad_strip, pre, pre_strip, block = (refs[14 + 4 * n : 18 + 4 * n] for n in range(7))
-    acc_up, acc, acc_strip, pooled = (refs[42 + 2 * n : 44 + 2 * n] for n in range(4))
-    acc_last = (refs[50], acc_up[1], acc_up[0], refs[50])
-    act_tail, grad_tail, edges, line, mask, strip_mask, w2t, w1t, wu = refs[51:]
+def conv_dot(lhs, w, axis):
+    return lax.dot_general(lhs, w, (((1,), (axis,)), ((), ())), preferred_element_type=F32)
+
+
+def split(value, b, main, strip, add):
+    main[pl.ds(17 * b, 17)] = value[: 17 * 32].reshape(17, 32, 192) + add
+    strip[pl.ds(2 * b, 3)] = value[17 * 32 :].reshape(3, 16, 192) + add
+
+
+def run_steps(steps):
+    for jobs, then in steps:
+
+        def step(b, carry):
+            for job in jobs:
+                job(b)
+            return carry
+
+        lax.fori_loop(0, 2, step, 0)
+        for job in then:
+            job()
+
+
+def forward(*refs):
+    feat, feat_side, before, after, w1, bias, gain1, pre, pre_strip = refs[:9]
+    act, act_strip = refs[9:13], refs[13:17]
+    act_tail, act_rows = refs[17:]
+    for n in range(4):
+        act[n][35, :, 576:640] = jnp.zeros((32, 64), BF16)
+    act_tail[:, 35 * 8 :, :] = jnp.zeros((5, 56, 128), F32)
+
+    def activate(t):
+        def one(r, x):
+            n = x * rms_scale(x) * gain1[...]
+            act_rows[r] = n * sigmoid(n)
+
+        def run(b):
+            for r in range(2):
+                x = jnp.where(b == 0, before[t, r].astype(F32), after[t, r].astype(F32))
+                one(r, x)
+            for r in range(16):
+                i = 16 * b + r
+                one(r + 2, jnp.concatenate([feat[t, i].astype(F32), feat_side[t, i].astype(F32)], axis=0))
+            for r in range(18):
+                put_row(act[t], act_tail, r + 34 * b if r < 2 else r + 16 * b, act_rows[r])
+
+        return run
+
+    def first_conv(t):
+        frames = range(max(0, t - 2), t + 1)
+
+        def run(b):
+            w = jnp.concatenate([weight_rows(w1, s - t + 2) for s in frames], axis=0)
+            lhs = operand(act, act_strip, frames, 17 * b, 17, 2 * b)
+            value = conv_dot(lhs, w, 0)
+            split(value, b, pre.at[t], pre_strip.at[t], bias[...].reshape(1, 1, 192))
+
+        return run
+
+    done = lambda t: lambda: build_strip(act_strip[t], act_tail)
+    run_steps(
+        [
+            ([activate(0)], [done(0)]),
+            ([first_conv(0), activate(1)], [done(1)]),
+            ([first_conv(1), activate(2)], [done(2)]),
+            ([first_conv(2), activate(3)], [done(3)]),
+            ([first_conv(3)], []),
+        ]
+    )
+
+
+def backward(*refs):
+    flags, feat, pre, pre_strip, cot, cot_side, before, after, w1, w2, wup, gain1, gain2, out = refs[:14]
+    act, grad, grad_strip, block = (refs[14 + 4 * n : 18 + 4 * n] for n in range(4))
+    acc_up, acc, acc_strip, pooled = (refs[30 + 2 * n : 32 + 2 * n] for n in range(4))
+    acc_last = (refs[38], acc_up[1], acc_up[0], refs[38])
+    grad_tail, grad_rows, edges, line, mask, strip_mask, w2t, w1t, wu = refs[39:]
 
     for n in range(4):
         act[n][35, :, 576:640] = jnp.zeros((32, 64), BF16)
         grad[n][35, :, 576:640] = jnp.zeros((32, 64), BF16)
-    for tail in (act_tail, grad_tail):
-        tail[:, 35 * 8 :, :] = jnp.zeros((5, 56, 128), F32)
+    grad_tail[:, 35 * 8 :, :] = jnp.zeros((5, 56, 128), F32)
     line[...] = jnp.zeros_like(line)
     s = lax.broadcasted_iota(jnp.int32, mask.shape, 0)
     good = (s < 32) | ((s < 34) & (flags[3] > 0)) | ((s >= 38) & (flags[2] > 0))
@@ -134,22 +198,6 @@
             return value * jnp.where((b == 1) & (flags[1] == 0), 0.0, 1.0)
         return value
 
-    def activate(t):
-        def one(e, x):
-            x = x.astype(F32)
-            n = x * rms_scale(x) * gain1[...]
-            put_row(act[t], act_tail, e, n * sigmoid(n))
-
-        def run(b):
-            for r in range(2):
-                x = jnp.where(b == 0, before[t, r].astype(F32), after[t, r].astype(F32))
-                one(r + 34 * b, jnp.concatenate([x[:COLS], x[COLS:]], axis=1))
-            for r in range(16):
-                i = 16 * b + r
-                one(i + 2, jnp.concatenate([feat[t, i].astype(F32), feat_side[t, i].astype(F32)], axis=0))
-
-        return run
-
     def pool(t):
         dst = pooled[t % 2]
 
@@ -166,8 +214,8 @@
                 dst[m, e, :COLS, 256:384] = (odd + pltpu.roll(even, 39, 0)).astype(BF16)
 
         def run(b):
-            top = [before[t, 2 + r].astype(F32) for r in range(5)] + [own(0), own(1)]
-            low = [own(63)] + [after[t, 2 + r].astype(F32) for r in range(5)]
+            top = [before[t, r].astype(F32) for r in range(5)] + [own(0), own(1)]
+            low = [own(63)] + [after[t, r].astype(F32) for r in range(5)]
             low.append(low[-1])
             ends = [jnp.where(b == 0, x, y) for x, y in zip(top, low)]
             for r in range(3):
@@ -197,7 +245,7 @@
         return scale * u - v * (scale * scale * scale * mean)
 
     def strip_grad(t):
-        g = norm_back(pre_strip[t][...], gain2[...].reshape(1, 1, 192), acc_strip[t % 2][...])
+        g = norm_back(pre_strip[t], gain2[...].reshape(1, 1, 192), acc_strip[t % 2][...])
         g = g * strip_mask[...]
         for r in range(DEEP):
             edges[16 * r : 16 * r + 16, :] = g[r]
@@ -208,11 +256,13 @@
         def run(b):
             for r in range(17):
                 o = 17 * b + r
-                g = norm_back(pre[t][o], gain2[...], acc[t % 2][o])
+                g = norm_back(pre[t, o], gain2[...], acc[t % 2][o])
                 at = 16 * lax.rem(o, DEEP) + lax.div(o, DEEP)
                 left, right = edges[pl.ds(at, 1), :], edges[pl.ds(at + 8, 1), :]
-                side = jnp.where(spot == 0, right, jnp.where(spot == 7, left, 0.0))
-                put_row(act[t], None, o, jnp.concatenate([edge(g, b, r, (0,), (16,)), side], axis=0))
+                grad_rows[r, :32] = edge(g, b, r, (0,), (16,))
+                grad_rows[r, 32:] = jnp.where(spot == 0, right, jnp.where(spot == 7, left, 0.0))
+            for r in range(17):
+                put_row(act[t], None, 17 * b + r, grad_rows[r])
 
         return run
 
@@ -225,24 +275,8 @@
 
         return run
 
-    def split(value, b, main, strip, add):
-        main[pl.ds(17 * b, 17)] = value[: 17 * 32].reshape(17, 32, 192) + add
-        strip[pl.ds(2 * b, 3)] = value[17 * 32 :].reshape(3, 16, 192) + add
-
-    def first_conv(t):
-        frames = range(max(0, t - 2), t + 1)
-
-        def run(b):
-            w = jnp.concatenate([weight_rows(w1, s - t + 2) for s in frames], axis=0)
-            lhs = operand(act, act_strip, frames, 17 * b, 17, 2 * b)
-            value = jnp.dot(lhs, w, preferred_element_type=F32)
-            split(value, b, pre[t], pre_strip[t], bias[...].reshape(1, 1, 192))
-
-        return run
-
     def transposed(lhs, w, frames):
-        rhs = jnp.concatenate([w[s - frames[0]] for s in frames], axis=1)
-        return lax.dot_general(lhs, rhs, (((1,), (1,)), ((), ())), preferred_element_type=F32)
+        return conv_dot(lhs, jnp.concatenate([w[s - frames[0]] for s in frames], axis=1), 1)
 
     def second(t):
         frames = range(t, min(4, t + 3))
@@ -268,85 +302,84 @@
         def run(b):
             parts = [src[0, pl.ds(18 * b, 18)], src[1, pl.ds(18 * b, 18)], src[0, pl.ds(18 * b + 1, 18)]]
             lhs = jnp.concatenate([x.reshape(18 * WIDE, 384) for x in parts], axis=1)
-            value = lax.dot_general(lhs, wu[...], (((1,), (1,)), ((), ())), preferred_element_type=F32)
+            value = conv_dot(lhs, wu[...], 1)
             acc_up[t % 2][pl.ds(18 * b, 18)] = value.reshape(18, WIDE, 192)[:, :COLS]
 
         return run
 
-    act_done = lambda t: lambda: build_strip(act_strip[t], act_tail)
     grad_done = lambda t: lambda: build_strip(grad_strip[t], grad_tail)
     second_done = lambda t: lambda: strip_grad(t)
-    steps = [
-        ([activate(0), pool(3)], [act_done(0)]),
-        ([first_conv(0), up_conv(3), activate(1), pool(2)], [act_done(1)]),
-        ([first_conv(1), up_conv(2), activate(2), keep_block(3)], [act_done(2), grad_done(3)]),
-        ([first_conv(2), activate(3), keep_block(2)], [act_done(3), grad_done(2)]),
-        ([first_conv(3), second(3), pool(1), pool(0)], [second_done(3)]),
-        ([second(2), up_conv(1), pre_grad(3)], [second_done(2)]),
-        ([up_conv(0), last(3), keep_block(1), pre_grad(2)], [grad_done(1)]),
-        ([second(1), keep_block(0), finish(3)], [grad_done(0), second_done(1)]),
-        ([second(0), pre_grad(1)], [second_done(0)]),
-        ([last(2), last(1), pre_grad(0)], []),
-        ([last(0), finish(2), finish(1)], []),
-        ([finish(0)], []),
-    ]
-    for jobs, then in steps:
-
-        def step(b, carry):
-            for job in jobs:
-                job(b)
-            return carry
-
-        lax.fori_loop(0, 2, step, 0)
-        for job in then:
-            job()
+    run_steps(
+        [
+            ([pool(3)], []),
+            ([up_conv(3), pool(2)], []),
+            ([up_conv(2), keep_block(3), pool(1)], [grad_done(3)]),
+            ([second(3), up_conv(1), keep_block(2), pool(0)], [grad_done(2), second_done(3)]),
+            ([second(2), up_conv(0), keep_block(1), pre_grad(3)], [grad_done(1), second_done(2)]),
+            ([last(3), second(1), keep_block(0), pre_grad(2)], [grad_done(0), second_done(1)]),
+            ([second(0), last(2), pre_grad(1), finish(3)], [second_done(0)]),
+            ([last(1), pre_grad(0), finish(2)], []),
+            ([last(0), finish(1)], []),
+            ([finish(0)], []),
+        ]
+    )
 
 
 def per_device(
     features, conv_first, bias_first, gain_first, conv_second, gain_second, up_weight, cotangent
 ):
-    def cols(lo_f, lo_c):
-        parts = [cotangent[:, :, lo_c : lo_c + 5], halves(features[:, :, lo_f : lo_f + 2], 1)]
-        return jnp.pad(jnp.concatenate(parts, axis=2), ((0, 0), (0, 0), (0, 1), (0, 0)))
-
-    left, right = shift_pair(cols(30, 59), cols(0, 0), "wa")
-
-    def ring(first, last, width):
-        gap = jnp.zeros(first.shape[:2] + (width - 2 * first.shape[2], first.shape[3]), BF16)
-        return jnp.concatenate([first, gap, last], axis=2)
-
-    cot_side = ring(right[:, :, :5], left[:, :, :5], 16)
-    whole = lambda side: jnp.concatenate([side[:, :32, 5:7], side[:, 32:, 5:7]], axis=3)
-    feat_side = ring(whole(right), whole(left), 8)
-
-    def rows(lo_f, lo_c):
-        f = jnp.concatenate([features[:, lo_f : lo_f + 2], feat_side[:, lo_f : lo_f + 2]], axis=2)
-        c = jnp.concatenate([cotangent[:, lo_c : lo_c + 5], cot_side[:, lo_c : lo_c + 5]], axis=2)
-        return jnp.concatenate([halves(f, 2), c], axis=1)
-
-    before, after = shift_pair(rows(30, 59), rows(0, 0), "ha")
+    left, right = shift_pair(features[:, :, 30:], features[:, :, :2], "wa")
+    gap = jnp.zeros(left.shape[:2] + (4, 192), BF16)
+    feat_side = jnp.concatenate([right, gap, left], axis=2)
+    cot_left, cot_right = shift_pair(cotangent[:, :, 56:], cotangent[:, :, :8], "wa")
+    cot_side = jnp.concatenate([cot_right, cot_left], axis=2)
+
+    def rows(field, side, lo, count):
+        part = slice(lo, lo + count)
+        return jnp.concatenate([field[:, part], side[:, part]], axis=2)
+
+    before, after = shift_pair(rows(features, feat_side, 30, 2), rows(features, feat_side, 0, 2), "ha")
+    cot_up, cot_down = rows(cotangent, cot_side, 59, 5), rows(cotangent, cot_side, 0, 5)
+    before, after, cot_up, cot_down = lax.optimization_barrier((before, after, cot_up, cot_down))
+    cot_before, cot_after = shift_pair(cot_up, cot_down, "ha")
+
+    bias, gain1, gain2 = (x.reshape(1, 192) for x in (bias_first, gain_first, gain_second))
     ha, wa = lax.axis_index("ha"), lax.axis_index("wa")
     flags = jnp.stack(
         [ha > 0, ha < lax.axis_size("ha") - 1, wa > 0, wa < lax.axis_size("wa") - 1]
     ).astype(jnp.int32)
     vmem = pl.BlockSpec(memory_space=pltpu.VMEM)
+    pre, pre_strip = pl.pallas_call(
+        forward,
+        out_shape=[
+            jax.ShapeDtypeStruct((4, 34, 32, 192), F32),
+            jax.ShapeDtypeStruct((4, DEEP, 16, 192), F32),
+        ],
+        in_specs=[vmem] * 7,
+        out_specs=[vmem] * 2,
+        scratch_shapes=[pltpu.VMEM((36, 32, 640), BF16)] * 4
+        + [pltpu.VMEM((DEEP + 2, 16, 640), BF16)] * 4
+        + [pltpu.VMEM((5, 8 * (7 + 7 * DEEP), 128), F32), pltpu.VMEM((18, COLS, 192), F32)],
+        compiler_params=pltpu.CompilerParams(vmem_limit_bytes=28 * 1024 * 1024),
+        cost_estimate=pl.CostEstimate(flops=20_000_000_000, transcendentals=1_000_000, bytes_accessed=12_000_000),
+        name="forward_block",
+    )(features, feat_side, before, after, conv_first, bias, gain1)
     return pl.pallas_call(
-        body,
+        backward,
         out_shape=jax.ShapeDtypeStruct(features.shape, BF16),
         in_specs=[pl.BlockSpec(memory_space=pltpu.SMEM)] + [vmem] * 12,
         out_specs=vmem,
         scratch_shapes=[pltpu.VMEM((36, 32, 640), BF16)] * 8
-        + [pltpu.VMEM((DEEP + 2, 16, 640), BF16)] * 8
-        + [pltpu.VMEM((34, 32, 192), F32)] * 4
-        + [pltpu.VMEM((DEEP, 16, 192), F32)] * 4
+        + [pltpu.VMEM((DEEP + 2, 16, 640), BF16)] * 4
         + [pltpu.VMEM((36, 32, 192), F32)] * 4
         + [pltpu.VMEM((36, COLS, 192), F32)] * 2
         + [pltpu.VMEM((34, 32, 192), F32)] * 2
         + [pltpu.VMEM((DEEP, 16, 192), F32)] * 2
         + [pltpu.VMEM((2, 37, WIDE, 384), BF16)] * 2
         + [pltpu.VMEM((32, 32, 192), F32)]
-        + [pltpu.VMEM((5, 8 * (7 + 7 * DEEP), 128), F32)] * 2
         + [
+            pltpu.VMEM((5, 8 * (7 + 7 * DEEP), 128), F32),
+            pltpu.VMEM((17, COLS, 192), F32),
             pltpu.VMEM((16 * DEEP, 192), F32),
             pltpu.VMEM((16, 2, 80, 128), F32),
             pltpu.VMEM((COLS, 192), F32),
@@ -355,11 +388,11 @@
             pltpu.VMEM((3, 192, 1792), BF16),
             pltpu.VMEM((192, 1152), BF16),
         ],
-        compiler_params=pltpu.CompilerParams(vmem_limit_bytes=60 * 1024 * 1024),
-        name="block_backward",
+        compiler_params=pltpu.CompilerParams(vmem_limit_bytes=58 * 1024 * 1024),
+        name="backward_block",
     )(
-        flags, features, feat_side, cotangent, cot_side, before, after, conv_first, conv_second,
-        up_weight, bias_first.reshape(1, 192), gain_first.reshape(1, 192), gain_second.reshape(1, 192),
+        flags, features, pre, pre_strip, cotangent, cot_side, cot_before, cot_after, conv_first,
+        conv_second, up_weight, gain1, gain2,
     )
 
 

time: 105 us -> 108 us (1.029); the launches traced: 103 us -> 108 us
  starting transfers between devices: 17.1 us -> 33.7 us
  waiting for transfers between devices: 14.3 us -> 0.28 us
  local copies, waits for them, and re-layouts: 6.76 us -> 12.3 us
  Pallas kernels: 62.1 us -> 59.2 us
    ppermute x2 -> x4, starting transfers between devices: 11.7 us -> 23 us  [shift_pair(): lax.ppermute(value_down, axis, down)]
    ppermute x2 -> x4, waiting for transfers between devices: 10.9 us -> 0.01 us  [shift_pair(): lax.ppermute(value_up, axis, up)]
    ppermute x2 -> x4, starting transfers between devices: 5.41 us -> 10.7 us  [shift_pair(): lax.ppermute(value_up, axis, up)]
    unnamed x8 -> x21, local copies, waits for them, and re-layouts: 1.1 us -> 4.82 us
    ppermute x2 -> x4, waiting for transfers between devices: 3.42 us -> 0.27 us  [shift_pair(): lax.ppermute(value_down, axis, down)]
    pallas_call x1 -> x2, Pallas kernels: 62.1 us -> 59.2 us  [the longest x1 45 us: per_device(): pl.pallas_call(backward, out_shape=jax.ShapeDtypeStruct(features.shape, B...]
    concatenate x2, local copies, waits for them, and re-layouts: 0.15 us -> 1.25 us  [the longest x1 1.17 us: per_device(): cot_side = jnp.concatenate([cot_right, cot_left], axis=2)]
    slice x8 -> x6, local copies, waits for them, and re-layouts: 5.5 us -> 6.2 us  [the longest x1 2.2 us: per_device(): left, right = shift_pair(features[:, :, 30:], features[:, :, :2], 'wa')]
  transfers between devices with their start and end apart: 4 -> 8, of which waited for: 4 -> 1; matrix products, arithmetic and copies ran while one was open for 3% -> 8% of each run, Pallas kernels for 0% -> 13%
where the time goes in v2:
time: 108 us
  Pallas kernels  59.2 us (55%)
  starting transfers between devices  33.7 us (31%)
  local copies, waits for them, and re-layouts  12.3 us (11%)
  other arithmetic  2.26 us (2%)
    pallas_call x1, Pallas kernels, per_device(): pl.pallas_call(backward, out_shape=jax.ShapeDtypeStruct(features.shape, B...  45 us
    ppermute x4, starting transfers between devices, shift_pair(): lax.ppermute(value_down, axis, down)  23 us
    pallas_call x1, Pallas kernels, per_device(): pl.pallas_call(forward, out_shape=[jax.ShapeDtypeStruct((4, 34, 32, 192),...  14.2 us
    ppermute x4, starting transfers between devices, shift_pair(): lax.ppermute(value_up, axis, up)  10.7 us
    unnamed x21, local copies, waits for them, and re-layouts  4.82 us
    slice x1, local copies, waits for them, and re-layouts, per_device(): left, right = shift_pair(features[:, :, 30:], features[:, :, :2], 'wa')  2.2 us
  transfers between devices with their start and end apart: 8, of which 1 were waited for; matrix products, arithmetic and copies ran while one was open for 8% of the time, Pallas kernels for 13%

profile of v2, /device:TPU:6, one launch (start us, length us, event | category | flops | bytes accessed | tf_op | source)
XLA Modules:
  0.0 107.9 jit_solution(1798648666526948436)
XLA Ops:
  0.0 0.0 copy-start.1
  0.0 2.2 %fusion.3 = (bf16[4,32,2,192]{3,2,1,0:T(2,128)(2,1)}, bf16[4,32,2,192]{3,2,1,0:T(2,128)(2,1)S(1)}) fusion(bf16[4,32,32,192]{3,2,1,0:T(8,128)(2,1)} %refs_1_.1), kind=kLoop, calls=%fused_computation.11 | loop fusion | bytes 393216 | tf_op jit(solution)/shard_map/slice | solution.py:331
  2.2 6.2 %collective-permute-start = (bf16[4,32,2,192]{3,2,1,0:T(2,128)(2,1)}, bf16[4,32,2,192]{3,2,1,0:T(2,128)(2,1)S(1)}, u32[]{:S(2)}, u32[]{:S(2)}) collective-permute-start(bf16[4,32,2,192]{3,2,1,0:T(2,128)(2,1)} %get-tuple-element.23), channel_id=1, source_target_pairs={{1,0},{2,1},{3,2},{4,3},{5,4},{6,5},{7,6},{8,7},{9,8},{10,9},{11,1... | collective-permute-start | bytes 294920 | tf_op jit(solution)/shard_map/ppermute | solution.py:20
  8.4 1.9 %collective-permute-start.1 = (bf16[4,32,2,192]{3,2,1,0:T(2,128)(2,1)S(1)}, bf16[4,32,2,192]{3,2,1,0:T(2,128)(2,1)}, u32[]{:S(2)}, u32[]{:S(2)}) collective-permute-start(bf16[4,32,2,192]{3,2,1,0:T(2,128)(2,1)S(1)} %get-tuple-element.24), channel_id=1, source_target_pairs={{0,1},{1,2},{2,3},{3,4},{4,5},{5,6},{6,7},{7,8},{8,9},{9,10},{10,1... | collective-permute-start | bytes 294920 | tf_op jit(solution)/shard_map/ppermute | solution.py:20
  10.4 2.1 %fusion.1 = (bf16[4,64,8,96]{3,2,1,0:T(8,128)(2,1)}, bf16[4,64,8,96]{3,2,1,0:T(8,128)(2,1)S(1)}) fusion(bf16[4,64,64,96]{3,2,1,0:T(8,128)(2,1)} %refs_4_.3), kind=kLoop, calls=%fused_computation.9 | loop fusion | bytes 1572864 | tf_op jit(solution)/shard_map/slice | solution.py:334
  12.4 1.9 %collective-permute-start.5 = (bf16[4,64,8,96]{3,2,1,0:T(8,128)(2,1)}, bf16[4,64,8,96]{3,2,1,0:T(8,128)(2,1)}, u32[]{:S(2)}, u32[]{:S(2)}) collective-permute-start(bf16[4,64,8,96]{3,2,1,0:T(8,128)(2,1)} %get-tuple-element.19), channel_id=1, source_target_pairs={{0,1},{1,2},{2,3},{3,4},{4,5},{5,6},{6,7},{7,8},{8,9},{9,10},{10,1... | collective-permute-start | bytes 1179656 | tf_op jit(solution)/shard_map/ppermute | solution.py:20
  14.4 7.3 %collective-permute-start.4 = (bf16[4,64,8,96]{3,2,1,0:T(8,128)(2,1)S(1)}, bf16[4,64,8,96]{3,2,1,0:T(8,128)(2,1)}, u32[]{:S(2)}, u32[]{:S(2)}) collective-permute-start(bf16[4,64,8,96]{3,2,1,0:T(8,128)(2,1)S(1)} %get-tuple-element.20), channel_id=1, source_target_pairs={{1,0},{2,1},{3,2},{4,3},{5,4},{6,5},{7,6},{8,7},{9,8},{10,9},{11,1... | collective-permute-start | bytes 1179656 | tf_op jit(solution)/shard_map/ppermute | solution.py:20
  21.6 0.0 copy-done.1
  21.7 1.9 %fusion = (bf16[4,5,64,96]{3,2,1,0:T(8,128)(2,1)S(1)}, bf16[4,5,64,96]{3,2,1,0:T(8,128)(2,1)}) fusion(bf16[4,64,64,96]{3,2,1,0:T(8,128)(2,1)} %refs_4_.3), kind=kLoop, calls=%fused_computation.8 | loop fusion | bytes 983040 | tf_op jit(solution)/shard_map/slice | solution.py:339
  23.5 0.0 copy-start.7
  23.5 0.1 pad.9.clone
  23.6 0.6 add_convert_fusion.refs_0_
  24.2 0.0 copy-start.2
  24.2 0.0 copy-start.4
  24.2 0.0 copy-start.5
  24.2 0.0 collective-permute-done
  24.2 0.0 collective-permute-done.1
  24.3 1.4 %pad_maximum_fusion.refs_1_ = bf16[4,32,8,192]{3,2,1,0:T(8,128)(2,1)S(1)} fusion(bf16[4,32,2,192]{3,2,1,0:T(2,128)(2,1)} %collective-permute-done.1, bf16[4,32,2,192]{3,2,1,0:T(2,128)(2,1)S(1)} %collective-permute-done, bf16[8]{0:T(256)(128)(2,1)S(1)} %pad.9.clone), kind=kLoop, calls=%fused_computation | loop fusion | flops 1179648 | bytes 589840 | tf_op jit(solution)/shard_map/concatenate | solution.py:333
  25.7 3.5 %collective-permute-start.2 = (bf16[4,2,40,192]{3,2,1,0:T(8,128)(2,1)S(1)}, bf16[4,2,40,192]{3,2,1,0:T(8,128)(2,1)S(1)}, u32[]{:S(2)}, u32[]{:S(2)}) collective-permute-start(bf16[4,2,40,192]{3,2,1,0:T(8,128)(2,1)S(1)} %pad_maximum_fusion.3), channel_id=1, source_target_pairs={{0,16},{16,32},{32,48},{48,64},{64,80},{80,96},{96,112},{1,17},{17... | collective-permute-start | bytes 368648 | tf_op jit(solution)/shard_map/ppermute | solution.py:20
  29.3 4.5 %collective-permute-start.3 = (bf16[4,2,40,192]{3,2,1,0:T(8,128)(2,1)S(1)}, bf16[4,2,40,192]{3,2,1,0:T(8,128)(2,1)S(1)}, u32[]{:S(2)}, u32[]{:S(2)}) collective-permute-start(bf16[4,2,40,192]{3,2,1,0:T(8,128)(2,1)S(1)} %pad_maximum_fusion.4), channel_id=1, source_target_pairs={{16,0},{32,16},{48,32},{64,48},{80,64},{96,80},{112,96},{17,1},{33... | collective-permute-start | bytes 368648 | tf_op jit(solution)/shard_map/ppermute | solution.py:20
  33.7 0.0 collective-permute-done.4
  33.7 1.1 %constant_dynamic-update-slice_fusion.1 = bf16[4,64,16,96]{3,2,1,0:T(8,128)(2,1)S(1)} fusion(bf16[4,64,8,96]{3,2,1,0:T(8,128)(2,1)} %collective-permute-done.4), kind=kLoop, calls=%fused_computation.6 | loop fusion | bytes 917504
  34.9 0.0 collective-permute-done.5
  34.9 1.2 %constant_dynamic-update-slice_fusion.refs_5_ = bf16[4,64,16,96]{3,2,1,0:T(8,128)(2,1)S(1)} fusion(bf16[4,64,16,96]{3,2,1,0:T(8,128)(2,1)S(1)} %constant_dynamic-update-slice_fusion.1, bf16[4,64,8,96]{3,2,1,0:T(8,128)(2,1)} %collective-permute-done.5), kind=kLoop, calls=%fused_computation.5 | loop fusion | bytes 917504 | tf_op jit(solution)/shard_map/concatenate | solution.py:335
  36.1 0.0 copy-start.6
  36.1 0.0 copy-done.7
  36.1 0.2 pad_maximum_fusion.1
  36.3 0.0 collective-permute-done.2.refs_2_
  36.3 0.3 collective-permute-done.3.refs_3_
  36.5 3.4 %collective-permute-start.6 = (bf16[4,5,80,96]{3,2,1,0:T(8,128)(2,1)S(1)}, bf16[4,5,80,96]{3,2,1,0:T(8,128)(2,1)S(1)}, u32[]{:S(2)}, u32[]{:S(2)}) collective-permute-start(bf16[4,5,80,96]{3,2,1,0:T(8,128)(2,1)S(1)} %get-tuple-element.15), channel_id=1, source_target_pairs={{0,16},{16,32},{32,48},{48,64},{64,80},{80,96},{96,112},{1,17},{17... | collective-permute-start | bytes 921608 | tf_op jit(solution)/shard_map/ppermute | solution.py:20
  40.0 5.0 %collective-permute-start.7 = (bf16[4,5,80,96]{3,2,1,0:T(8,128)(2,1)S(1)}, bf16[4,5,80,96]{3,2,1,0:T(8,128)(2,1)S(1)}, u32[]{:S(2)}, u32[]{:S(2)}) collective-permute-start(bf16[4,5,80,96]{3,2,1,0:T(8,128)(2,1)S(1)} %get-tuple-element.16), channel_id=1, source_target_pairs={{16,0},{32,16},{48,32},{64,48},{80,64},{96,80},{112,96},{17,1},{33... | collective-permute-start | bytes 921608 | tf_op jit(solution)/shard_map/ppermute | solution.py:20
  45.0 0.0 copy-done.2
  45.0 0.0 copy-done.4
  45.0 0.0 copy-done.5
  45.0 14.2 %forward_block.1 = (f32[4,34,32,192]{3,2,1,0:T(8,128)S(1)}, f32[4,5,16,192]{3,2,1,0:T(8,128)S(1)}) custom-call(bf16[4,32,32,192]{3,2,1,0:T(8,128)(2,1)S(1)} %copy-done.1, bf16[4,32,8,192]{3,2,1,0:T(8,128)(2,1)S(1)} %pad_maximum_fusion.refs_1_, bf16[4,2,40,192]{3,2,1,0:T(8,128)(2,1)S(1)} %collective-permute-done.2.refs_2_, ...), custom_call_target="tpu_custom_call" | custom-call | flops 20000000000 | bytes 12000000 | tf_op jit(solution)/shard_map/forward_block/pallas_call | solution.py:352
  59.2 0.0 copy-done.6
  59.2 0.0 copy-start
  59.2 2.0 %copy-done = f32[4,34,32,192]{3,2,1,0:T(8,128)} copy-done((f32[4,34,32,192]{3,2,1,0:T(8,128)}, f32[4,34,32,192]{3,2,1,0:T(8,128)S(1)}, u32[]{:S(2)}) %copy-start) | copy-done | bytes 3342360
  61.3 0.0 copy-start.3
  61.3 0.7 copy-done.3
  62.0 0.0 collective-permute-done.6.refs_6_
  62.0 0.0 copy-start.8
  62.0 0.0 collective-permute-done.7.refs_7_
  62.0 0.0 copy-start.9
  62.0 0.8 copy-done.9
  62.8 0.1 copy-done.8
  62.9 45.0 %backward_block.1 = bf16[4,32,32,192]{3,2,1,0:T(8,128)(2,1)} custom-call(s32[4]{0:T(128)} %add_convert_fusion.refs_0_, bf16[4,32,32,192]{3,2,1,0:T(8,128)(2,1)} %refs_1_.1, f32[4,34,32,192]{3,2,1,0:T(8,128)} %copy-done, f32[4,5,16,192]{3,2,1,0:T(8,128)} %copy-done.3, bf16[4,64,64,96]{3,2,1,0:T(8,128)(2,1)} %refs_4_.3, bf16[4,64,16,96]{3,2,1,0:T(8,128)(2,1)} %copy-done.6, ...), custom_call_target="tpu_custom_call" | custom-call | tf_op jit(solution)/shard_map/backward_block/pallas_call | solution.py:367
  (6 shorter events, 0.1 us)
Async XLA Ops:
  0.0 21.6 %copy-start.1 = (bf16[4,32,32,192]{3,2,1,0:T(8,128)(2,1)S(1)}, bf16[4,32,32,192]{3,2,1,0:T(8,128)(2,1)}, u32[]{:S(2)}) copy-start(bf16[4,32,32,192]{3,2,1,0:T(8,128)(2,1)} %refs_1_.1) | copy-start | bytes 4718596
  2.2 22.0 %collective-permute-start = (bf16[4,32,2,192]{3,2,1,0:T(2,128)(2,1)}, bf16[4,32,2,192]{3,2,1,0:T(2,128)(2,1)S(1)}, u32[]{:S(2)}, u32[]{:S(2)}) collective-permute-start(bf16[4,32,2,192]{3,2,1,0:T(2,128)(2,1)} %get-tuple-element.23), channel_id=1, source_target_pairs={{1,0},{2,1},{3,2},{4,3},{5,4},{6,5},{7,6},{8,7},{9,8},{10,9},{11,1... | collective-permute-start | bytes 294920 | tf_op jit(solution)/shard_map/ppermute | solution.py:20
  8.4 15.8 %collective-permute-start.1 = (bf16[4,32,2,192]{3,2,1,0:T(2,128)(2,1)S(1)}, bf16[4,32,2,192]{3,2,1,0:T(2,128)(2,1)}, u32[]{:S(2)}, u32[]{:S(2)}) collective-permute-start(bf16[4,32,2,192]{3,2,1,0:T(2,128)(2,1)S(1)} %get-tuple-element.24), channel_id=1, source_target_pairs={{0,1},{1,2},{2,3},{3,4},{4,5},{5,6},{6,7},{7,8},{8,9},{9,10},{10,1... | collective-permute-start | bytes 294920 | tf_op jit(solution)/shard_map/ppermute | solution.py:20
  12.4 22.4 %collective-permute-start.5 = (bf16[4,64,8,96]{3,2,1,0:T(8,128)(2,1)}, bf16[4,64,8,96]{3,2,1,0:T(8,128)(2,1)}, u32[]{:S(2)}, u32[]{:S(2)}) collective-permute-start(bf16[4,64,8,96]{3,2,1,0:T(8,128)(2,1)} %get-tuple-element.19), channel_id=1, source_target_pairs={{0,1},{1,2},{2,3},{3,4},{4,5},{5,6},{6,7},{7,8},{8,9},{9,10},{10,1... | collective-permute-start | bytes 1179656 | tf_op jit(solution)/shard_map/ppermute | solution.py:20
  14.4 19.4 %collective-permute-start.4 = (bf16[4,64,8,96]{3,2,1,0:T(8,128)(2,1)S(1)}, bf16[4,64,8,96]{3,2,1,0:T(8,128)(2,1)}, u32[]{:S(2)}, u32[]{:S(2)}) collective-permute-start(bf16[4,64,8,96]{3,2,1,0:T(8,128)(2,1)S(1)} %get-tuple-element.20), channel_id=1, source_target_pairs={{1,0},{2,1},{3,2},{4,3},{5,4},{6,5},{7,6},{8,7},{9,8},{10,9},{11,1... | collective-permute-start | bytes 1179656 | tf_op jit(solution)/shard_map/ppermute | solution.py:20
  23.5 12.6 %copy-start.7 = (bf16[4,5,64,96]{3,2,1,0:T(8,128)(2,1)S(1)}, bf16[4,5,64,96]{3,2,1,0:T(8,128)(2,1)}, u32[]{:S(2)}) copy-start(bf16[4,5,64,96]{3,2,1,0:T(8,128)(2,1)} %get-tuple-element.18) | copy-start | bytes 737284
  24.2 20.7 %copy-start.2 = (bf16[3,3,3,192,192]{4,3,2,1,0:T(8,128)(2,1)S(1)}, bf16[3,3,3,192,192]{4,3,2,1,0:T(8,128)(2,1)}, u32[]{:S(2)}) copy-start(bf16[3,3,3,192,192]{4,3,2,1,0:T(8,128)(2,1)} %refs_8_.1) | copy-start | bytes 5971972
  24.2 20.7 %copy-start.4 = (f32[192]{0:T(256)S(1)}, f32[192]{0:T(256)}, u32[]{:S(2)}) copy-start(f32[192]{0:T(256)} %param.11) | copy-start | bytes 2308
  24.2 20.8 %copy-start.5 = (f32[192]{0:T(256)S(1)}, f32[192]{0:T(256)}, u32[]{:S(2)}) copy-start(f32[192]{0:T(256)} %param.10) | copy-start | bytes 2308
  25.7 10.5 %collective-permute-start.2 = (bf16[4,2,40,192]{3,2,1,0:T(8,128)(2,1)S(1)}, bf16[4,2,40,192]{3,2,1,0:T(8,128)(2,1)S(1)}, u32[]{:S(2)}, u32[]{:S(2)}) collective-permute-start(bf16[4,2,40,192]{3,2,1,0:T(8,128)(2,1)S(1)} %pad_maximum_fusion.3), channel_id=1, source_target_pairs={{0,16},{16,32},{32,48},{48,64},{64,80},{80,96},{96,112},{1,17},{17... | collective-permute-start | bytes 368648 | tf_op jit(solution)/shard_map/ppermute | solution.py:20
  29.3 7.3 %collective-permute-start.3 = (bf16[4,2,40,192]{3,2,1,0:T(8,128)(2,1)S(1)}, bf16[4,2,40,192]{3,2,1,0:T(8,128)(2,1)S(1)}, u32[]{:S(2)}, u32[]{:S(2)}) collective-permute-start(bf16[4,2,40,192]{3,2,1,0:T(8,128)(2,1)S(1)} %pad_maximum_fusion.4), channel_id=1, source_target_pairs={{16,0},{32,16},{48,32},{64,48},{80,64},{96,80},{112,96},{17,1},{33... | collective-permute-start | bytes 368648 | tf_op jit(solution)/shard_map/ppermute | solution.py:20
  36.1 23.2 %copy-start.6 = (bf16[4,64,16,96]{3,2,1,0:T(8,128)(2,1)}, bf16[4,64,16,96]{3,2,1,0:T(8,128)(2,1)S(1)}, u32[]{:S(2)}) copy-start(bf16[4,64,16,96]{3,2,1,0:T(8,128)(2,1)S(1)} %constant_dynamic-update-slice_fusion.refs_5_) | copy-start | bytes 2359300
  36.5 25.5 %collective-permute-start.6 = (bf16[4,5,80,96]{3,2,1,0:T(8,128)(2,1)S(1)}, bf16[4,5,80,96]{3,2,1,0:T(8,128)(2,1)S(1)}, u32[]{:S(2)}, u32[]{:S(2)}) collective-permute-start(bf16[4,5,80,96]{3,2,1,0:T(8,128)(2,1)S(1)} %get-tuple-element.15), channel_id=1, source_target_pairs={{0,16},{16,32},{32,48},{48,64},{64,80},{80,96},{96,112},{1,17},{17... | collective-permute-start | bytes 921608 | tf_op jit(solution)/shard_map/ppermute | solution.py:20
  40.0 22.1 %collective-permute-start.7 = (bf16[4,5,80,96]{3,2,1,0:T(8,128)(2,1)S(1)}, bf16[4,5,80,96]{3,2,1,0:T(8,128)(2,1)S(1)}, u32[]{:S(2)}, u32[]{:S(2)}) collective-permute-start(bf16[4,5,80,96]{3,2,1,0:T(8,128)(2,1)S(1)} %get-tuple-element.16), channel_id=1, source_target_pairs={{16,0},{32,16},{48,32},{64,48},{80,64},{96,80},{112,96},{17,1},{33... | collective-permute-start | bytes 921608 | tf_op jit(solution)/shard_map/ppermute | solution.py:20
  59.2 2.1 %copy-start = (f32[4,34,32,192]{3,2,1,0:T(8,128)}, f32[4,34,32,192]{3,2,1,0:T(8,128)S(1)}, u32[]{:S(2)}) copy-start(f32[4,34,32,192]{3,2,1,0:T(8,128)S(1)} %get-tuple-element.13.refs_2_) | copy-start | bytes 10027012
  61.3 0.7 copy-start.3
  62.0 0.9 copy-start.8
  62.0 0.8 copy-start.9

commit v3 on v2

--- a/solution.py
+++ b/solution.py
@@ -116,9 +116,14 @@
 
 
 def forward(*refs):
-    feat, feat_side, before, after, w1, bias, gain1, pre, pre_strip = refs[:9]
+    feat_in, feat_side, before, after, w1_in, bias, gain1, pre_out, pre_strip = refs[:9]
     act, act_strip = refs[9:13], refs[13:17]
-    act_tail, act_rows = refs[17:]
+    act_tail, act_rows, pre, feat, w1, sem = refs[17:]
+    load_feat = [pltpu.make_async_copy(feat_in.at[t], feat.at[t], sem.at[4 + t]) for t in range(4)]
+    load_w1 = pltpu.make_async_copy(w1_in, w1, sem.at[8])
+    for copy in (load_feat[0], load_w1, *load_feat[1:]):
+        copy.start()
+    stores = [pltpu.make_async_copy(pre.at[t], pre_out.at[t], sem.at[t]) for t in range(4)]
     for n in range(4):
         act[n][35, :, 576:640] = jnp.zeros((32, 64), BF16)
     act_tail[:, 35 * 8 :, :] = jnp.zeros((5, 56, 128), F32)
@@ -152,23 +157,40 @@
         return run
 
     done = lambda t: lambda: build_strip(act_strip[t], act_tail)
+    load_feat[0].wait()
     run_steps(
         [
-            ([activate(0)], [done(0)]),
-            ([first_conv(0), activate(1)], [done(1)]),
-            ([first_conv(1), activate(2)], [done(2)]),
-            ([first_conv(2), activate(3)], [done(3)]),
-            ([first_conv(3)], []),
+            ([activate(0)], [done(0), load_w1.wait, load_feat[1].wait]),
+            ([first_conv(0), activate(1)], [done(1), stores[0].start, load_feat[2].wait]),
+            ([first_conv(1), activate(2)], [done(2), stores[1].start, load_feat[3].wait]),
+            ([first_conv(2), activate(3)], [done(3), stores[2].start]),
+            ([first_conv(3)], [stores[3].start]),
         ]
     )
+    for copy in stores:
+        copy.wait()
 
 
 def backward(*refs):
-    flags, feat, pre, pre_strip, cot, cot_side, before, after, w1, w2, wup, gain1, gain2, out = refs[:14]
+    flags, feat_in, pre_in, pre_strip, cot_in, cot_side, before, after, w1_in, w2_in = refs[:10]
+    wup, gain1, gain2, result = refs[10:14]
     act, grad, grad_strip, block = (refs[14 + 4 * n : 18 + 4 * n] for n in range(4))
     acc_up, acc, acc_strip, pooled = (refs[30 + 2 * n : 32 + 2 * n] for n in range(4))
     acc_last = (refs[38], acc_up[1], acc_up[0], refs[38])
-    grad_tail, grad_rows, edges, line, mask, strip_mask, w2t, w1t, wu = refs[39:]
+    grad_tail, grad_rows, edges, line, mask, strip_mask, w2t, w1t, wu = refs[39:48]
+    feat, pre, cot, w1, w2, out, sem = refs[48:]
+
+    def copies(src, dst, first):
+        return [pltpu.make_async_copy(src.at[t], dst.at[t], sem.at[first + t]) for t in range(4)]
+
+    load_cot, load_pre, store = copies(cot_in, cot, 0), copies(pre_in, pre, 4), copies(out, result, 8)
+    load_w2 = pltpu.make_async_copy(w2_in, w2, sem.at[12])
+    load_w1 = pltpu.make_async_copy(w1_in, w1, sem.at[13])
+    load_feat = pltpu.make_async_copy(feat_in, feat, sem.at[14])
+    for copy in (load_cot[3], load_w2, load_cot[2], load_cot[1], load_cot[0], load_pre[3], load_w1):
+        copy.start()
+    for copy in (load_pre[2], load_pre[1], load_feat, load_pre[0]):
+        copy.start()
 
     for n in range(4):
         act[n][35, :, 576:640] = jnp.zeros((32, 64), BF16)
@@ -183,8 +205,6 @@
     good = jnp.where(s < 8, flags[2], flags[3]) > 0
     good &= ((o > 0) | (flags[0] > 0)) & ((o < 33) | (flags[1] > 0))
     strip_mask[...] = jnp.where(good, 1.0, 0.0)
-    pack_adjoint(w2t, w2)
-    pack_adjoint(w1t, w1)
     for p in range(3):
         for q in range(3):
             tap = 128 * (3 * p + q)
@@ -309,38 +329,68 @@
 
     grad_done = lambda t: lambda: build_strip(grad_strip[t], grad_tail)
     second_done = lambda t: lambda: strip_grad(t)
+    pack2, pack1 = lambda: pack_adjoint(w2t, w2), lambda: pack_adjoint(w1t, w1)
+    load_cot[3].wait()
     run_steps(
         [
-            ([pool(3)], []),
-            ([up_conv(3), pool(2)], []),
-            ([up_conv(2), keep_block(3), pool(1)], [grad_done(3)]),
-            ([second(3), up_conv(1), keep_block(2), pool(0)], [grad_done(2), second_done(3)]),
-            ([second(2), up_conv(0), keep_block(1), pre_grad(3)], [grad_done(1), second_done(2)]),
-            ([last(3), second(1), keep_block(0), pre_grad(2)], [grad_done(0), second_done(1)]),
-            ([second(0), last(2), pre_grad(1), finish(3)], [second_done(0)]),
-            ([last(1), pre_grad(0), finish(2)], []),
-            ([last(0), finish(1)], []),
-            ([finish(0)], []),
+            ([pool(3)], [load_cot[2].wait]),
+            ([up_conv(3), pool(2)], [load_cot[1].wait]),
+            ([up_conv(2), keep_block(3), pool(1)], [grad_done(3), load_w2.wait, pack2, load_cot[0].wait]),
+            (
+                [second(3), up_conv(1), keep_block(2), pool(0)],
+                [grad_done(2), load_pre[3].wait, second_done(3)],
+            ),
+            (
+                [second(2), up_conv(0), keep_block(1), pre_grad(3)],
+                [grad_done(1), second_done(2), load_w1.wait, pack1, load_pre[2].wait],
+            ),
+            (
+                [last(3), second(1), keep_block(0), pre_grad(2)],
+                [grad_done(0), second_done(1), load_pre[1].wait, load_feat.wait],
+            ),
+            (
+                [second(0), last(2), pre_grad(1), finish(3)],
+                [second_done(0), load_pre[0].wait, store[3].start],
+            ),
+            ([last(1), pre_grad(0), finish(2)], [store[2].start]),
+            ([last(0), finish(1)], [store[1].start]),
+            ([finish(0)], [store[0].start]),
         ]
     )
+    for copy in store:
+        copy.wait()
+
+
+def halves(field, axis):
+    half = field.shape[-1] // 2
+    return jnp.concatenate([field[..., :half], field[..., half:]], axis=axis)
 
 
 def per_device(
     features, conv_first, bias_first, gain_first, conv_second, gain_second, up_weight, cotangent
 ):
-    left, right = shift_pair(features[:, :, 30:], features[:, :, :2], "wa")
-    gap = jnp.zeros(left.shape[:2] + (4, 192), BF16)
-    feat_side = jnp.concatenate([right, gap, left], axis=2)
-    cot_left, cot_right = shift_pair(cotangent[:, :, 56:], cotangent[:, :, :8], "wa")
-    cot_side = jnp.concatenate([cot_right, cot_left], axis=2)
+    def cols(lo_f, lo_c):
+        parts = [cotangent[:, :, lo_c : lo_c + 5], halves(features[:, :, lo_f : lo_f + 2], 1)]
+        return jnp.pad(jnp.concatenate(parts, axis=2), ((0, 0), (0, 0), (0, 1), (0, 0)))
+
+    left, right = shift_pair(cols(30, 59), cols(0, 0), "wa")
+
+    def ring(first, last, width):
+        gap = jnp.zeros(first.shape[:2] + (width - 2 * first.shape[2], first.shape[3]), BF16)
+        return jnp.concatenate([first, gap, last], axis=2)
+
+    cot_side = ring(right[:, :, :5], left[:, :, :5], 16)
+    whole = lambda side: jnp.concatenate([side[:, :32, 5:7], side[:, 32:, 5:7]], axis=3)
+    feat_side = ring(whole(right), whole(left), 8)
 
     def rows(field, side, lo, count):
         part = slice(lo, lo + count)
         return jnp.concatenate([field[:, part], side[:, part]], axis=2)
 
-    before, after = shift_pair(rows(features, feat_side, 30, 2), rows(features, feat_side, 0, 2), "ha")
+    up, down = rows(features, feat_side, 30, 2), rows(features, feat_side, 0, 2)
     cot_up, cot_down = rows(cotangent, cot_side, 59, 5), rows(cotangent, cot_side, 0, 5)
-    before, after, cot_up, cot_down = lax.optimization_barrier((before, after, cot_up, cot_down))
+    up, down, cot_up, cot_down = lax.optimization_barrier((up, down, cot_up, cot_down))
+    before, after = shift_pair(up, down, "ha")
     cot_before, cot_after = shift_pair(cot_up, cot_down, "ha")
 
     bias, gain1, gain2 = (x.reshape(1, 192) for x in (bias_first, gain_first, gain_second))
@@ -348,27 +398,34 @@
     flags = jnp.stack(
         [ha > 0, ha < lax.axis_size("ha") - 1, wa > 0, wa < lax.axis_size("wa") - 1]
     ).astype(jnp.int32)
-    vmem = pl.BlockSpec(memory_space=pltpu.VMEM)
+    vmem, own = pl.BlockSpec(memory_space=pltpu.VMEM), pl.BlockSpec(memory_space=pltpu.HBM)
     pre, pre_strip = pl.pallas_call(
         forward,
         out_shape=[
             jax.ShapeDtypeStruct((4, 34, 32, 192), F32),
             jax.ShapeDtypeStruct((4, DEEP, 16, 192), F32),
         ],
-        in_specs=[vmem] * 7,
-        out_specs=[vmem] * 2,
+        in_specs=[own] + [vmem] * 3 + [own] + [vmem] * 2,
+        out_specs=[own, vmem],
         scratch_shapes=[pltpu.VMEM((36, 32, 640), BF16)] * 4
         + [pltpu.VMEM((DEEP + 2, 16, 640), BF16)] * 4
-        + [pltpu.VMEM((5, 8 * (7 + 7 * DEEP), 128), F32), pltpu.VMEM((18, COLS, 192), F32)],
-        compiler_params=pltpu.CompilerParams(vmem_limit_bytes=28 * 1024 * 1024),
+        + [pltpu.VMEM((5, 8 * (7 + 7 * DEEP), 128), F32), pltpu.VMEM((18, COLS, 192), F32)]
+        + [
+            pltpu.VMEM((4, 34, 32, 192), F32),
+            pltpu.VMEM((4, 32, 32, 192), BF16),
+            pltpu.VMEM((3, 3, 3, 192, 192), BF16),
+            pltpu.SemaphoreType.DMA((9,)),
+        ],
+        compiler_params=pltpu.CompilerParams(vmem_limit_bytes=60 * 1024 * 1024),
         cost_estimate=pl.CostEstimate(flops=20_000_000_000, transcendentals=1_000_000, bytes_accessed=12_000_000),
         name="forward_block",
     )(features, feat_side, before, after, conv_first, bias, gain1)
     return pl.pallas_call(
         backward,
         out_shape=jax.ShapeDtypeStruct(features.shape, BF16),
-        in_specs=[pl.BlockSpec(memory_space=pltpu.SMEM)] + [vmem] * 12,
-        out_specs=vmem,
+        in_specs=[pl.BlockSpec(memory_space=pltpu.SMEM), own, own, vmem, own] + [vmem] * 3
+        + [own, own] + [vmem] * 3,
+        out_specs=own,
         scratch_shapes=[pltpu.VMEM((36, 32, 640), BF16)] * 8
         + [pltpu.VMEM((DEEP + 2, 16, 640), BF16)] * 4
         + [pltpu.VMEM((36, 32, 192), F32)] * 4
@@ -387,6 +444,13 @@
             pltpu.VMEM((3, 192, 1792), BF16),
             pltpu.VMEM((3, 192, 1792), BF16),
             pltpu.VMEM((192, 1152), BF16),
+            pltpu.VMEM((4, 32, 32, 192), BF16),
+            pltpu.VMEM((4, 34, 32, 192), F32),
+            pltpu.VMEM((4, 64, 64, 96), BF16),
+            pltpu.VMEM((3, 3, 3, 192, 192), BF16),
+            pltpu.VMEM((3, 3, 3, 192, 192), BF16),
+            pltpu.VMEM((4, 32, 32, 192), BF16),
+            pltpu.SemaphoreType.DMA((15,)),
         ],
         compiler_params=pltpu.CompilerParams(vmem_limit_bytes=58 * 1024 * 1024),
         name="backward_block",

time: 108 us -> 99.4 us (0.920)
  starting transfers between devices: 33.7 us -> 25.2 us
  local copies, waits for them, and re-layouts: 12.3 us -> 7.29 us
  waiting for transfers between devices: 0.28 us -> 4.25 us
    ppermute x4 -> x3, starting transfers between devices: 23 us -> 17.9 us  [shift_pair(): lax.ppermute(value_down, axis, down)]
    pallas_call x1, Pallas kernels: 45 us -> 40.6 us  [per_device(): pl.pallas_call(backward, out_shape=jax.ShapeDtypeStruct(features.shape, B...]
    pallas_call x1, Pallas kernels: 14.2 us -> 18.2 us  [per_device(): pl.pallas_call(forward, out_shape=[jax.ShapeDtypeStruct((4, 34, 32, 192),...]
    ppermute x4 -> x3, starting transfers between devices: 10.7 us -> 7.3 us  [shift_pair(): lax.ppermute(value_up, axis, up)]
    unnamed x21 -> x12, local copies, waits for them, and re-layouts: 4.82 us -> 1.62 us
    ppermute x4 -> x3, waiting for transfers between devices: 0.01 us -> 2.18 us  [shift_pair(): lax.ppermute(value_up, axis, up)]
    ppermute x4 -> x3, waiting for transfers between devices: 0.27 us -> 2.07 us  [shift_pair(): lax.ppermute(value_down, axis, down)]
    concatenate x2, local copies, waits for them, and re-layouts: 1.25 us -> 0.15 us  [ring(): return jnp.concatenate([first, gap, last], axis=2)]
  transfers between devices with their start and end apart: 8 -> 6, of which waited for: 1 -> 2; matrix products, arithmetic and copies ran while one was open for 8% -> 4% of each run, Pallas kernels for 13% -> 18%
where the time goes in v3:
time: 99.4 us; the launch traced here: 98.9 us
  Pallas kernels  58.9 us (59%)
  starting transfers between devices  25.2 us (25%)
  local copies, waits for them, and re-layouts  7.29 us (7%)
  waiting for transfers between devices  4.25 us (4%)
  other arithmetic  2.86 us (3%)
    pallas_call x1, Pallas kernels, per_device(): pl.pallas_call(backward, out_shape=jax.ShapeDtypeStruct(features.shape, B...  40.6 us
    pallas_call x1, Pallas kernels, per_device(): pl.pallas_call(forward, out_shape=[jax.ShapeDtypeStruct((4, 34, 32, 192),...  18.2 us
    ppermute x3, starting transfers between devices, shift_pair(): lax.ppermute(value_down, axis, down)  17.9 us
    ppermute x3, starting transfers between devices, shift_pair(): lax.ppermute(value_up, axis, up)  7.3 us
    ppermute x3, waiting for transfers between devices, shift_pair(): lax.ppermute(value_up, axis, up)  2.18 us
    slice x4, local copies, waits for them, and re-layouts, rows(): return jnp.concatenate([field[:, part], side[:, part]], axis=2)  2.13 us
    ppermute x3, waiting for transfers between devices, shift_pair(): lax.ppermute(value_down, axis, down)  2.07 us
  transfers between devices with their start and end apart: 6, of which 2 were waited for; matrix products, arithmetic and copies ran while one was open for 4% of the time, Pallas kernels for 18%

profile of v3, /device:TPU:6, one launch (start us, length us, event | category | flops | bytes accessed | tf_op | source)
XLA Modules:
  0.0 98.9 jit_solution(13800320071576058249)
XLA Ops:
  0.0 1.7 %fusion.13 = (bf16[4,32,2,96]{3,2,1,0:T(2,128)(2,1)S(1)}, bf16[4,32,2,96]{3,2,1,0:T(2,128)(2,1)S(1)}, bf16[4,32,2,96]{3,2,1,0:T(2,128)(2,1)S(1)}, bf16[4,32,2,96]{3,2,1,0:T(2,128)(2,1)S(1)}) fusion(bf16[4,32,32,192]{3,2,1,0:T(8,128)(2,1)} %refs_1_.1), kind=kLoop, calls=%fused_computation.21 | loop fusion | bytes 393216 | tf_op jit(solution)/shard_map/slice | solution.py:366
  1.7 1.4 %fusion.11 = (bf16[4,64,5,96]{3,2,1,0:T(8,128)(2,1)S(1)}, bf16[4,64,5,96]{3,2,1,0:T(8,128)(2,1)S(1)}) fusion(bf16[4,64,64,96]{3,2,1,0:T(8,128)(2,1)} %refs_4_.3), kind=kLoop, calls=%fused_computation.19 | loop fusion | bytes 983040 | tf_op jit(solution)/shard_map/slice | solution.py:373
  3.1 0.4 fusion.8
  3.6 1.9 %collective-permute-start.1 = (bf16[4,64,8,96]{3,2,1,0:T(8,128)(2,1)S(1)}, bf16[4,64,8,96]{3,2,1,0:T(8,128)(2,1)S(1)}, u32[]{:S(2)}, u32[]{:S(2)}) collective-permute-start(bf16[4,64,8,96]{3,2,1,0:T(8,128)(2,1)S(1)} %fusion.8), channel_id=1, source_target_pairs={{0,1},{1,2},{2,3},{3,4},{4,5},{5,6},{6,7},{7,8},{8,9},{9,10},{10,1... | collective-permute-start | bytes 1179656 | tf_op jit(solution)/shard_map/ppermute | solution.py:20
  5.5 0.4 fusion.6
  5.9 7.3 %collective-permute-start = (bf16[4,64,8,96]{3,2,1,0:T(8,128)(2,1)S(1)}, bf16[4,64,8,96]{3,2,1,0:T(8,128)(2,1)S(1)}, u32[]{:S(2)}, u32[]{:S(2)}) collective-permute-start(bf16[4,64,8,96]{3,2,1,0:T(8,128)(2,1)S(1)} %fusion.6), channel_id=1, source_target_pairs={{1,0},{2,1},{3,2},{4,3},{5,4},{6,5},{7,6},{8,7},{9,8},{10,9},{11,1... | collective-permute-start | bytes 1179656 | tf_op jit(solution)/shard_map/ppermute | solution.py:20
  13.2 0.1 pad.22.clone
  13.3 0.1 pad.14.clone
  13.4 1.1 %fusion.10 = (bf16[4,5,64,96]{3,2,1,0:T(8,128)(2,1)S(1)}, bf16[4,5,64,96]{3,2,1,0:T(8,128)(2,1)S(1)}) fusion(bf16[4,64,64,96]{3,2,1,0:T(8,128)(2,1)} %refs_4_.3), kind=kLoop, calls=%fused_computation.18 | loop fusion | bytes 983040 | tf_op jit(solution)/shard_map/slice | solution.py:388
  14.5 1.0 %fusion.12 = (bf16[4,2,32,192]{3,2,1,0:T(8,128)(2,1)S(1)}, bf16[4,2,32,192]{3,2,1,0:T(8,128)(2,1)S(1)}) fusion(bf16[4,32,32,192]{3,2,1,0:T(8,128)(2,1)} %refs_1_.1), kind=kLoop, calls=%fused_computation.20 | loop fusion | bytes 393216 | tf_op jit(solution)/shard_map/slice | solution.py:388
  15.5 2.2 %collective-permute-done.1 = bf16[4,64,8,96]{3,2,1,0:T(8,128)(2,1)S(1)} collective-permute-done((bf16[4,64,8,96]{3,2,1,0:T(8,128)(2,1)S(1)}, bf16[4,64,8,96]{3,2,1,0:T(8,128)(2,1)S(1)}, u32[]{:S(2)}, u32[]{:S(2)}) %collective-permute-start.1) | collective-permute-done | bytes 393248 | tf_op jit(solution)/shard_map/ppermute | solution.py:20
  17.7 0.1 fusion.17
  17.8 2.1 %collective-permute-done = bf16[4,64,8,96]{3,2,1,0:T(8,128)(2,1)S(1)} collective-permute-done((bf16[4,64,8,96]{3,2,1,0:T(8,128)(2,1)S(1)}, bf16[4,64,8,96]{3,2,1,0:T(8,128)(2,1)S(1)}, u32[]{:S(2)}, u32[]{:S(2)}) %collective-permute-start) | collective-permute-done | bytes 393248 | tf_op jit(solution)/shard_map/ppermute | solution.py:20
  19.9 0.1 fusion.16
  20.0 0.7 maximum_maximum_fusion.refs_1_
  20.7 0.0 copy-start.1
  20.7 0.5 pad_maximum_fusion.refs_5_
  21.2 0.0 copy-start
  21.2 0.1 pad_maximum_fusion.3
  21.3 0.2 pad_maximum_fusion.1
  21.5 0.0 copy-done.1
  21.5 3.5 %collective-permute-start.2 = (bf16[4,2,40,192]{3,2,1,0:T(8,128)(2,1)S(1)}, bf16[4,2,40,192]{3,2,1,0:T(8,128)(2,1)S(1)}, u32[]{:S(2)}, u32[]{:S(2)}) collective-permute-start(bf16[4,2,40,192]{3,2,1,0:T(8,128)(2,1)S(1)} %get-tuple-element.11), channel_id=1, source_target_pairs={{0,16},{16,32},{32,48},{48,64},{64,80},{80,96},{96,112},{1,17},{17... | collective-permute-start | bytes 368648 | tf_op jit(solution)/shard_map/ppermute | solution.py:20
  25.0 4.5 %collective-permute-start.3 = (bf16[4,2,40,192]{3,2,1,0:T(8,128)(2,1)S(1)}, bf16[4,2,40,192]{3,2,1,0:T(8,128)(2,1)S(1)}, u32[]{:S(2)}, u32[]{:S(2)}) collective-permute-start(bf16[4,2,40,192]{3,2,1,0:T(8,128)(2,1)S(1)} %get-tuple-element.12), channel_id=1, source_target_pairs={{16,0},{32,16},{48,32},{64,48},{80,64},{96,80},{112,96},{17,1},{33... | collective-permute-start | bytes 368648 | tf_op jit(solution)/shard_map/ppermute | solution.py:20
  29.5 0.6 add_convert_fusion.refs_0_
  30.1 1.9 %collective-permute-start.4 = (bf16[4,5,80,96]{3,2,1,0:T(8,128)(2,1)S(1)}, bf16[4,5,80,96]{3,2,1,0:T(8,128)(2,1)S(1)}, u32[]{:S(2)}, u32[]{:S(2)}) collective-permute-start(bf16[4,5,80,96]{3,2,1,0:T(8,128)(2,1)S(1)} %get-tuple-element.15), channel_id=1, source_target_pairs={{0,16},{16,32},{32,48},{48,64},{64,80},{80,96},{96,112},{1,17},{17... | collective-permute-start | bytes 921608 | tf_op jit(solution)/shard_map/ppermute | solution.py:20
  32.0 6.2 %collective-permute-start.5 = (bf16[4,5,80,96]{3,2,1,0:T(8,128)(2,1)S(1)}, bf16[4,5,80,96]{3,2,1,0:T(8,128)(2,1)S(1)}, u32[]{:S(2)}, u32[]{:S(2)}) collective-permute-start(bf16[4,5,80,96]{3,2,1,0:T(8,128)(2,1)S(1)} %get-tuple-element.16), channel_id=1, source_target_pairs={{16,0},{32,16},{48,32},{64,48},{80,64},{96,80},{112,96},{17,1},{33... | collective-permute-start | bytes 921608 | tf_op jit(solution)/shard_map/ppermute | solution.py:20
  38.2 0.0 collective-permute-done.2.refs_2_
  38.2 0.0 copy-start.4
  38.2 0.0 collective-permute-done.3.refs_3_
  38.2 0.0 copy-start.5
  38.2 0.7 copy-done.4
  38.9 0.0 copy-done.5
  39.0 18.2 %forward_block.1 = (f32[4,34,32,192]{3,2,1,0:T(8,128)}, f32[4,5,16,192]{3,2,1,0:T(8,128)}) custom-call(bf16[4,32,32,192]{3,2,1,0:T(8,128)(2,1)} %refs_1_.1, bf16[4,32,8,192]{3,2,1,0:T(8,128)(2,1)} %copy-done.1, bf16[4,2,40,192]{3,2,1,0:T(8,128)(2,1)} %copy-done.4, bf16[4,2,40,192]{3,2,1,0:T(8,128)(2,1)} %copy-done.5, bf16[3,3,3,192,192]{4,3,2,1,0:T(8,128)(2,1)} %refs_8_.1, ...), custom_call_target="tpu_custom_call" | custom-call | flops 20000000000 | bytes 12000000 | tf_op jit(solution)/shard_map/forward_block/pallas_call | solution.py:402
  57.2 0.0 copy-done
  57.2 0.0 collective-permute-done.4.refs_6_
  57.2 0.0 copy-start.2
  57.2 0.0 collective-permute-done.5.refs_7_
  57.2 0.0 copy-start.3
  57.3 0.7 copy-done.2
  58.0 0.1 copy-done.3
  58.1 40.6 %backward_block.1 = bf16[4,32,32,192]{3,2,1,0:T(8,128)(2,1)} custom-call(s32[4]{0:T(128)} %add_convert_fusion.refs_0_, bf16[4,32,32,192]{3,2,1,0:T(8,128)(2,1)} %refs_1_.1, f32[4,34,32,192]{3,2,1,0:T(8,128)} %get-tuple-element.13.refs_2_, f32[4,5,16,192]{3,2,1,0:T(8,128)} %get-tuple-element.14.refs_3_, bf16[4,64,64,96]{3,2,1,0:T(8,128)(2,1)} %refs_4_.3, ...), custom_call_target="tpu_custom_call" | custom-call | tf_op jit(solution)/shard_map/backward_block/pallas_call | solution.py:423
  (4 shorter events, 0.0 us)
Async XLA Ops:
  3.6 14.1 %collective-permute-start.1 = (bf16[4,64,8,96]{3,2,1,0:T(8,128)(2,1)S(1)}, bf16[4,64,8,96]{3,2,1,0:T(8,128)(2,1)S(1)}, u32[]{:S(2)}, u32[]{:S(2)}) collective-permute-start(bf16[4,64,8,96]{3,2,1,0:T(8,128)(2,1)S(1)} %fusion.8), channel_id=1, source_target_pairs={{0,1},{1,2},{2,3},{3,4},{4,5},{5,6},{6,7},{7,8},{8,9},{9,10},{10,1... | collective-permute-start | bytes 1179656 | tf_op jit(solution)/shard_map/ppermute | solution.py:20
  5.9 13.9 %collective-permute-start = (bf16[4,64,8,96]{3,2,1,0:T(8,128)(2,1)S(1)}, bf16[4,64,8,96]{3,2,1,0:T(8,128)(2,1)S(1)}, u32[]{:S(2)}, u32[]{:S(2)}) collective-permute-start(bf16[4,64,8,96]{3,2,1,0:T(8,128)(2,1)S(1)} %fusion.6), channel_id=1, source_target_pairs={{1,0},{2,1},{3,2},{4,3},{5,4},{6,5},{7,6},{8,7},{9,8},{10,9},{11,1... | collective-permute-start | bytes 1179656 | tf_op jit(solution)/shard_map/ppermute | solution.py:20
  20.7 0.8 copy-start.1
  21.2 36.0 %copy-start = (bf16[4,64,16,96]{3,2,1,0:T(8,128)(2,1)}, bf16[4,64,16,96]{3,2,1,0:T(8,128)(2,1)S(1)}, u32[]{:S(2)}) copy-start(bf16[4,64,16,96]{3,2,1,0:T(8,128)(2,1)S(1)} %pad_maximum_fusion.refs_5_) | copy-start | bytes 2359300
  21.5 16.7 %collective-permute-start.2 = (bf16[4,2,40,192]{3,2,1,0:T(8,128)(2,1)S(1)}, bf16[4,2,40,192]{3,2,1,0:T(8,128)(2,1)S(1)}, u32[]{:S(2)}, u32[]{:S(2)}) collective-permute-start(bf16[4,2,40,192]{3,2,1,0:T(8,128)(2,1)S(1)} %get-tuple-element.11), channel_id=1, source_target_pairs={{0,16},{16,32},{32,48},{48,64},{64,80},{80,96},{96,112},{1,17},{17... | collective-permute-start | bytes 368648 | tf_op jit(solution)/shard_map/ppermute | solution.py:20
  25.0 13.3 %collective-permute-start.3 = (bf16[4,2,40,192]{3,2,1,0:T(8,128)(2,1)S(1)}, bf16[4,2,40,192]{3,2,1,0:T(8,128)(2,1)S(1)}, u32[]{:S(2)}, u32[]{:S(2)}) collective-permute-start(bf16[4,2,40,192]{3,2,1,0:T(8,128)(2,1)S(1)} %get-tuple-element.12), channel_id=1, source_target_pairs={{16,0},{32,16},{48,32},{64,48},{80,64},{96,80},{112,96},{17,1},{33... | collective-permute-start | bytes 368648 | tf_op jit(solution)/shard_map/ppermute | solution.py:20
  30.1 27.1 %collective-permute-start.4 = (bf16[4,5,80,96]{3,2,1,0:T(8,128)(2,1)S(1)}, bf16[4,5,80,96]{3,2,1,0:T(8,128)(2,1)S(1)}, u32[]{:S(2)}, u32[]{:S(2)}) collective-permute-start(bf16[4,5,80,96]{3,2,1,0:T(8,128)(2,1)S(1)} %get-tuple-element.15), channel_id=1, source_target_pairs={{0,16},{16,32},{32,48},{48,64},{64,80},{80,96},{96,112},{1,17},{17... | collective-permute-start | bytes 921608 | tf_op jit(solution)/shard_map/ppermute | solution.py:20
  32.0 25.2 %collective-permute-start.5 = (bf16[4,5,80,96]{3,2,1,0:T(8,128)(2,1)S(1)}, bf16[4,5,80,96]{3,2,1,0:T(8,128)(2,1)S(1)}, u32[]{:S(2)}, u32[]{:S(2)}) collective-permute-start(bf16[4,5,80,96]{3,2,1,0:T(8,128)(2,1)S(1)} %get-tuple-element.16), channel_id=1, source_target_pairs={{16,0},{32,16},{48,32},{64,48},{80,64},{96,80},{112,96},{17,1},{33... | collective-permute-start | bytes 921608 | tf_op jit(solution)/shard_map/ppermute | solution.py:20
  38.2 0.7 copy-start.4
  38.2 0.7 copy-start.5
  57.2 0.8 copy-start.2
  57.2 0.9 copy-start.3

commit v4 on v3

--- a/solution.py
+++ b/solution.py
@@ -80,6 +80,16 @@
             base += LANES[p]
 
 
+def pack_weights(w1, w2, wup, w1t, w2t, wu):
+    pack_adjoint(w2t, w2)
+    pack_adjoint(w1t, w1)
+    for p in range(3):
+        for q in range(3):
+            tap = 128 * (3 * p + q)
+            wu[:, tap : tap + 96] = wup[2 - p, 2 - q]
+            wu[:, tap + 96 : tap + 128] = jnp.zeros((192, 32), BF16)
+
+
 def operand(refs, strips, frames, row, rows, strip_row):
     parts = []
     for s in frames:
@@ -116,13 +126,9 @@
 
 
 def forward(*refs):
-    feat_in, feat_side, before, after, w1_in, bias, gain1, pre_out, pre_strip = refs[:9]
+    feat, feat_side, before, after, w1, bias, gain1, pre_out, pre_strip = refs[:9]
     act, act_strip = refs[9:13], refs[13:17]
-    act_tail, act_rows, pre, feat, w1, sem = refs[17:]
-    load_feat = [pltpu.make_async_copy(feat_in.at[t], feat.at[t], sem.at[4 + t]) for t in range(4)]
-    load_w1 = pltpu.make_async_copy(w1_in, w1, sem.at[8])
-    for copy in (load_feat[0], load_w1, *load_feat[1:]):
-        copy.start()
+    act_tail, act_rows, pre, sem = refs[17:]
     stores = [pltpu.make_async_copy(pre.at[t], pre_out.at[t], sem.at[t]) for t in range(4)]
     for n in range(4):
         act[n][35, :, 576:640] = jnp.zeros((32, 64), BF16)
@@ -157,12 +163,11 @@
         return run
 
     done = lambda t: lambda: build_strip(act_strip[t], act_tail)
-    load_feat[0].wait()
     run_steps(
         [
-            ([activate(0)], [done(0), load_w1.wait, load_feat[1].wait]),
-            ([first_conv(0), activate(1)], [done(1), stores[0].start, load_feat[2].wait]),
-            ([first_conv(1), activate(2)], [done(2), stores[1].start, load_feat[3].wait]),
+            ([activate(0)], [done(0)]),
+            ([first_conv(0), activate(1)], [done(1), stores[0].start]),
+            ([first_conv(1), activate(2)], [done(2), stores[1].start]),
             ([first_conv(2), activate(3)], [done(3), stores[2].start]),
             ([first_conv(3)], [stores[3].start]),
         ]
@@ -173,19 +178,19 @@
 
 def backward(*refs):
     flags, feat_in, pre_in, pre_strip, cot_in, cot_side, before, after, w1_in, w2_in = refs[:10]
-    wup, gain1, gain2, result = refs[10:14]
+    wu, gain1, gain2, result = refs[10:14]
     act, grad, grad_strip, block = (refs[14 + 4 * n : 18 + 4 * n] for n in range(4))
     acc_up, acc, acc_strip, pooled = (refs[30 + 2 * n : 32 + 2 * n] for n in range(4))
     acc_last = (refs[38], acc_up[1], acc_up[0], refs[38])
-    grad_tail, grad_rows, edges, line, mask, strip_mask, w2t, w1t, wu = refs[39:48]
-    feat, pre, cot, w1, w2, out, sem = refs[48:]
+    grad_tail, grad_rows, edges, line, mask, strip_mask = refs[39:45]
+    feat, pre, cot, w1t, w2t, out, sem = refs[45:]
 
     def copies(src, dst, first):
         return [pltpu.make_async_copy(src.at[t], dst.at[t], sem.at[first + t]) for t in range(4)]
 
     load_cot, load_pre, store = copies(cot_in, cot, 0), copies(pre_in, pre, 4), copies(out, result, 8)
-    load_w2 = pltpu.make_async_copy(w2_in, w2, sem.at[12])
-    load_w1 = pltpu.make_async_copy(w1_in, w1, sem.at[13])
+    load_w2 = pltpu.make_async_copy(w2_in, w2t, sem.at[12])
+    load_w1 = pltpu.make_async_copy(w1_in, w1t, sem.at[13])
     load_feat = pltpu.make_async_copy(feat_in, feat, sem.at[14])
     for copy in (load_cot[3], load_w2, load_cot[2], load_cot[1], load_cot[0], load_pre[3], load_w1):
         copy.start()
@@ -205,12 +210,6 @@
     good = jnp.where(s < 8, flags[2], flags[3]) > 0
     good &= ((o > 0) | (flags[0] > 0)) & ((o < 33) | (flags[1] > 0))
     strip_mask[...] = jnp.where(good, 1.0, 0.0)
-    for p in range(3):
-        for q in range(3):
-            tap = 128 * (3 * p + q)
-            wu[:, tap : tap + 96] = wup[2 - p, 2 - q]
-            wu[:, tap + 96 : tap + 128] = jnp.zeros((192, 32), BF16)
-
     def edge(value, b, r, first, last):
         if r in first:
             return value * jnp.where((b == 0) & (flags[0] == 0), 0.0, 1.0)
@@ -329,20 +328,19 @@
 
     grad_done = lambda t: lambda: build_strip(grad_strip[t], grad_tail)
     second_done = lambda t: lambda: strip_grad(t)
-    pack2, pack1 = lambda: pack_adjoint(w2t, w2), lambda: pack_adjoint(w1t, w1)
     load_cot[3].wait()
     run_steps(
         [
             ([pool(3)], [load_cot[2].wait]),
             ([up_conv(3), pool(2)], [load_cot[1].wait]),
-            ([up_conv(2), keep_block(3), pool(1)], [grad_done(3), load_w2.wait, pack2, load_cot[0].wait]),
+            ([up_conv(2), keep_block(3), pool(1)], [grad_done(3), load_w2.wait, load_cot[0].wait]),
             (
                 [second(3), up_conv(1), keep_block(2), pool(0)],
                 [grad_done(2), load_pre[3].wait, second_done(3)],
             ),
             (
                 [second(2), up_conv(0), keep_block(1), pre_grad(3)],
-                [grad_done(1), second_done(2), load_w1.wait, pack1, load_pre[2].wait],
+                [grad_done(1), second_done(2), load_w1.wait, load_pre[2].wait],
             ),
             (
                 [last(3), second(1), keep_block(0), pre_grad(2)],
@@ -373,7 +371,19 @@
         parts = [cotangent[:, :, lo_c : lo_c + 5], halves(features[:, :, lo_f : lo_f + 2], 1)]
         return jnp.pad(jnp.concatenate(parts, axis=2), ((0, 0), (0, 0), (0, 1), (0, 0)))
 
-    left, right = shift_pair(cols(30, 59), cols(0, 0), "wa")
+    last_cols, first_cols, w1, w2, wup = lax.optimization_barrier(
+        (cols(30, 59), cols(0, 0), conv_first, conv_second, up_weight)
+    )
+    left, right = shift_pair(last_cols, first_cols, "wa")
+    vmem, own = pl.BlockSpec(memory_space=pltpu.VMEM), pl.BlockSpec(memory_space=pltpu.HBM)
+    w1t, w2t, wu = pl.pallas_call(
+        pack_weights,
+        out_shape=[pltpu.HBM((3, 192, 1792), BF16), pltpu.HBM((3, 192, 1792), BF16), pltpu.HBM((192, 1152), BF16)],
+        in_specs=[vmem] * 3,
+        out_specs=[vmem] * 3,
+        compiler_params=pltpu.CompilerParams(vmem_limit_bytes=16 * 1024 * 1024),
+        name="pack_weights",
+    )(w1, w2, wup)
 
     def ring(first, last, width):
         gap = jnp.zeros(first.shape[:2] + (width - 2 * first.shape[2], first.shape[3]), BF16)
@@ -398,25 +408,22 @@
     flags = jnp.stack(
         [ha > 0, ha < lax.axis_size("ha") - 1, wa > 0, wa < lax.axis_size("wa") - 1]
     ).astype(jnp.int32)
-    vmem, own = pl.BlockSpec(memory_space=pltpu.VMEM), pl.BlockSpec(memory_space=pltpu.HBM)
     pre, pre_strip = pl.pallas_call(
         forward,
         out_shape=[
-            jax.ShapeDtypeStruct((4, 34, 32, 192), F32),
+            pltpu.HBM((4, 34, 32, 192), F32),
             jax.ShapeDtypeStruct((4, DEEP, 16, 192), F32),
         ],
-        in_specs=[own] + [vmem] * 3 + [own] + [vmem] * 2,
+        in_specs=[vmem] * 7,
         out_specs=[own, vmem],
         scratch_shapes=[pltpu.VMEM((36, 32, 640), BF16)] * 4
         + [pltpu.VMEM((DEEP + 2, 16, 640), BF16)] * 4
         + [pltpu.VMEM((5, 8 * (7 + 7 * DEEP), 128), F32), pltpu.VMEM((18, COLS, 192), F32)]
         + [
             pltpu.VMEM((4, 34, 32, 192), F32),
-            pltpu.VMEM((4, 32, 32, 192), BF16),
-            pltpu.VMEM((3, 3, 3, 192, 192), BF16),
-            pltpu.SemaphoreType.DMA((9,)),
+            pltpu.SemaphoreType.DMA((4,)),
         ],
-        compiler_params=pltpu.CompilerParams(vmem_limit_bytes=60 * 1024 * 1024),
+        compiler_params=pltpu.CompilerParams(vmem_limit_bytes=30 * 1024 * 1024),
         cost_estimate=pl.CostEstimate(flops=20_000_000_000, transcendentals=1_000_000, bytes_accessed=12_000_000),
         name="forward_block",
     )(features, feat_side, before, after, conv_first, bias, gain1)
@@ -441,22 +448,19 @@
             pltpu.VMEM((16, 2, 80, 128), F32),
             pltpu.VMEM((COLS, 192), F32),
             pltpu.VMEM((DEEP, 16, 192), F32),
-            pltpu.VMEM((3, 192, 1792), BF16),
-            pltpu.VMEM((3, 192, 1792), BF16),
-            pltpu.VMEM((192, 1152), BF16),
             pltpu.VMEM((4, 32, 32, 192), BF16),
             pltpu.VMEM((4, 34, 32, 192), F32),
             pltpu.VMEM((4, 64, 64, 96), BF16),
-            pltpu.VMEM((3, 3, 3, 192, 192), BF16),
-            pltpu.VMEM((3, 3, 3, 192, 192), BF16),
+            pltpu.VMEM((3, 192, 1792), BF16),
+            pltpu.VMEM((3, 192, 1792), BF16),
             pltpu.VMEM((4, 32, 32, 192), BF16),
             pltpu.SemaphoreType.DMA((15,)),
         ],
         compiler_params=pltpu.CompilerParams(vmem_limit_bytes=58 * 1024 * 1024),
         name="backward_block",
     )(
-        flags, features, pre, pre_strip, cotangent, cot_side, cot_before, cot_after, conv_first,
-        conv_second, up_weight, gain1, gain2,
+        flags, features, pre, pre_strip, cotangent, cot_side, cot_before, cot_after, w1t, w2t, wu,
+        gain1, gain2,
     )
 
 

time: 99.4 us -> 109 us (1.097)
  waiting for transfers between devices: 4.25 us -> 10.7 us
  local copies, waits for them, and re-layouts: 7.29 us -> 9.81 us
  other arithmetic: 2.86 us -> 5.2 us
    ppermute x3, waiting for transfers between devices: 2.18 us -> 7.3 us  [shift_pair(): lax.ppermute(value_up, axis, up)]
    unnamed x12 -> x26, local copies, waits for them, and re-layouts: 1.62 us -> 5.12 us
    concatenate x2 -> x4, other arithmetic: 0.22 us -> 2.53 us  [rows(): return jnp.concatenate([field[:, part], side[:, part]], axis=2)]
    ppermute x3, waiting for transfers between devices: 2.07 us -> 3.42 us  [shift_pair(): lax.ppermute(value_down, axis, down)]
    pallas_call x1 -> x2, Pallas kernels: 18.2 us -> 18.1 us  [the longest x1 15.2 us: per_device(): pl.pallas_call(forward, out_shape=[pltpu.HBM((4, 34, 32, 192), F32), jax....]
  transfers between devices with their start and end apart: 6 -> 6, of which waited for: 2 -> 2; matrix products, arithmetic and copies ran while one was open for 4% -> 2% of each run, Pallas kernels for 18% -> 17%
where the time goes in v4:
time: 109 us; the launch traced here: 108 us
  Pallas kernels  57.9 us (53%)
  starting transfers between devices  24.2 us (22%)
  waiting for transfers between devices  10.7 us (10%)
  local copies, waits for them, and re-layouts  9.81 us (9%)
  other arithmetic  5.2 us (5%)
    pallas_call x1, Pallas kernels, per_device(): pl.pallas_call(backward, out_shape=jax.ShapeDtypeStruct(features.shape, B...  39.8 us
    ppermute x3, starting transfers between devices, shift_pair(): lax.ppermute(value_down, axis, down)  16.9 us
    pallas_call x1, Pallas kernels, per_device(): pl.pallas_call(forward, out_shape=[pltpu.HBM((4, 34, 32, 192), F32), jax....  15.2 us
    ppermute x3, starting transfers between devices, shift_pair(): lax.ppermute(value_up, axis, up)  7.3 us
    ppermute x3, waiting for transfers between devices, shift_pair(): lax.ppermute(value_up, axis, up)  7.3 us
    unnamed x26, local copies, waits for them, and re-layouts  5.12 us
    ppermute x3, waiting for transfers between devices, shift_pair(): lax.ppermute(value_down, axis, down)  3.42 us
    pallas_call x1, Pallas kernels, per_device(): pl.pallas_call(pack_weights, out_shape=[pltpu.HBM((3, 192, 1792), BF16),...  2.83 us
  transfers between devices with their start and end apart: 6, of which 2 were waited for; matrix products, arithmetic and copies ran while one was open for 2% of the time, Pallas kernels for 17%

profile of v4, /device:TPU:6, one launch (start us, length us, event | category | flops | bytes accessed | tf_op | source)
XLA Modules:
  0.0 108.3 jit_solution(5630845184394300842)
XLA Ops:
  0.0 1.7 %fusion.13 = (bf16[4,32,2,96]{3,2,1,0:T(2,128)(2,1)S(1)}, bf16[4,32,2,96]{3,2,1,0:T(2,128)(2,1)S(1)}, bf16[4,32,2,96]{3,2,1,0:T(2,128)(2,1)S(1)}, bf16[4,32,2,96]{3,2,1,0:T(2,128)(2,1)S(1)}) fusion(bf16[4,32,32,192]{3,2,1,0:T(8,128)(2,1)} %refs_1_.1), kind=kLoop, calls=%fused_computation.21 | loop fusion | bytes 393216 | tf_op jit(solution)/shard_map/slice | solution.py:364
  1.7 1.4 %fusion.11 = (bf16[4,64,5,96]{3,2,1,0:T(8,128)(2,1)S(1)}, bf16[4,64,5,96]{3,2,1,0:T(8,128)(2,1)S(1)}) fusion(bf16[4,64,64,96]{3,2,1,0:T(8,128)(2,1)} %refs_4_.3), kind=kLoop, calls=%fused_computation.19 | loop fusion | bytes 983040 | tf_op jit(solution)/shard_map/slice | solution.py:371
  3.1 0.0 copy-start
  3.1 0.9 fusion.6
  4.0 6.2 %collective-permute-start = (bf16[4,64,8,96]{3,2,1,0:T(8,128)(2,1)S(1)}, bf16[4,64,8,96]{3,2,1,0:T(8,128)(2,1)S(1)}, u32[]{:S(2)}, u32[]{:S(2)}) collective-permute-start(bf16[4,64,8,96]{3,2,1,0:T(8,128)(2,1)S(1)} %get-tuple-element.19), channel_id=1, source_target_pairs={{1,0},{2,1},{3,2},{4,3},{5,4},{6,5},{7,6},{8,7},{9,8},{10,9},{11,1... | collective-permute-start | bytes 1179656 | tf_op jit(solution)/shard_map/ppermute | solution.py:20
  10.2 1.9 %collective-permute-start.1 = (bf16[4,64,8,96]{3,2,1,0:T(8,128)(2,1)S(1)}, bf16[4,64,8,96]{3,2,1,0:T(8,128)(2,1)S(1)}, u32[]{:S(2)}, u32[]{:S(2)}) collective-permute-start(bf16[4,64,8,96]{3,2,1,0:T(8,128)(2,1)S(1)} %get-tuple-element.20), channel_id=1, source_target_pairs={{0,1},{1,2},{2,3},{3,4},{4,5},{5,6},{6,7},{7,8},{8,9},{9,10},{10,1... | collective-permute-start | bytes 1179656 | tf_op jit(solution)/shard_map/ppermute | solution.py:20
  12.2 0.1 pad.14.clone
  12.3 0.1 pad.22.clone
  12.3 1.1 %fusion.10 = (bf16[4,5,64,96]{3,2,1,0:T(8,128)(2,1)S(1)}, bf16[4,5,64,96]{3,2,1,0:T(8,128)(2,1)S(1)}) fusion(bf16[4,64,64,96]{3,2,1,0:T(8,128)(2,1)} %refs_4_.3), kind=kLoop, calls=%fused_computation.18 | loop fusion | bytes 983040 | tf_op jit(solution)/shard_map/slice | solution.py:398
  13.5 0.0 copy-done
  13.5 3.4 %collective-permute-done = bf16[4,64,8,96]{3,2,1,0:T(8,128)(2,1)S(1)} collective-permute-done((bf16[4,64,8,96]{3,2,1,0:T(8,128)(2,1)S(1)}, bf16[4,64,8,96]{3,2,1,0:T(8,128)(2,1)S(1)}, u32[]{:S(2)}, u32[]{:S(2)}) %collective-permute-start) | collective-permute-done | bytes 393248 | tf_op jit(solution)/shard_map/ppermute | solution.py:20
  16.9 0.1 fusion.16
  17.1 7.3 %collective-permute-done.1 = bf16[4,64,8,96]{3,2,1,0:T(8,128)(2,1)S(1)} collective-permute-done((bf16[4,64,8,96]{3,2,1,0:T(8,128)(2,1)S(1)}, bf16[4,64,8,96]{3,2,1,0:T(8,128)(2,1)S(1)}, u32[]{:S(2)}, u32[]{:S(2)}) %collective-permute-start.1) | collective-permute-done | bytes 393248 | tf_op jit(solution)/shard_map/ppermute | solution.py:20
  24.4 0.1 fusion.17
  24.5 0.7 maximum_maximum_fusion.refs_1_
  25.2 0.0 copy-start.4
  25.2 0.5 pad_maximum_fusion.refs_5_
  25.7 0.0 copy-start.8
  25.7 0.8 pad_maximum_fusion.3
  26.6 0.9 pad_maximum_fusion.2
  27.4 0.8 pad_maximum_fusion.1
  28.2 0.0 copy-done.8
  28.2 3.5 %collective-permute-start.2 = (bf16[4,2,40,192]{3,2,1,0:T(8,128)(2,1)}, bf16[4,2,40,192]{3,2,1,0:T(8,128)(2,1)S(1)}, u32[]{:S(2)}, u32[]{:S(2)}) collective-permute-start(bf16[4,2,40,192]{3,2,1,0:T(8,128)(2,1)} %pad_maximum_fusion.3), channel_id=1, source_target_pairs={{0,16},{16,32},{32,48},{48,64},{64,80},{80,96},{96,112},{1,17},{17... | collective-permute-start | bytes 368648 | tf_op jit(solution)/shard_map/ppermute | solution.py:20
  31.7 4.5 %collective-permute-start.3 = (bf16[4,2,40,192]{3,2,1,0:T(8,128)(2,1)S(1)}, bf16[4,2,40,192]{3,2,1,0:T(8,128)(2,1)S(1)}, u32[]{:S(2)}, u32[]{:S(2)}) collective-permute-start(bf16[4,2,40,192]{3,2,1,0:T(8,128)(2,1)S(1)} %pad_maximum_fusion.4), channel_id=1, source_target_pairs={{16,0},{32,16},{48,32},{64,48},{80,64},{96,80},{112,96},{17,1},{33... | collective-permute-start | bytes 368648 | tf_op jit(solution)/shard_map/ppermute | solution.py:20
  36.2 0.0 copy-done.4
  36.2 0.0 copy-start.1
  36.2 1.7 %copy-done.1 = bf16[3,3,3,192,192]{4,3,2,1,0:T(8,128)(2,1)S(1)} copy-done((bf16[3,3,3,192,192]{4,3,2,1,0:T(8,128)(2,1)S(1)}, bf16[3,3,3,192,192]{4,3,2,1,0:T(8,128)(2,1)}, u32[]{:S(2)}) %copy-start.1) | copy-done | bytes 1990680
  38.0 1.7 %copy-done.2 = bf16[3,3,3,192,192]{4,3,2,1,0:T(8,128)(2,1)S(1)} copy-done((bf16[3,3,3,192,192]{4,3,2,1,0:T(8,128)(2,1)S(1)}, bf16[3,3,3,192,192]{4,3,2,1,0:T(8,128)(2,1)}, u32[]{:S(2)}) %copy-start.2) | copy-done | bytes 1990680
  39.7 0.0 copy-start.7
  39.8 2.8 %pack_weights.1 = (bf16[3,192,1792]{2,1,0:T(8,128)(2,1)}, bf16[3,192,1792]{2,1,0:T(8,128)(2,1)}, bf16[192,1152]{1,0:T(8,128)(2,1)}) custom-call(bf16[3,3,3,192,192]{4,3,2,1,0:T(8,128)(2,1)S(1)} %copy-done.2, bf16[3,3,3,192,192]{4,3,2,1,0:T(8,128)(2,1)S(1)} %copy-done.1, bf16[3,3,192,96]{3,2,1,0:T(8,128)(2,1)S(1)} %copy-done.4), custom_call_target="tpu_custom_call" | custom-call | tf_op jit(solution)/shard_map/pack_weights/pallas_call | solution.py:379
  42.6 0.6 add_convert_fusion.refs_0_
  43.2 0.0 copy-done.12
  43.2 1.9 %collective-permute-start.4 = (bf16[4,5,80,96]{3,2,1,0:T(8,128)(2,1)S(1)}, bf16[4,5,80,96]{3,2,1,0:T(8,128)(2,1)S(1)}, u32[]{:S(2)}, u32[]{:S(2)}) collective-permute-start(bf16[4,5,80,96]{3,2,1,0:T(8,128)(2,1)S(1)} %copy-done.12), channel_id=1, source_target_pairs={{0,16},{16,32},{32,48},{48,64},{64,80},{80,96},{96,112},{1,17},{17... | collective-permute-start | bytes 921608 | tf_op jit(solution)/shard_map/ppermute | solution.py:20
  45.1 0.0 copy-done.11
  45.2 6.2 %collective-permute-start.5 = (bf16[4,5,80,96]{3,2,1,0:T(8,128)(2,1)S(1)}, bf16[4,5,80,96]{3,2,1,0:T(8,128)(2,1)S(1)}, u32[]{:S(2)}, u32[]{:S(2)}) collective-permute-start(bf16[4,5,80,96]{3,2,1,0:T(8,128)(2,1)S(1)} %copy-done.11), channel_id=1, source_target_pairs={{16,0},{32,16},{48,32},{64,48},{80,64},{96,80},{112,96},{17,1},{33... | collective-permute-start | bytes 921608 | tf_op jit(solution)/shard_map/ppermute | solution.py:20
  51.4 0.0 collective-permute-done.2.refs_2_
  51.4 0.0 collective-permute-done.3.refs_3_
  51.4 0.0 copy-done.3
  51.4 0.0 copy-done.6
  51.4 0.0 copy-done.7
  51.4 15.2 %forward_block.1 = (f32[4,34,32,192]{3,2,1,0:T(8,128)}, f32[4,5,16,192]{3,2,1,0:T(8,128)S(1)}) custom-call(bf16[4,32,32,192]{3,2,1,0:T(8,128)(2,1)S(1)} %copy-done, bf16[4,32,8,192]{3,2,1,0:T(8,128)(2,1)S(1)} %maximum_maximum_fusion.refs_1_, bf16[4,2,40,192]{3,2,1,0:T(8,128)(2,1)S(1)} %collective-permute-done.2.refs_2_, ...), custom_call_target="tpu_custom_call" | custom-call | flops 20000000000 | bytes 12000000 | tf_op jit(solution)/shard_map/forward_block/pallas_call | solution.py:411
  66.7 0.0 copy-start.5
  66.7 0.7 copy-done.5
  67.4 0.0 collective-permute-done.4.refs_6_
  67.4 0.0 collective-permute-done.5.refs_7_
  67.4 0.8 copy-done.9
  68.1 0.1 copy-done.10
  68.3 39.8 %backward_block.1 = bf16[4,32,32,192]{3,2,1,0:T(8,128)(2,1)} custom-call(s32[4]{0:T(128)} %add_convert_fusion.refs_0_, bf16[4,32,32,192]{3,2,1,0:T(8,128)(2,1)} %refs_1_.1, f32[4,34,32,192]{3,2,1,0:T(8,128)} %get-tuple-element.23.refs_2_, f32[4,5,16,192]{3,2,1,0:T(8,128)} %copy-done.5, bf16[4,64,64,96]{3,2,1,0:T(8,128)(2,1)} %refs_4_.3, ...), custom_call_target="tpu_custom_call" | custom-call | tf_op jit(solution)/shard_map/backward_block/pallas_call | solution.py:430
  (13 shorter events, 0.1 us)
Async XLA Ops:
  3.1 10.4 %copy-start = (bf16[4,32,32,192]{3,2,1,0:T(8,128)(2,1)S(1)}, bf16[4,32,32,192]{3,2,1,0:T(8,128)(2,1)}, u32[]{:S(2)}) copy-start(bf16[4,32,32,192]{3,2,1,0:T(8,128)(2,1)} %refs_1_.1) | copy-start | bytes 4718596
  4.0 12.9 %collective-permute-start = (bf16[4,64,8,96]{3,2,1,0:T(8,128)(2,1)S(1)}, bf16[4,64,8,96]{3,2,1,0:T(8,128)(2,1)S(1)}, u32[]{:S(2)}, u32[]{:S(2)}) collective-permute-start(bf16[4,64,8,96]{3,2,1,0:T(8,128)(2,1)S(1)} %get-tuple-element.19), channel_id=1, source_target_pairs={{1,0},{2,1},{3,2},{4,3},{5,4},{6,5},{7,6},{8,7},{9,8},{10,9},{11,1... | collective-permute-start | bytes 1179656 | tf_op jit(solution)/shard_map/ppermute | solution.py:20
  10.2 14.1 %collective-permute-start.1 = (bf16[4,64,8,96]{3,2,1,0:T(8,128)(2,1)S(1)}, bf16[4,64,8,96]{3,2,1,0:T(8,128)(2,1)S(1)}, u32[]{:S(2)}, u32[]{:S(2)}) collective-permute-start(bf16[4,64,8,96]{3,2,1,0:T(8,128)(2,1)S(1)} %get-tuple-element.20), channel_id=1, source_target_pairs={{0,1},{1,2},{2,3},{3,4},{4,5},{5,6},{6,7},{7,8},{8,9},{9,10},{10,1... | collective-permute-start | bytes 1179656 | tf_op jit(solution)/shard_map/ppermute | solution.py:20
  25.2 11.0 %copy-start.4 = (bf16[3,3,192,96]{3,2,1,0:T(8,128)(2,1)S(1)}, bf16[3,3,192,96]{3,2,1,0:T(8,128)(2,1)}, u32[]{:S(2)}) copy-start(bf16[3,3,192,96]{3,2,1,0:T(8,128)(2,1)} %wup) | copy-start | bytes 995332
  25.7 2.6 %copy-start.8 = (bf16[4,64,16,96]{3,2,1,0:T(8,128)(2,1)}, bf16[4,64,16,96]{3,2,1,0:T(8,128)(2,1)S(1)}, u32[]{:S(2)}) copy-start(bf16[4,64,16,96]{3,2,1,0:T(8,128)(2,1)S(1)} %pad_maximum_fusion.refs_5_) | copy-start | bytes 2359300
  28.2 23.1 %collective-permute-start.2 = (bf16[4,2,40,192]{3,2,1,0:T(8,128)(2,1)}, bf16[4,2,40,192]{3,2,1,0:T(8,128)(2,1)S(1)}, u32[]{:S(2)}, u32[]{:S(2)}) collective-permute-start(bf16[4,2,40,192]{3,2,1,0:T(8,128)(2,1)} %pad_maximum_fusion.3), channel_id=1, source_target_pairs={{0,16},{16,32},{32,48},{48,64},{64,80},{80,96},{96,112},{1,17},{17... | collective-permute-start | bytes 368648 | tf_op jit(solution)/shard_map/ppermute | solution.py:20
  31.7 19.7 %collective-permute-start.3 = (bf16[4,2,40,192]{3,2,1,0:T(8,128)(2,1)S(1)}, bf16[4,2,40,192]{3,2,1,0:T(8,128)(2,1)S(1)}, u32[]{:S(2)}, u32[]{:S(2)}) collective-permute-start(bf16[4,2,40,192]{3,2,1,0:T(8,128)(2,1)S(1)} %pad_maximum_fusion.4), channel_id=1, source_target_pairs={{16,0},{32,16},{48,32},{64,48},{80,64},{96,80},{112,96},{17,1},{33... | collective-permute-start | bytes 368648 | tf_op jit(solution)/shard_map/ppermute | solution.py:20
  36.2 1.8 %copy-start.1 = (bf16[3,3,3,192,192]{4,3,2,1,0:T(8,128)(2,1)S(1)}, bf16[3,3,3,192,192]{4,3,2,1,0:T(8,128)(2,1)}, u32[]{:S(2)}) copy-start(bf16[3,3,3,192,192]{4,3,2,1,0:T(8,128)(2,1)} %w2) | copy-start | bytes 5971972
  38.0 1.7 %copy-start.2 = (bf16[3,3,3,192,192]{4,3,2,1,0:T(8,128)(2,1)S(1)}, bf16[3,3,3,192,192]{4,3,2,1,0:T(8,128)(2,1)}, u32[]{:S(2)}) copy-start(bf16[3,3,3,192,192]{4,3,2,1,0:T(8,128)(2,1)} %w1) | copy-start | bytes 5971972
  39.7 3.5 %copy-start.12 = (bf16[4,5,80,96]{3,2,1,0:T(8,128)(2,1)S(1)}, bf16[4,5,80,96]{3,2,1,0:T(8,128)(2,1)}, u32[]{:S(2)}) copy-start(bf16[4,5,80,96]{3,2,1,0:T(8,128)(2,1)} %pad_maximum_fusion.1) | copy-start | bytes 921604
  39.7 5.4 %copy-start.11 = (bf16[4,5,80,96]{3,2,1,0:T(8,128)(2,1)S(1)}, bf16[4,5,80,96]{3,2,1,0:T(8,128)(2,1)}, u32[]{:S(2)}) copy-start(bf16[4,5,80,96]{3,2,1,0:T(8,128)(2,1)} %pad_maximum_fusion.2) | copy-start | bytes 921604
  39.7 11.7 %copy-start.3 = (bf16[3,3,3,192,192]{4,3,2,1,0:T(8,128)(2,1)S(1)}, bf16[3,3,3,192,192]{4,3,2,1,0:T(8,128)(2,1)}, u32[]{:S(2)}) copy-start(bf16[3,3,3,192,192]{4,3,2,1,0:T(8,128)(2,1)} %w1) | copy-start | bytes 5971972
  39.7 11.7 %copy-start.6 = (f32[192]{0:T(256)S(1)}, f32[192]{0:T(256)}, u32[]{:S(2)}) copy-start(f32[192]{0:T(256)} %param.11) | copy-start | bytes 2308
  39.7 11.7 %copy-start.7 = (f32[192]{0:T(256)S(1)}, f32[192]{0:T(256)}, u32[]{:S(2)}) copy-start(f32[192]{0:T(256)} %param.10) | copy-start | bytes 2308
  43.2 24.1 %collective-permute-start.4 = (bf16[4,5,80,96]{3,2,1,0:T(8,128)(2,1)S(1)}, bf16[4,5,80,96]{3,2,1,0:T(8,128)(2,1)S(1)}, u32[]{:S(2)}, u32[]{:S(2)}) collective-permute-start(bf16[4,5,80,96]{3,2,1,0:T(8,128)(2,1)S(1)} %copy-done.12), channel_id=1, source_target_pairs={{0,16},{16,32},{32,48},{48,64},{64,80},{80,96},{96,112},{1,17},{17... | collective-permute-start | bytes 921608 | tf_op jit(solution)/shard_map/ppermute | solution.py:20
  45.2 22.2 %collective-permute-start.5 = (bf16[4,5,80,96]{3,2,1,0:T(8,128)(2,1)S(1)}, bf16[4,5,80,96]{3,2,1,0:T(8,128)(2,1)S(1)}, u32[]{:S(2)}, u32[]{:S(2)}) collective-permute-start(bf16[4,5,80,96]{3,2,1,0:T(8,128)(2,1)S(1)} %copy-done.11), channel_id=1, source_target_pairs={{16,0},{32,16},{48,32},{64,48},{80,64},{96,80},{112,96},{17,1},{33... | collective-permute-start | bytes 921608 | tf_op jit(solution)/shard_map/ppermute | solution.py:20
  66.7 0.7 copy-start.5
  67.4 0.8 copy-start.9
  67.4 0.9 copy-start.10

commit v5 on v3

--- a/solution.py
+++ b/solution.py
@@ -116,13 +116,9 @@
 
 
 def forward(*refs):
-    feat_in, feat_side, before, after, w1_in, bias, gain1, pre_out, pre_strip = refs[:9]
+    feat, feat_side, before, after, w1, bias, gain1, pre_out, pre_strip = refs[:9]
     act, act_strip = refs[9:13], refs[13:17]
-    act_tail, act_rows, pre, feat, w1, sem = refs[17:]
-    load_feat = [pltpu.make_async_copy(feat_in.at[t], feat.at[t], sem.at[4 + t]) for t in range(4)]
-    load_w1 = pltpu.make_async_copy(w1_in, w1, sem.at[8])
-    for copy in (load_feat[0], load_w1, *load_feat[1:]):
-        copy.start()
+    act_tail, act_rows, pre, sem = refs[17:]
     stores = [pltpu.make_async_copy(pre.at[t], pre_out.at[t], sem.at[t]) for t in range(4)]
     for n in range(4):
         act[n][35, :, 576:640] = jnp.zeros((32, 64), BF16)
@@ -157,12 +153,11 @@
         return run
 
     done = lambda t: lambda: build_strip(act_strip[t], act_tail)
-    load_feat[0].wait()
     run_steps(
         [
-            ([activate(0)], [done(0), load_w1.wait, load_feat[1].wait]),
-            ([first_conv(0), activate(1)], [done(1), stores[0].start, load_feat[2].wait]),
-            ([first_conv(1), activate(2)], [done(2), stores[1].start, load_feat[3].wait]),
+            ([activate(0)], [done(0)]),
+            ([first_conv(0), activate(1)], [done(1), stores[0].start]),
+            ([first_conv(1), activate(2)], [done(2), stores[1].start]),
             ([first_conv(2), activate(3)], [done(3), stores[2].start]),
             ([first_conv(3)], [stores[3].start]),
         ]
@@ -402,21 +397,19 @@
     pre, pre_strip = pl.pallas_call(
         forward,
         out_shape=[
-            jax.ShapeDtypeStruct((4, 34, 32, 192), F32),
-            jax.ShapeDtypeStruct((4, DEEP, 16, 192), F32),
+            pltpu.HBM((4, 34, 32, 192), F32),
+            pltpu.HBM((4, DEEP, 16, 192), F32),
         ],
-        in_specs=[own] + [vmem] * 3 + [own] + [vmem] * 2,
+        in_specs=[vmem] * 7,
         out_specs=[own, vmem],
         scratch_shapes=[pltpu.VMEM((36, 32, 640), BF16)] * 4
         + [pltpu.VMEM((DEEP + 2, 16, 640), BF16)] * 4
         + [pltpu.VMEM((5, 8 * (7 + 7 * DEEP), 128), F32), pltpu.VMEM((18, COLS, 192), F32)]
         + [
             pltpu.VMEM((4, 34, 32, 192), F32),
-            pltpu.VMEM((4, 32, 32, 192), BF16),
-            pltpu.VMEM((3, 3, 3, 192, 192), BF16),
-            pltpu.SemaphoreType.DMA((9,)),
+            pltpu.SemaphoreType.DMA((4,)),
         ],
-        compiler_params=pltpu.CompilerParams(vmem_limit_bytes=60 * 1024 * 1024),
+        compiler_params=pltpu.CompilerParams(vmem_limit_bytes=30 * 1024 * 1024),
         cost_estimate=pl.CostEstimate(flops=20_000_000_000, transcendentals=1_000_000, bytes_accessed=12_000_000),
         name="forward_block",
     )(features, feat_side, before, after, conv_first, bias, gain1)

time: 99.4 us -> 99.8 us (level)
  Pallas kernels: 58.9 us -> 56.6 us
  other arithmetic: 2.86 us -> 4.42 us
    pallas_call x1, Pallas kernels: 18.2 us -> 16 us  [per_device(): pl.pallas_call(forward, out_shape=[pltpu.HBM((4, 34, 32, 192), F32), pltp...]
    concatenate x2, other arithmetic: 0.22 us -> 1.74 us  [rows(): return jnp.concatenate([field[:, part], side[:, part]], axis=2)]
    unnamed x12 -> x14, local copies, waits for them, and re-layouts: 1.62 us -> 2.64 us
  transfers between devices with their start and end apart: 6 -> 6, of which waited for: 2 -> 2; matrix products, arithmetic and copies ran while one was open for 4% -> 3% of each run, Pallas kernels for 18% -> 16%
where the time goes in v5:
time: 99.8 us; the launch traced here: 99.3 us
  Pallas kernels  56.6 us (57%)
  starting transfers between devices  25.4 us (25%)
  local copies, waits for them, and re-layouts  7.33 us (7%)
  waiting for transfers between devices  5.21 us (5%)
  other arithmetic  4.42 us (4%)
    pallas_call x1, Pallas kernels, per_device(): pl.pallas_call(backward, out_shape=jax.ShapeDtypeStruct(features.shape, B...  40.6 us
    ppermute x3, starting transfers between devices, shift_pair(): lax.ppermute(value_down, axis, down)  17.9 us
    pallas_call x1, Pallas kernels, per_device(): pl.pallas_call(forward, out_shape=[pltpu.HBM((4, 34, 32, 192), F32), pltp...  16 us
    ppermute x3, starting transfers between devices, shift_pair(): lax.ppermute(value_up, axis, up)  7.43 us
    ppermute x3, waiting for transfers between devices, shift_pair(): lax.ppermute(value_up, axis, up)  3.14 us
    unnamed x14, local copies, waits for them, and re-layouts  2.64 us
    ppermute x3, waiting for transfers between devices, shift_pair(): lax.ppermute(value_down, axis, down)  2.07 us
  transfers between devices with their start and end apart: 6, of which 2 were waited for; matrix products, arithmetic and copies ran while one was open for 3% of the time, Pallas kernels for 16%

profile of v5, /device:TPU:6, one launch (start us, length us, event | category | flops | bytes accessed | tf_op | source)
XLA Modules:
  0.0 99.3 jit_solution(408988544807800008)
XLA Ops:
  0.0 1.7 %fusion.13 = (bf16[4,32,2,96]{3,2,1,0:T(2,128)(2,1)S(1)}, bf16[4,32,2,96]{3,2,1,0:T(2,128)(2,1)S(1)}, bf16[4,32,2,96]{3,2,1,0:T(2,128)(2,1)S(1)}, bf16[4,32,2,96]{3,2,1,0:T(2,128)(2,1)S(1)}) fusion(bf16[4,32,32,192]{3,2,1,0:T(8,128)(2,1)} %refs_1_.1), kind=kLoop, calls=%fused_computation.21 | loop fusion | bytes 393216 | tf_op jit(solution)/shard_map/slice | solution.py:361
  1.7 1.4 %fusion.11 = (bf16[4,64,5,96]{3,2,1,0:T(8,128)(2,1)S(1)}, bf16[4,64,5,96]{3,2,1,0:T(8,128)(2,1)S(1)}) fusion(bf16[4,64,64,96]{3,2,1,0:T(8,128)(2,1)} %refs_4_.3), kind=kLoop, calls=%fused_computation.19 | loop fusion | bytes 983040 | tf_op jit(solution)/shard_map/slice | solution.py:368
  3.1 0.0 copy-start
  3.1 0.4 fusion.8
  3.6 2.1 %collective-permute-start.1 = (bf16[4,64,8,96]{3,2,1,0:T(8,128)(2,1)S(1)}, bf16[4,64,8,96]{3,2,1,0:T(8,128)(2,1)S(1)}, u32[]{:S(2)}, u32[]{:S(2)}) collective-permute-start(bf16[4,64,8,96]{3,2,1,0:T(8,128)(2,1)S(1)} %fusion.8), channel_id=1, source_target_pairs={{0,1},{1,2},{2,3},{3,4},{4,5},{5,6},{6,7},{7,8},{8,9},{9,10},{10,1... | collective-permute-start | bytes 1179656 | tf_op jit(solution)/shard_map/ppermute | solution.py:20
  5.6 0.4 fusion.6
  6.1 7.3 %collective-permute-start = (bf16[4,64,8,96]{3,2,1,0:T(8,128)(2,1)S(1)}, bf16[4,64,8,96]{3,2,1,0:T(8,128)(2,1)S(1)}, u32[]{:S(2)}, u32[]{:S(2)}) collective-permute-start(bf16[4,64,8,96]{3,2,1,0:T(8,128)(2,1)S(1)} %fusion.6), channel_id=1, source_target_pairs={{1,0},{2,1},{3,2},{4,3},{5,4},{6,5},{7,6},{8,7},{9,8},{10,9},{11,1... | collective-permute-start | bytes 1179656 | tf_op jit(solution)/shard_map/ppermute | solution.py:20
  13.4 0.1 pad.22.clone
  13.4 0.1 pad.14.clone
  13.5 1.1 %fusion.10 = (bf16[4,5,64,96]{3,2,1,0:T(8,128)(2,1)S(1)}, bf16[4,5,64,96]{3,2,1,0:T(8,128)(2,1)S(1)}) fusion(bf16[4,64,64,96]{3,2,1,0:T(8,128)(2,1)} %refs_4_.3), kind=kLoop, calls=%fused_computation.18 | loop fusion | bytes 983040 | tf_op jit(solution)/shard_map/slice | solution.py:383
  14.6 0.0 copy-done
  14.7 3.1 %collective-permute-done.1 = bf16[4,64,8,96]{3,2,1,0:T(8,128)(2,1)S(1)} collective-permute-done((bf16[4,64,8,96]{3,2,1,0:T(8,128)(2,1)S(1)}, bf16[4,64,8,96]{3,2,1,0:T(8,128)(2,1)S(1)}, u32[]{:S(2)}, u32[]{:S(2)}) %collective-permute-start.1) | collective-permute-done | bytes 393248 | tf_op jit(solution)/shard_map/ppermute | solution.py:20
  17.8 0.1 fusion.17
  18.0 2.1 %collective-permute-done = bf16[4,64,8,96]{3,2,1,0:T(8,128)(2,1)S(1)} collective-permute-done((bf16[4,64,8,96]{3,2,1,0:T(8,128)(2,1)S(1)}, bf16[4,64,8,96]{3,2,1,0:T(8,128)(2,1)S(1)}, u32[]{:S(2)}, u32[]{:S(2)}) %collective-permute-start) | collective-permute-done | bytes 393248 | tf_op jit(solution)/shard_map/ppermute | solution.py:20
  20.0 0.1 fusion.16
  20.2 0.7 maximum_maximum_fusion.refs_1_
  20.9 0.0 copy-start.2
  20.9 0.0 copy-start.3
  20.9 0.5 pad_maximum_fusion.refs_5_
  21.4 0.0 copy-start.4
  21.4 0.8 pad_maximum_fusion.3
  22.2 0.9 pad_maximum_fusion.1
  23.1 0.0 copy-done.4
  23.1 3.5 %collective-permute-start.2 = (bf16[4,2,40,192]{3,2,1,0:T(8,128)(2,1)}, bf16[4,2,40,192]{3,2,1,0:T(8,128)(2,1)S(1)}, u32[]{:S(2)}, u32[]{:S(2)}) collective-permute-start(bf16[4,2,40,192]{3,2,1,0:T(8,128)(2,1)} %get-tuple-element.11), channel_id=1, source_target_pairs={{0,16},{16,32},{32,48},{48,64},{64,80},{80,96},{96,112},{1,17},{17... | collective-permute-start | bytes 368648 | tf_op jit(solution)/shard_map/ppermute | solution.py:20
  26.6 4.5 %collective-permute-start.3 = (bf16[4,2,40,192]{3,2,1,0:T(8,128)(2,1)S(1)}, bf16[4,2,40,192]{3,2,1,0:T(8,128)(2,1)S(1)}, u32[]{:S(2)}, u32[]{:S(2)}) collective-permute-start(bf16[4,2,40,192]{3,2,1,0:T(8,128)(2,1)S(1)} %get-tuple-element.12), channel_id=1, source_target_pairs={{16,0},{32,16},{48,32},{64,48},{80,64},{96,80},{112,96},{17,1},{33... | collective-permute-start | bytes 368648 | tf_op jit(solution)/shard_map/ppermute | solution.py:20
  31.1 0.6 add_convert_fusion.refs_0_
  31.7 1.9 %collective-permute-start.4 = (bf16[4,5,80,96]{3,2,1,0:T(8,128)(2,1)}, bf16[4,5,80,96]{3,2,1,0:T(8,128)(2,1)S(1)}, u32[]{:S(2)}, u32[]{:S(2)}) collective-permute-start(bf16[4,5,80,96]{3,2,1,0:T(8,128)(2,1)} %get-tuple-element.15), channel_id=1, source_target_pairs={{0,16},{16,32},{32,48},{48,64},{64,80},{80,96},{96,112},{1,17},{17... | collective-permute-start | bytes 921608 | tf_op jit(solution)/shard_map/ppermute | solution.py:20
  33.7 6.2 %collective-permute-start.5 = (bf16[4,5,80,96]{3,2,1,0:T(8,128)(2,1)S(1)}, bf16[4,5,80,96]{3,2,1,0:T(8,128)(2,1)S(1)}, u32[]{:S(2)}, u32[]{:S(2)}) collective-permute-start(bf16[4,5,80,96]{3,2,1,0:T(8,128)(2,1)S(1)} %get-tuple-element.16), channel_id=1, source_target_pairs={{16,0},{32,16},{48,32},{64,48},{80,64},{96,80},{112,96},{17,1},{33... | collective-permute-start | bytes 921608 | tf_op jit(solution)/shard_map/ppermute | solution.py:20
  39.9 0.0 collective-permute-done.2.refs_2_
  39.9 0.0 collective-permute-done.3.refs_3_
  39.9 0.0 copy-done.2
  39.9 0.0 copy-done.3
  39.9 0.0 copy-start.1
  39.9 1.7 %copy-done.1 = bf16[3,3,3,192,192]{4,3,2,1,0:T(8,128)(2,1)S(1)} copy-done((bf16[3,3,3,192,192]{4,3,2,1,0:T(8,128)(2,1)S(1)}, bf16[3,3,3,192,192]{4,3,2,1,0:T(8,128)(2,1)}, u32[]{:S(2)}) %copy-start.1) | copy-done | bytes 1990680
  41.7 16.0 %forward_block.1 = (f32[4,34,32,192]{3,2,1,0:T(8,128)}, f32[4,5,16,192]{3,2,1,0:T(8,128)}) custom-call(bf16[4,32,32,192]{3,2,1,0:T(8,128)(2,1)S(1)} %copy-done, bf16[4,32,8,192]{3,2,1,0:T(8,128)(2,1)S(1)} %maximum_maximum_fusion.refs_1_, bf16[4,2,40,192]{3,2,1,0:T(8,128)(2,1)S(1)} %collective-permute-done.2.refs_2_, ...), custom_call_target="tpu_custom_call" | custom-call | flops 20000000000 | bytes 12000000 | tf_op jit(solution)/shard_map/forward_block/pallas_call | solution.py:397
  57.7 0.0 collective-permute-done.4.refs_6_
  57.7 0.0 copy-start.5
  57.7 0.0 collective-permute-done.5.refs_7_
  57.7 0.0 copy-start.6
  57.7 0.7 copy-done.5
  58.4 0.1 copy-done.6
  58.6 40.6 %backward_block.1 = bf16[4,32,32,192]{3,2,1,0:T(8,128)(2,1)} custom-call(s32[4]{0:T(128)} %add_convert_fusion.refs_0_, bf16[4,32,32,192]{3,2,1,0:T(8,128)(2,1)} %refs_1_.1, f32[4,34,32,192]{3,2,1,0:T(8,128)} %get-tuple-element.13.refs_2_, f32[4,5,16,192]{3,2,1,0:T(8,128)} %get-tuple-element.14.refs_3_, bf16[4,64,64,96]{3,2,1,0:T(8,128)(2,1)} %refs_4_.3, ...), custom_call_target="tpu_custom_call" | custom-call | tf_op jit(solution)/shard_map/backward_block/pallas_call | solution.py:416
  (5 shorter events, 0.0 us)
Async XLA Ops:
  3.1 11.5 %copy-start = (bf16[4,32,32,192]{3,2,1,0:T(8,128)(2,1)S(1)}, bf16[4,32,32,192]{3,2,1,0:T(8,128)(2,1)}, u32[]{:S(2)}) copy-start(bf16[4,32,32,192]{3,2,1,0:T(8,128)(2,1)} %refs_1_.1) | copy-start | bytes 4718596
  3.6 14.2 %collective-permute-start.1 = (bf16[4,64,8,96]{3,2,1,0:T(8,128)(2,1)S(1)}, bf16[4,64,8,96]{3,2,1,0:T(8,128)(2,1)S(1)}, u32[]{:S(2)}, u32[]{:S(2)}) collective-permute-start(bf16[4,64,8,96]{3,2,1,0:T(8,128)(2,1)S(1)} %fusion.8), channel_id=1, source_target_pairs={{0,1},{1,2},{2,3},{3,4},{4,5},{5,6},{6,7},{7,8},{8,9},{9,10},{10,1... | collective-permute-start | bytes 1179656 | tf_op jit(solution)/shard_map/ppermute | solution.py:20
  6.1 13.9 %collective-permute-start = (bf16[4,64,8,96]{3,2,1,0:T(8,128)(2,1)S(1)}, bf16[4,64,8,96]{3,2,1,0:T(8,128)(2,1)S(1)}, u32[]{:S(2)}, u32[]{:S(2)}) collective-permute-start(bf16[4,64,8,96]{3,2,1,0:T(8,128)(2,1)S(1)} %fusion.6), channel_id=1, source_target_pairs={{1,0},{2,1},{3,2},{4,3},{5,4},{6,5},{7,6},{8,7},{9,8},{10,9},{11,1... | collective-permute-start | bytes 1179656 | tf_op jit(solution)/shard_map/ppermute | solution.py:20
  20.9 19.0 %copy-start.2 = (f32[192]{0:T(256)S(1)}, f32[192]{0:T(256)}, u32[]{:S(2)}) copy-start(f32[192]{0:T(256)} %param.11) | copy-start | bytes 2308
  20.9 19.0 %copy-start.3 = (f32[192]{0:T(256)S(1)}, f32[192]{0:T(256)}, u32[]{:S(2)}) copy-start(f32[192]{0:T(256)} %param.10) | copy-start | bytes 2308
  21.4 1.8 %copy-start.4 = (bf16[4,64,16,96]{3,2,1,0:T(8,128)(2,1)}, bf16[4,64,16,96]{3,2,1,0:T(8,128)(2,1)S(1)}, u32[]{:S(2)}) copy-start(bf16[4,64,16,96]{3,2,1,0:T(8,128)(2,1)S(1)} %pad_maximum_fusion.refs_5_) | copy-start | bytes 2359300
  23.1 16.8 %collective-permute-start.2 = (bf16[4,2,40,192]{3,2,1,0:T(8,128)(2,1)}, bf16[4,2,40,192]{3,2,1,0:T(8,128)(2,1)S(1)}, u32[]{:S(2)}, u32[]{:S(2)}) collective-permute-start(bf16[4,2,40,192]{3,2,1,0:T(8,128)(2,1)} %get-tuple-element.11), channel_id=1, source_target_pairs={{0,16},{16,32},{32,48},{48,64},{64,80},{80,96},{96,112},{1,17},{17... | collective-permute-start | bytes 368648 | tf_op jit(solution)/shard_map/ppermute | solution.py:20
  26.6 13.3 %collective-permute-start.3 = (bf16[4,2,40,192]{3,2,1,0:T(8,128)(2,1)S(1)}, bf16[4,2,40,192]{3,2,1,0:T(8,128)(2,1)S(1)}, u32[]{:S(2)}, u32[]{:S(2)}) collective-permute-start(bf16[4,2,40,192]{3,2,1,0:T(8,128)(2,1)S(1)} %get-tuple-element.12), channel_id=1, source_target_pairs={{16,0},{32,16},{48,32},{64,48},{80,64},{96,80},{112,96},{17,1},{33... | collective-permute-start | bytes 368648 | tf_op jit(solution)/shard_map/ppermute | solution.py:20
  31.7 25.9 %collective-permute-start.4 = (bf16[4,5,80,96]{3,2,1,0:T(8,128)(2,1)}, bf16[4,5,80,96]{3,2,1,0:T(8,128)(2,1)S(1)}, u32[]{:S(2)}, u32[]{:S(2)}) collective-permute-start(bf16[4,5,80,96]{3,2,1,0:T(8,128)(2,1)} %get-tuple-element.15), channel_id=1, source_target_pairs={{0,16},{16,32},{32,48},{48,64},{64,80},{80,96},{96,112},{1,17},{17... | collective-permute-start | bytes 921608 | tf_op jit(solution)/shard_map/ppermute | solution.py:20
  33.7 24.0 %collective-permute-start.5 = (bf16[4,5,80,96]{3,2,1,0:T(8,128)(2,1)S(1)}, bf16[4,5,80,96]{3,2,1,0:T(8,128)(2,1)S(1)}, u32[]{:S(2)}, u32[]{:S(2)}) collective-permute-start(bf16[4,5,80,96]{3,2,1,0:T(8,128)(2,1)S(1)} %get-tuple-element.16), channel_id=1, source_target_pairs={{16,0},{32,16},{48,32},{64,48},{80,64},{96,80},{112,96},{17,1},{33... | collective-permute-start | bytes 921608 | tf_op jit(solution)/shard_map/ppermute | solution.py:20
  39.9 1.8 %copy-start.1 = (bf16[3,3,3,192,192]{4,3,2,1,0:T(8,128)(2,1)S(1)}, bf16[3,3,3,192,192]{4,3,2,1,0:T(8,128)(2,1)}, u32[]{:S(2)}) copy-start(bf16[3,3,3,192,192]{4,3,2,1,0:T(8,128)(2,1)} %refs_8_.1) | copy-start | bytes 5971972
  57.7 0.8 copy-start.5
  57.7 0.9 copy-start.6

commit v6 on v5

--- a/solution.py
+++ b/solution.py
@@ -116,9 +116,11 @@
 
 
 def forward(*refs):
-    feat, feat_side, before, after, w1, bias, gain1, pre_out, pre_strip = refs[:9]
+    feat, feat_side, before, after, w1_in, bias, gain1, pre_out, pre_strip = refs[:9]
     act, act_strip = refs[9:13], refs[13:17]
-    act_tail, act_rows, pre, sem = refs[17:]
+    act_tail, act_rows, pre, w1, sem = refs[17:]
+    load_w1 = pltpu.make_async_copy(w1_in, w1, sem.at[4])
+    load_w1.start()
     stores = [pltpu.make_async_copy(pre.at[t], pre_out.at[t], sem.at[t]) for t in range(4)]
     for n in range(4):
         act[n][35, :, 576:640] = jnp.zeros((32, 64), BF16)
@@ -155,7 +157,7 @@
     done = lambda t: lambda: build_strip(act_strip[t], act_tail)
     run_steps(
         [
-            ([activate(0)], [done(0)]),
+            ([activate(0)], [done(0), load_w1.wait]),
             ([first_conv(0), activate(1)], [done(1), stores[0].start]),
             ([first_conv(1), activate(2)], [done(2), stores[1].start]),
             ([first_conv(2), activate(3)], [done(3), stores[2].start]),
@@ -400,16 +402,17 @@
             pltpu.HBM((4, 34, 32, 192), F32),
             pltpu.HBM((4, DEEP, 16, 192), F32),
         ],
-        in_specs=[vmem] * 7,
+        in_specs=[vmem] * 4 + [own] + [vmem] * 2,
         out_specs=[own, vmem],
         scratch_shapes=[pltpu.VMEM((36, 32, 640), BF16)] * 4
         + [pltpu.VMEM((DEEP + 2, 16, 640), BF16)] * 4
         + [pltpu.VMEM((5, 8 * (7 + 7 * DEEP), 128), F32), pltpu.VMEM((18, COLS, 192), F32)]
         + [
             pltpu.VMEM((4, 34, 32, 192), F32),
-            pltpu.SemaphoreType.DMA((4,)),
+            pltpu.VMEM((3, 3, 3, 192, 192), BF16),
+            pltpu.SemaphoreType.DMA((5,)),
         ],
-        compiler_params=pltpu.CompilerParams(vmem_limit_bytes=30 * 1024 * 1024),
+        compiler_params=pltpu.CompilerParams(vmem_limit_bytes=34 * 1024 * 1024),
         cost_estimate=pl.CostEstimate(flops=20_000_000_000, transcendentals=1_000_000, bytes_accessed=12_000_000),
         name="forward_block",
     )(features, feat_side, before, after, conv_first, bias, gain1)

time: 99.8 us -> 100 us (level)
  no operation moved by 1% of the time
where the time goes in v6:
time: 100 us; the launch traced here: 99.6 us
  Pallas kernels  56.8 us (57%)
  starting transfers between devices  25.4 us (25%)
  local copies, waits for them, and re-layouts  7.33 us (7%)
  waiting for transfers between devices  5.21 us (5%)
  other arithmetic  4.42 us (4%)
    pallas_call x1, Pallas kernels, per_device(): pl.pallas_call(backward, out_shape=jax.ShapeDtypeStruct(features.shape, B...  40.6 us
    ppermute x3, starting transfers between devices, shift_pair(): lax.ppermute(value_down, axis, down)  17.9 us
    pallas_call x1, Pallas kernels, per_device(): pl.pallas_call(forward, out_shape=[pltpu.HBM((4, 34, 32, 192), F32), pltp...  16.2 us
    ppermute x3, starting transfers between devices, shift_pair(): lax.ppermute(value_up, axis, up)  7.43 us
    ppermute x3, waiting for transfers between devices, shift_pair(): lax.ppermute(value_up, axis, up)  3.14 us
    unnamed x14, local copies, waits for them, and re-layouts  2.64 us
    ppermute x3, waiting for transfers between devices, shift_pair(): lax.ppermute(value_down, axis, down)  2.07 us
  transfers between devices with their start and end apart: 6, of which 2 were waited for; matrix products, arithmetic and copies ran while one was open for 3% of the time, Pallas kernels for 16%

profile of v6, /device:TPU:6, one launch (start us, length us, event | category | flops | bytes accessed | tf_op | source)
XLA Modules:
  0.0 99.6 jit_solution(12780410177735692359)
XLA Ops:
  0.0 1.7 %fusion.13 = (bf16[4,32,2,96]{3,2,1,0:T(2,128)(2,1)S(1)}, bf16[4,32,2,96]{3,2,1,0:T(2,128)(2,1)S(1)}, bf16[4,32,2,96]{3,2,1,0:T(2,128)(2,1)S(1)}, bf16[4,32,2,96]{3,2,1,0:T(2,128)(2,1)S(1)}) fusion(bf16[4,32,32,192]{3,2,1,0:T(8,128)(2,1)} %refs_1_.1), kind=kLoop, calls=%fused_computation.21 | loop fusion | bytes 393216 | tf_op jit(solution)/shard_map/slice | solution.py:363
  1.7 1.4 %fusion.11 = (bf16[4,64,5,96]{3,2,1,0:T(8,128)(2,1)S(1)}, bf16[4,64,5,96]{3,2,1,0:T(8,128)(2,1)S(1)}) fusion(bf16[4,64,64,96]{3,2,1,0:T(8,128)(2,1)} %refs_4_.3), kind=kLoop, calls=%fused_computation.19 | loop fusion | bytes 983040 | tf_op jit(solution)/shard_map/slice | solution.py:370
  3.1 0.0 copy-start
  3.1 0.4 fusion.8
  3.6 2.1 %collective-permute-start.1 = (bf16[4,64,8,96]{3,2,1,0:T(8,128)(2,1)S(1)}, bf16[4,64,8,96]{3,2,1,0:T(8,128)(2,1)S(1)}, u32[]{:S(2)}, u32[]{:S(2)}) collective-permute-start(bf16[4,64,8,96]{3,2,1,0:T(8,128)(2,1)S(1)} %fusion.8), channel_id=1, source_target_pairs={{0,1},{1,2},{2,3},{3,4},{4,5},{5,6},{6,7},{7,8},{8,9},{9,10},{10,1... | collective-permute-start | bytes 1179656 | tf_op jit(solution)/shard_map/ppermute | solution.py:20
  5.6 0.4 fusion.6
  6.1 7.3 %collective-permute-start = (bf16[4,64,8,96]{3,2,1,0:T(8,128)(2,1)S(1)}, bf16[4,64,8,96]{3,2,1,0:T(8,128)(2,1)S(1)}, u32[]{:S(2)}, u32[]{:S(2)}) collective-permute-start(bf16[4,64,8,96]{3,2,1,0:T(8,128)(2,1)S(1)} %fusion.6), channel_id=1, source_target_pairs={{1,0},{2,1},{3,2},{4,3},{5,4},{6,5},{7,6},{8,7},{9,8},{10,9},{11,1... | collective-permute-start | bytes 1179656 | tf_op jit(solution)/shard_map/ppermute | solution.py:20
  13.4 0.1 pad.22.clone
  13.4 0.1 pad.14.clone
  13.5 1.1 %fusion.10 = (bf16[4,5,64,96]{3,2,1,0:T(8,128)(2,1)S(1)}, bf16[4,5,64,96]{3,2,1,0:T(8,128)(2,1)S(1)}) fusion(bf16[4,64,64,96]{3,2,1,0:T(8,128)(2,1)} %refs_4_.3), kind=kLoop, calls=%fused_computation.18 | loop fusion | bytes 983040 | tf_op jit(solution)/shard_map/slice | solution.py:385
  14.6 0.0 copy-done
  14.7 3.1 %collective-permute-done.1 = bf16[4,64,8,96]{3,2,1,0:T(8,128)(2,1)S(1)} collective-permute-done((bf16[4,64,8,96]{3,2,1,0:T(8,128)(2,1)S(1)}, bf16[4,64,8,96]{3,2,1,0:T(8,128)(2,1)S(1)}, u32[]{:S(2)}, u32[]{:S(2)}) %collective-permute-start.1) | collective-permute-done | bytes 393248 | tf_op jit(solution)/shard_map/ppermute | solution.py:20
  17.8 0.1 fusion.17
  18.0 2.1 %collective-permute-done = bf16[4,64,8,96]{3,2,1,0:T(8,128)(2,1)S(1)} collective-permute-done((bf16[4,64,8,96]{3,2,1,0:T(8,128)(2,1)S(1)}, bf16[4,64,8,96]{3,2,1,0:T(8,128)(2,1)S(1)}, u32[]{:S(2)}, u32[]{:S(2)}) %collective-permute-start) | collective-permute-done | bytes 393248 | tf_op jit(solution)/shard_map/ppermute | solution.py:20
  20.0 0.1 fusion.16
  20.2 0.7 maximum_maximum_fusion.refs_1_
  20.9 0.0 copy-start.2
  20.9 0.0 copy-start.3
  20.9 0.5 pad_maximum_fusion.refs_5_
  21.4 0.0 copy-start.4
  21.4 0.8 pad_maximum_fusion.3
  22.2 0.9 pad_maximum_fusion.1
  23.1 0.0 copy-done.4
  23.1 3.5 %collective-permute-start.2 = (bf16[4,2,40,192]{3,2,1,0:T(8,128)(2,1)}, bf16[4,2,40,192]{3,2,1,0:T(8,128)(2,1)S(1)}, u32[]{:S(2)}, u32[]{:S(2)}) collective-permute-start(bf16[4,2,40,192]{3,2,1,0:T(8,128)(2,1)} %get-tuple-element.11), channel_id=1, source_target_pairs={{0,16},{16,32},{32,48},{48,64},{64,80},{80,96},{96,112},{1,17},{17... | collective-permute-start | bytes 368648 | tf_op jit(solution)/shard_map/ppermute | solution.py:20
  26.6 4.5 %collective-permute-start.3 = (bf16[4,2,40,192]{3,2,1,0:T(8,128)(2,1)S(1)}, bf16[4,2,40,192]{3,2,1,0:T(8,128)(2,1)S(1)}, u32[]{:S(2)}, u32[]{:S(2)}) collective-permute-start(bf16[4,2,40,192]{3,2,1,0:T(8,128)(2,1)S(1)} %get-tuple-element.12), channel_id=1, source_target_pairs={{16,0},{32,16},{48,32},{64,48},{80,64},{96,80},{112,96},{17,1},{33... | collective-permute-start | bytes 368648 | tf_op jit(solution)/shard_map/ppermute | solution.py:20
  31.1 0.6 add_convert_fusion.refs_0_
  31.7 1.9 %collective-permute-start.4 = (bf16[4,5,80,96]{3,2,1,0:T(8,128)(2,1)}, bf16[4,5,80,96]{3,2,1,0:T(8,128)(2,1)S(1)}, u32[]{:S(2)}, u32[]{:S(2)}) collective-permute-start(bf16[4,5,80,96]{3,2,1,0:T(8,128)(2,1)} %get-tuple-element.15), channel_id=1, source_target_pairs={{0,16},{16,32},{32,48},{48,64},{64,80},{80,96},{96,112},{1,17},{17... | collective-permute-start | bytes 921608 | tf_op jit(solution)/shard_map/ppermute | solution.py:20
  33.7 6.2 %collective-permute-start.5 = (bf16[4,5,80,96]{3,2,1,0:T(8,128)(2,1)S(1)}, bf16[4,5,80,96]{3,2,1,0:T(8,128)(2,1)S(1)}, u32[]{:S(2)}, u32[]{:S(2)}) collective-permute-start(bf16[4,5,80,96]{3,2,1,0:T(8,128)(2,1)S(1)} %get-tuple-element.16), channel_id=1, source_target_pairs={{16,0},{32,16},{48,32},{64,48},{80,64},{96,80},{112,96},{17,1},{33... | collective-permute-start | bytes 921608 | tf_op jit(solution)/shard_map/ppermute | solution.py:20
  39.9 0.0 collective-permute-done.2.refs_2_
  39.9 0.0 collective-permute-done.3.refs_3_
  39.9 0.0 copy-done.2
  39.9 0.0 copy-done.3
  39.9 0.0 copy-start.1
  39.9 1.7 %copy-done.1 = bf16[3,3,3,192,192]{4,3,2,1,0:T(8,128)(2,1)S(1)} copy-done((bf16[3,3,3,192,192]{4,3,2,1,0:T(8,128)(2,1)S(1)}, bf16[3,3,3,192,192]{4,3,2,1,0:T(8,128)(2,1)}, u32[]{:S(2)}) %copy-start.1) | copy-done | bytes 1990680
  41.7 16.2 %forward_block.1 = (f32[4,34,32,192]{3,2,1,0:T(8,128)}, f32[4,5,16,192]{3,2,1,0:T(8,128)}) custom-call(bf16[4,32,32,192]{3,2,1,0:T(8,128)(2,1)S(1)} %copy-done, bf16[4,32,8,192]{3,2,1,0:T(8,128)(2,1)S(1)} %maximum_maximum_fusion.refs_1_, bf16[4,2,40,192]{3,2,1,0:T(8,128)(2,1)S(1)} %collective-permute-done.2.refs_2_, ...), custom_call_target="tpu_custom_call" | custom-call | flops 20000000000 | bytes 12000000 | tf_op jit(solution)/shard_map/forward_block/pallas_call | solution.py:399
  57.9 0.0 collective-permute-done.4.refs_6_
  57.9 0.0 copy-start.5
  57.9 0.0 collective-permute-done.5.refs_7_
  57.9 0.0 copy-start.6
  57.9 0.7 copy-done.5
  58.7 0.1 copy-done.6
  58.8 40.6 %backward_block.1 = bf16[4,32,32,192]{3,2,1,0:T(8,128)(2,1)} custom-call(s32[4]{0:T(128)} %add_convert_fusion.refs_0_, bf16[4,32,32,192]{3,2,1,0:T(8,128)(2,1)} %refs_1_.1, f32[4,34,32,192]{3,2,1,0:T(8,128)} %get-tuple-element.13.refs_2_, f32[4,5,16,192]{3,2,1,0:T(8,128)} %get-tuple-element.14.refs_3_, bf16[4,64,64,96]{3,2,1,0:T(8,128)(2,1)} %refs_4_.3, ...), custom_call_target="tpu_custom_call" | custom-call | tf_op jit(solution)/shard_map/backward_block/pallas_call | solution.py:419
  (5 shorter events, 0.0 us)
Async XLA Ops:
  3.1 11.5 %copy-start = (bf16[4,32,32,192]{3,2,1,0:T(8,128)(2,1)S(1)}, bf16[4,32,32,192]{3,2,1,0:T(8,128)(2,1)}, u32[]{:S(2)}) copy-start(bf16[4,32,32,192]{3,2,1,0:T(8,128)(2,1)} %refs_1_.1) | copy-start | bytes 4718596
  3.6 14.2 %collective-permute-start.1 = (bf16[4,64,8,96]{3,2,1,0:T(8,128)(2,1)S(1)}, bf16[4,64,8,96]{3,2,1,0:T(8,128)(2,1)S(1)}, u32[]{:S(2)}, u32[]{:S(2)}) collective-permute-start(bf16[4,64,8,96]{3,2,1,0:T(8,128)(2,1)S(1)} %fusion.8), channel_id=1, source_target_pairs={{0,1},{1,2},{2,3},{3,4},{4,5},{5,6},{6,7},{7,8},{8,9},{9,10},{10,1... | collective-permute-start | bytes 1179656 | tf_op jit(solution)/shard_map/ppermute | solution.py:20
  6.1 13.9 %collective-permute-start = (bf16[4,64,8,96]{3,2,1,0:T(8,128)(2,1)S(1)}, bf16[4,64,8,96]{3,2,1,0:T(8,128)(2,1)S(1)}, u32[]{:S(2)}, u32[]{:S(2)}) collective-permute-start(bf16[4,64,8,96]{3,2,1,0:T(8,128)(2,1)S(1)} %fusion.6), channel_id=1, source_target_pairs={{1,0},{2,1},{3,2},{4,3},{5,4},{6,5},{7,6},{8,7},{9,8},{10,9},{11,1... | collective-permute-start | bytes 1179656 | tf_op jit(solution)/shard_map/ppermute | solution.py:20
  20.9 19.0 %copy-start.2 = (f32[192]{0:T(256)S(1)}, f32[192]{0:T(256)}, u32[]{:S(2)}) copy-start(f32[192]{0:T(256)} %param.11) | copy-start | bytes 2308
  20.9 19.0 %copy-start.3 = (f32[192]{0:T(256)S(1)}, f32[192]{0:T(256)}, u32[]{:S(2)}) copy-start(f32[192]{0:T(256)} %param.10) | copy-start | bytes 2308
  21.4 1.8 %copy-start.4 = (bf16[4,64,16,96]{3,2,1,0:T(8,128)(2,1)}, bf16[4,64,16,96]{3,2,1,0:T(8,128)(2,1)S(1)}, u32[]{:S(2)}) copy-start(bf16[4,64,16,96]{3,2,1,0:T(8,128)(2,1)S(1)} %pad_maximum_fusion.refs_5_) | copy-start | bytes 2359300
  23.1 16.8 %collective-permute-start.2 = (bf16[4,2,40,192]{3,2,1,0:T(8,128)(2,1)}, bf16[4,2,40,192]{3,2,1,0:T(8,128)(2,1)S(1)}, u32[]{:S(2)}, u32[]{:S(2)}) collective-permute-start(bf16[4,2,40,192]{3,2,1,0:T(8,128)(2,1)} %get-tuple-element.11), channel_id=1, source_target_pairs={{0,16},{16,32},{32,48},{48,64},{64,80},{80,96},{96,112},{1,17},{17... | collective-permute-start | bytes 368648 | tf_op jit(solution)/shard_map/ppermute | solution.py:20
  26.6 13.3 %collective-permute-start.3 = (bf16[4,2,40,192]{3,2,1,0:T(8,128)(2,1)S(1)}, bf16[4,2,40,192]{3,2,1,0:T(8,128)(2,1)S(1)}, u32[]{:S(2)}, u32[]{:S(2)}) collective-permute-start(bf16[4,2,40,192]{3,2,1,0:T(8,128)(2,1)S(1)} %get-tuple-element.12), channel_id=1, source_target_pairs={{16,0},{32,16},{48,32},{64,48},{80,64},{96,80},{112,96},{17,1},{33... | collective-permute-start | bytes 368648 | tf_op jit(solution)/shard_map/ppermute | solution.py:20
  31.7 26.1 %collective-permute-start.4 = (bf16[4,5,80,96]{3,2,1,0:T(8,128)(2,1)}, bf16[4,5,80,96]{3,2,1,0:T(8,128)(2,1)S(1)}, u32[]{:S(2)}, u32[]{:S(2)}) collective-permute-start(bf16[4,5,80,96]{3,2,1,0:T(8,128)(2,1)} %get-tuple-element.15), channel_id=1, source_target_pairs={{0,16},{16,32},{32,48},{48,64},{64,80},{80,96},{96,112},{1,17},{17... | collective-permute-start | bytes 921608 | tf_op jit(solution)/shard_map/ppermute | solution.py:20
  33.7 24.3 %collective-permute-start.5 = (bf16[4,5,80,96]{3,2,1,0:T(8,128)(2,1)S(1)}, bf16[4,5,80,96]{3,2,1,0:T(8,128)(2,1)S(1)}, u32[]{:S(2)}, u32[]{:S(2)}) collective-permute-start(bf16[4,5,80,96]{3,2,1,0:T(8,128)(2,1)S(1)} %get-tuple-element.16), channel_id=1, source_target_pairs={{16,0},{32,16},{48,32},{64,48},{80,64},{96,80},{112,96},{17,1},{33... | collective-permute-start | bytes 921608 | tf_op jit(solution)/shard_map/ppermute | solution.py:20
  39.9 1.8 %copy-start.1 = (bf16[3,3,3,192,192]{4,3,2,1,0:T(8,128)(2,1)S(1)}, bf16[3,3,3,192,192]{4,3,2,1,0:T(8,128)(2,1)}, u32[]{:S(2)}) copy-start(bf16[3,3,3,192,192]{4,3,2,1,0:T(8,128)(2,1)} %refs_8_.1) | copy-start | bytes 5971972
  57.9 0.8 copy-start.5
  57.9 0.9 copy-start.6
